TPU v7x, 32 devices: a whole 2x2x4 slice. The times are simulated.
32 devices in a mesh: fsdp: 32 (over z, y, x, core).
Axes of the slice: x: 2, y: 2, z: 4, core: 2. Of those that a mesh axis runs over, the one named last changes fastest.
Arguments:
- tokens: bfloat16 [65536, 768], P('fsdp'), may hold values from -6 to 6
- segments: int32 [65536], P('fsdp'), may hold values from 0 to 4, as said below
- cotangent: bfloat16 [65536, 768], P('fsdp'), may hold values from -6 to 6
- ln1_gain: float32 [768], P('fsdp'), may hold values from 0.25 to 1.75
- ln1_shift: float32 [768], P('fsdp'), may hold values from -3 to 3
- w_qkv: float32 [768, 2304], P('fsdp'), may hold values from -0.21875 to 0.21875
- bias_q: float32 [768], P('fsdp'), may hold values from -3 to 3
- bias_v: float32 [768], P('fsdp'), may hold values from -3 to 3
- w_out: float32 [768, 768], P('fsdp'), may hold values from -1.75 to 1.75
- bias_out: float32 [768], P('fsdp'), may hold values from -3 to 3
- ln2_gain: float32 [768], P('fsdp'), may hold values from 0.25 to 1.75
- ln2_shift: float32 [768], P('fsdp'), may hold values from -3 to 3
- w_up: float32 [768, 3072], P('fsdp'), may hold values from -0.21875 to 0.21875
- bias_up: float32 [3072], P('fsdp'), may hold values from -3 to 3
- w_down: float32 [3072, 768], P('fsdp'), may hold values from -0.109375 to 0.109375
- bias_down: float32 [768], P('fsdp'), may hold values from -3 to 3
Outputs:
- layer_out: bfloat16 [65536, 768], P('fsdp')
- input_grad: bfloat16 [65536, 768], P('fsdp')
- grad_ln1_gain: float32 [768], P('fsdp')
- grad_ln1_shift: float32 [768], P('fsdp')
- grad_w_qkv: float32 [768, 2304], P('fsdp')
- grad_bias_q: float32 [768], P('fsdp')
- grad_bias_v: float32 [768], P('fsdp')
- grad_w_out: float32 [768, 768], P('fsdp')
- grad_bias_out: float32 [768], P('fsdp')
- grad_ln2_gain: float32 [768], P('fsdp')
- grad_ln2_shift: float32 [768], P('fsdp')
- grad_w_up: float32 [768, 3072], P('fsdp')
- grad_bias_up: float32 [3072], P('fsdp')
- grad_w_down: float32 [3072, 768], P('fsdp')
- grad_bias_down: float32 [768], P('fsdp')
Inputs may be any that keep to these rules, and one draw needn't show every extreme that they name: `segments`: in each sequence of 1024 positions, documents with ids 1 to 4 follow one another in order, each of 60 tokens or more, then padding with id 0, of one token or more, to the end.
All inputs are finite; a program needn't handle non-finite values.
Results may differ from a plain program's by a relative error of at most 0.012.
The roundings to bfloat16 on the way count: a program that leaves them out, or rounds other values in their place, can miss the bound.
Values may be sent and summed in bfloat16 or wider, within the bound.
A program may use at most 192 MiB of HBM per device.

v0:
```python
import jax
import jax.numpy as jnp
from jax import lax
from jax.sharding import PartitionSpec as P

HD = 64
TOK_DEV = 1024
MICRO = 2


EPSILON = 1e-06
MASKED = -1000000000.0


def layer_norm(rows, gain, shift):
    mean = jnp.mean(rows, axis=-1, keepdims=True)
    centered = rows - mean
    var = jnp.mean(centered * centered, axis=-1, keepdims=True)
    return centered * lax.rsqrt(var + EPSILON) * gain + shift


def gelu_tanh(values):
    return jax.nn.gelu(values, approximate=True)


def heads_first(rows):
    return rows.reshape(rows.shape[0], -1, 2 * HD).swapaxes(0, 1)


def heads_last(stacked):
    return stacked.swapaxes(0, 1).reshape(stacked.shape[1], -1)


def split_pair(block):
    return block.reshape(block.shape[0], 2, HD)


def masked_scores(q_pair, k_pair, allowed):
    scores = jnp.einsum(
        "qhd,khd->hqk", q_pair, k_pair, preferred_element_type=jnp.float32
    ) * HD ** (-0.5)
    return jnp.where(allowed[None], scores, MASKED)


def attention_forward(query, keys, values, allowed):

    def one_group(pieces):
        q_block, k_block, v_block = pieces
        scores = masked_scores(split_pair(q_block), split_pair(k_block), allowed)
        top = jnp.max(scores, axis=-1, keepdims=True)
        expo = jnp.exp(scores - top)
        total = jnp.sum(expo, axis=-1, keepdims=True)
        probs = (expo / total).astype(jnp.bfloat16)
        mixed = jnp.einsum(
            "hqk,khd->qhd", probs, split_pair(v_block), preferred_element_type=jnp.float32
        )
        return (mixed.reshape(q_block.shape[0], 2 * HD), top + jnp.log(total))

    mixed, logsum = lax.map(one_group, (heads_first(query), heads_first(keys), heads_first(values)))
    return (heads_last(mixed).astype(jnp.bfloat16), logsum)


def attention_backward(query, keys, values, d_attn, logsum, allowed):

    def one_group(pieces):
        q_block, k_block, v_block, d_block, l_block = pieces
        q_pair = split_pair(q_block)
        k_pair = split_pair(k_block)
        d_pair = split_pair(d_block)
        weights = jnp.exp(masked_scores(q_pair, k_pair, allowed) - l_block)
        d_probs = jnp.einsum(
            "qhd,khd->hqk", d_pair, split_pair(v_block), preferred_element_type=jnp.float32
        )
        delta = jnp.sum(weights * d_probs, axis=-1, keepdims=True)
        d_scores = (weights * (d_probs - delta)).astype(jnp.bfloat16)
        scale = HD ** (-0.5)
        d_query = (
            jnp.einsum("hqk,khd->qhd", d_scores, k_pair, preferred_element_type=jnp.float32) * scale
        )
        d_keys = (
            jnp.einsum("hqk,qhd->khd", d_scores, q_pair, preferred_element_type=jnp.float32) * scale
        )
        d_values = jnp.einsum(
            "hqk,qhd->khd", weights.astype(jnp.bfloat16), d_pair, preferred_element_type=jnp.float32
        )
        return (
            d_query.reshape(q_block.shape[0], 2 * HD),
            d_keys.reshape(k_block.shape[0], 2 * HD),
            d_values.reshape(k_block.shape[0], 2 * HD),
        )

    pieces = (
        heads_first(query),
        heads_first(keys),
        heads_first(values),
        heads_first(d_attn),
        logsum,
    )
    d_query, d_keys, d_values = lax.map(one_group, pieces)
    return (heads_last(d_query), heads_last(d_keys), heads_last(d_values))


def gather_forward(parts):
    return (
        lax.all_gather(parts[0], "fsdp", axis=0, tiled=True),
        lax.all_gather(parts[1], "fsdp", axis=0, tiled=True),
        lax.all_gather(parts[2], "fsdp", axis=0, tiled=True),
        lax.all_gather(parts[3], "fsdp", axis=0, tiled=True),
        lax.all_gather(parts[4], "fsdp", axis=0, tiled=True),
        lax.all_gather(parts[5], "fsdp", axis=0, tiled=True),
        lax.all_gather(parts[6], "fsdp", axis=0, tiled=True),
        lax.all_gather(parts[7], "fsdp", axis=0, tiled=True),
        lax.all_gather(parts[8], "fsdp", axis=0, tiled=True),
        lax.all_gather(parts[9], "fsdp", axis=0, tiled=True),
        lax.all_gather(parts[10], "fsdp", axis=0, tiled=True),
        lax.all_gather(parts[11], "fsdp", axis=0, tiled=True),
        lax.all_gather(parts[12], "fsdp", axis=0, tiled=True),
    )


def gather_backward(parts):
    return (
        lax.all_gather(parts[0], "fsdp", axis=0, tiled=True),
        lax.all_gather(parts[2], "fsdp", axis=0, tiled=True),
        lax.all_gather(parts[5], "fsdp", axis=0, tiled=True),
        lax.all_gather(parts[7], "fsdp", axis=0, tiled=True),
        lax.all_gather(parts[9], "fsdp", axis=0, tiled=True),
        lax.all_gather(parts[11], "fsdp", axis=0, tiled=True),
    )


def local(
    tokens,
    segments,
    cotangent,
    ln1_gain,
    ln1_shift,
    w_qkv,
    bias_q,
    bias_v,
    w_out,
    bias_out,
    ln2_gain,
    ln2_shift,
    w_up,
    bias_up,
    w_down,
    bias_down,
):
    masters = (
        ln1_gain,
        ln1_shift,
        w_qkv,
        bias_q,
        bias_v,
        w_out,
        bias_out,
        ln2_gain,
        ln2_shift,
        w_up,
        bias_up,
        w_down,
        bias_down,
    )
    low_parts = [master.astype(jnp.bfloat16) for master in masters]
    width = tokens.shape[1]
    rows_micro = TOK_DEV
    accum = [
        jnp.zeros((lax.axis_size("fsdp") * master.shape[0],) + master.shape[1:], jnp.float32)
        for master in masters
    ]
    reduced = [None] * 13
    outputs = []
    in_grads = []
    for micro in range(MICRO):
        lo_row = micro * rows_micro
        rows = tokens[lo_row : lo_row + rows_micro].astype(jnp.float32)
        seg_rows = segments[lo_row : lo_row + rows_micro]
        d_out = cotangent[lo_row : lo_row + rows_micro]
        g1, c1, wqkv, bq, bv, wo, bo, g2, c2, w1, b1, w2, b2 = gather_forward(low_parts)
        n1 = layer_norm(rows, g1.astype(jnp.float32), c1.astype(jnp.float32)).astype(jnp.bfloat16)
        qkv = jnp.dot(n1, wqkv, preferred_element_type=jnp.float32)
        query = (qkv[:, :width] + bq.astype(jnp.float32)).astype(jnp.bfloat16)
        keys = qkv[:, width : 2 * width].astype(jnp.bfloat16)
        values = (qkv[:, 2 * width :] + bv.astype(jnp.float32)).astype(jnp.bfloat16)
        allowed = seg_rows[:, None] == seg_rows[None, :]
        attn, logsum = attention_forward(query, keys, values, allowed)
        middle = (
            rows + jnp.dot(attn, wo, preferred_element_type=jnp.float32) + bo.astype(jnp.float32)
        )
        n2 = layer_norm(middle, g2.astype(jnp.float32), c2.astype(jnp.float32)).astype(jnp.bfloat16)
        pre = jnp.dot(n2, w1, preferred_element_type=jnp.float32) + b1.astype(jnp.float32)
        act_value, gelu_pull = jax.vjp(gelu_tanh, pre)
        act = act_value.astype(jnp.bfloat16)
        result = (
            middle + jnp.dot(act, w2, preferred_element_type=jnp.float32) + b2.astype(jnp.float32)
        )
        outputs.append(result.astype(jnp.bfloat16))
        g1, wqkv, wo, g2, w1, w2 = gather_backward(low_parts)
        d_out_f = d_out.astype(jnp.float32)
        accum[12] = accum[12] + jnp.sum(d_out_f, axis=0)
        accum[11] = accum[11] + jnp.einsum(
            "nf,nd->fd", act, d_out, preferred_element_type=jnp.float32
        )
        d_act = jnp.einsum("nd,fd->nf", d_out, w2, preferred_element_type=jnp.float32)
        d_pre = gelu_pull(d_act)[0].astype(jnp.bfloat16)
        accum[10] = accum[10] + jnp.sum(d_pre.astype(jnp.float32), axis=0)
        accum[9] = accum[9] + jnp.einsum("nd,nf->df", n2, d_pre, preferred_element_type=jnp.float32)
        d_n2 = jnp.einsum("nf,df->nd", d_pre, w1, preferred_element_type=jnp.float32)
        norm_two, pull_two = jax.vjp(
            layer_norm, middle, g2.astype(jnp.float32), jnp.zeros((width,), jnp.float32)
        )
        d_mid_ln, d_g2, d_c2 = pull_two(d_n2)
        accum[7] = accum[7] + d_g2
        accum[8] = accum[8] + d_c2
        d_mid = d_out_f + d_mid_ln
        d_branch = d_mid.astype(jnp.bfloat16)
        accum[6] = accum[6] + jnp.sum(d_branch.astype(jnp.float32), axis=0)
        accum[5] = accum[5] + jnp.einsum(
            "nd,ne->de", attn, d_branch, preferred_element_type=jnp.float32
        )
        d_attn = jnp.einsum("ne,de->nd", d_branch, wo, preferred_element_type=jnp.float32).astype(
            jnp.bfloat16
        )
        d_query, d_keys, d_values = attention_backward(query, keys, values, d_attn, logsum, allowed)
        d_query_low = d_query.astype(jnp.bfloat16)
        d_keys_low = d_keys.astype(jnp.bfloat16)
        d_values_low = d_values.astype(jnp.bfloat16)
        accum[3] = accum[3] + jnp.sum(d_query_low.astype(jnp.float32), axis=0)
        accum[4] = accum[4] + jnp.sum(d_values_low.astype(jnp.float32), axis=0)
        d_qkv = jnp.concatenate([d_query_low, d_keys_low, d_values_low], axis=1)
        accum[2] = accum[2] + jnp.einsum("nd,ne->de", n1, d_qkv, preferred_element_type=jnp.float32)
        d_n1 = jnp.einsum("ne,de->nd", d_qkv, wqkv, preferred_element_type=jnp.float32)
        norm_one, pull_one = jax.vjp(
            layer_norm, rows, g1.astype(jnp.float32), jnp.zeros((width,), jnp.float32)
        )
        d_rows_ln, d_g1, d_c1 = pull_one(d_n1)
        accum[0] = accum[0] + d_g1
        accum[1] = accum[1] + d_c1
        in_grads.append((d_mid + d_rows_ln).astype(jnp.bfloat16))
    reduced = (
        lax.psum_scatter(accum[0], "fsdp", scatter_dimension=0, tiled=True),
        lax.psum_scatter(accum[1], "fsdp", scatter_dimension=0, tiled=True),
        lax.psum_scatter(accum[2], "fsdp", scatter_dimension=0, tiled=True),
        lax.psum_scatter(accum[3], "fsdp", scatter_dimension=0, tiled=True),
        lax.psum_scatter(accum[4], "fsdp", scatter_dimension=0, tiled=True),
        lax.psum_scatter(accum[5], "fsdp", scatter_dimension=0, tiled=True),
        lax.psum_scatter(accum[6], "fsdp", scatter_dimension=0, tiled=True),
        lax.psum_scatter(accum[7], "fsdp", scatter_dimension=0, tiled=True),
        lax.psum_scatter(accum[8], "fsdp", scatter_dimension=0, tiled=True),
        lax.psum_scatter(accum[9], "fsdp", scatter_dimension=0, tiled=True),
        lax.psum_scatter(accum[10], "fsdp", scatter_dimension=0, tiled=True),
        lax.psum_scatter(accum[11], "fsdp", scatter_dimension=0, tiled=True),
        lax.psum_scatter(accum[12], "fsdp", scatter_dimension=0, tiled=True),
    )
    layer_out = jnp.concatenate(outputs, axis=0)
    input_grad = jnp.concatenate(in_grads, axis=0)
    return (
        layer_out,
        input_grad,
        reduced[0],
        reduced[1],
        reduced[2],
        reduced[3],
        reduced[4],
        reduced[5],
        reduced[6],
        reduced[7],
        reduced[8],
        reduced[9],
        reduced[10],
        reduced[11],
        reduced[12],
    )


def solution(mesh):
    placed = (
        P("fsdp", None),
        P("fsdp"),
        P("fsdp", None),
        P("fsdp"),
        P("fsdp"),
        P("fsdp", None),
        P("fsdp"),
        P("fsdp"),
        P("fsdp", None),
        P("fsdp"),
        P("fsdp"),
        P("fsdp"),
        P("fsdp", None),
        P("fsdp"),
        P("fsdp", None),
        P("fsdp"),
    )
    return jax.shard_map(
        local,
        mesh=mesh,
        in_specs=placed,
        out_specs=(
            P("fsdp", None),
            P("fsdp", None),
            P("fsdp"),
            P("fsdp"),
            P("fsdp", None),
            P("fsdp"),
            P("fsdp"),
            P("fsdp", None),
            P("fsdp"),
            P("fsdp"),
            P("fsdp"),
            P("fsdp", None),
            P("fsdp"),
            P("fsdp", None),
            P("fsdp"),
        ),
        check_vma=False,
    )
```

profile of v0, /device:TPU:0, one launch (start us, length us, event | category | flops | bytes accessed | tf_op | source)
XLA Modules:
  0.0 1000.0 jit_solution(6145620416811009983)
XLA Ops:
  21.8 42.8 %all-reduce.19 = (bf16[768]{0:T(1024)(128)(2,1)S(1)}, bf16[768]{0:T(1024)(128)(2,1)S(1)}, bf16[768]{0:T(1024)(128)(2,1)S(1)}, bf16[768]{0:T(1024)(128)(2,1)S(1)}...) all-reduce(bf16[768]{0:T(1024)(128)(2,1)S(1)} %dynamic-update-slice, ...), channel_id=1, replica_groups=mesh['fsdp'=32] {'fsdp'}, use_global_device_ids=true, to_apply=%add.1 | all-reduce | flops 9216 | bytes 36864
  74.9 6.1 fusion.94
  88.6 6.1 fusion.91
  100.1 7.2 fusion.68
  111.2 55.2 %while.57 = (s32[]{:T(128)}, bf16[6,1024,128]{1,2,0:T(8,128)(2,1)}, f32[6,2,1024,1]{2,1,3,0:T(2,128)S(1)}, bf16[6,1024,128]{1,2,0:T(8,128)(2,1)S(1)}, bf16[6,102...) while((s32[]{:T(128)}, bf16[6,1024,128]{1,2,0:T(8,128)(2,1)}, ...), condition=%wide.region_13.14_spmd.clone, body=%wide.region_10.13_spmd.clone.sunk | while | flops 563083264 | bytes 32575596 | solution.py:59
  166.5 3.7 copy.67
  174.2 61.7 %while.56 = (s32[]{:T(128)}, bf16[6,1024,128]{1,2,0:T(8,128)(2,1)}, f32[6,2,1024,1]{2,1,3,0:T(2,128)S(1)}, bf16[6,1024,128]{1,2,0:T(8,128)(2,1)}, bf16[6,1024,12...) while((s32[]{:T(128)}, bf16[6,1024,128]{1,2,0:T(8,128)(2,1)}, ...), condition=%wide.region_5.6_spmd.clone, body=%wide.region_2.5_spmd.clone.sunk | while | flops 563083264 | bytes 32575596 | solution.py:59
  246.4 11.2 %fusion.100 = f32[1024,3072]{1,0:T(8,128)} fusion(bf16[768,3072]{1,0:T(8,128)(2,1)} %all-gather.9.cloned.1.call-done, f32[1024,768]{1,0:T(8,128)} %copy-done.6, f32[1024]{0:T(1024)S(1)} %fusion.85, f32[1024]{0:T(1024)S(1)} %broadcast_multiply_fusion, f32[768]{0:T(1024)S(1)} %copy-done.47, f32[768]{0:T(1024)S(1)} %copy-done.45), kind=kOutput, calls=%fused_computation.210 | convolution fusion | flops 4835770368 | bytes 20461568 | tf_op jit(solution)/shard_map/dot_general | solution.py:192
  257.6 5.0 all-gather.11.cloned.1.call-done
  262.6 15.5 %convert_reduce_fusion = (f32[3072]{0:T(1024)}, bf16[1024,3072]{1,0:T(8,128)(2,1)S(1)}) fusion(f32[1024,3072]{1,0:T(8,128)} %fusion.100, f32[3072]{0:T(1024)S(1)} %copy-done.81, bf16[3072,768]{1,0:T(8,128)(2,1)} %all-gather.11.cloned.1.call-done, bf16[2048,768]{1,0:T(8,128)(2,1)S(1)} %copy-done.17), kind=kOutput, calls=%fused_computation.88 | convolution fusion | flops 4904186880 | bytes 25190400 | tf_op jit(solution)/shard_map/nd,fd->nf/dot_general | solution.py:205
  278.1 9.7 fusion.110
  287.8 8.3 fusion.99
  296.1 15.7 %convert_reduce_fusion.1 = (f32[3072]{0:T(1024)}, bf16[1024,3072]{1,0:T(8,128)(2,1)S(1)}) fusion(f32[1024,3072]{1,0:T(8,128)} %fusion.99, f32[3072]{0:T(1024)S(1)} %copy-done.81, bf16[3072,768]{1,0:T(8,128)(2,1)} %all-gather.11.cloned.1.call-done, bf16[2048,768]{1,0:T(8,128)(2,1)S(1)} %copy-done.17), kind=kOutput, calls=%fused_computation.89 | convolution fusion | flops 4904186880 | bytes 25190400 | tf_op jit(solution)/shard_map/nd,fd->nf/dot_general | solution.py:205
  311.8 12.8 %multiply_reduce_fusion.3 = (f32[768]{0:T(1024)}, f32[1024]{0:T(1024)S(1)}, f32[768]{0:T(1024)}, f32[768]{0:T(1024)}, f32[1024]{0:T(1024)S(1)}, /*index=5*/f32[768]{0:T(1024)}, f32[1024,768]{1,0:T(8,128)}) fusion(f32[1024,768]{1,0:T(8,128)S(1)} %copy-done.4, f32[1024]{0:T(1024)S(1)} %fusion.83, f32[1024]{0:T(1024)S(1)} %broadcast_multiply_fusion.2, ...), kind=kOutput, calls=%fused_computation.148 | convolution fusion | flops 4844414976 | bytes 23632896 | tf_op jit(solution)/shard_map/nf,df->nd/dot_general | solution.py:209
  324.6 4.1 fusion.104
  336.9 4.0 convolution_convert_fusion
  342.7 109.7 %while.59 = (s32[]{:T(128)}, bf16[6,1024,128]{1,2,0:T(8,128)(2,1)S(1)}, bf16[6,1024,128]{1,2,0:T(8,128)(2,1)}, bf16[6,1024,128]{1,2,0:T(8,128)(2,1)S(1)}, bf16[6...) while((s32[]{:T(128)}, ...), condition=%wide.region_27.28_spmd.clone, body=%wide.region_25.27_spmd.clone.sunk | while | flops 1375205376 | bytes 73461904 | solution.py:99
  452.5 5.4 convolution_convert_fusion.1
  462.0 115.1 %while.58 = (s32[]{:T(128)}, bf16[6,1024,128]{1,2,0:T(8,128)(2,1)}, bf16[6,1024,128]{1,2,0:T(8,128)(2,1)}, bf16[6,1024,128]{1,2,0:T(8,128)(2,1)}, bf16[6,1024,12...) while((s32[]{:T(128)}, bf16[6,1024,128]{1,2,0:T(8,128)(2,1)}, ...), condition=%wide.region_20.21_spmd.clone, body=%wide.region_18.20_spmd.clone.sunk | while | flops 1375205376 | bytes 73461904 | solution.py:99
  577.2 6.8 fusion.75
  584.1 7.3 convolution_add_fusion
  592.1 9.3 fusion.98
  601.5 11.3 %convolution_add_fusion.2 = f32[768,3072]{1,0:T(8,128)} fusion(f32[768,3072]{1,0:T(8,128)S(1)} %fusion.98, bf16[1024,3072]{1,0:T(8,128)(2,1)} %copy-done.33, f32[1024,768]{1,0:T(8,128)S(1)} %copy-done.8, f32[1024]{0:T(1024)S(1)} %copy-done.56, f32[1024]{0:T(1024)S(1)} %copy-done.52, f32[768]{0:T(1024)S(1)} %copy-done.48, f32[768]{0:T(1024)S(1)} %copy-done.46), kind=kOutput, calls=%fused_computation.94 | convolution fusion | flops 4838129664 | bytes 28325888 | tf_op jit(solution)/shard_map/nd,nf->df/dot_general | solution.py:208
  613.5 13.2 %fusion.79 = f32[3072,768]{1,0:T(8,128)S(1)} fusion(bf16[2048,768]{1,0:T(8,128)(2,1)} %param.26, f32[1024,3072]{1,0:T(8,128)} %fusion.99, f32[3072]{0:T(1024)S(1)} %copy-done.82), kind=kOutput, calls=%fused_computation.175 | convolution fusion | flops 4863295488 | bytes 23605248 | tf_op jit(solution)/shard_map/nf,nd->fd/dot_general | solution.py:202
  626.7 13.5 %convolution_add_fusion.1 = f32[3072,768]{1,0:T(8,128)} fusion(f32[3072,768]{1,0:T(8,128)S(1)} %fusion.79, bf16[2048,768]{1,0:T(8,128)(2,1)S(1)} %copy-done.18, f32[1024,3072]{1,0:T(8,128)} %fusion.100, f32[3072]{0:T(1024)S(1)} %copy-done.82), kind=kOutput, calls=%fused_computation.93 | convolution fusion | flops 4865654784 | bytes 33042432 | tf_op jit(solution)/shard_map/nf,nd->fd/dot_general | solution.py:202
  641.1 8.2 fusion.74
  649.4 5.0 fusion.63
  660.2 41.6 %all-reduce.18 = (f32[768]{0:T(1024)S(1)}, f32[768]{0:T(1024)S(1)}, f32[768]{0:T(1024)S(1)}, f32[768]{0:T(1024)S(1)}, f32[768]{0:T(1024)S(1)}, /*index=5*/f32[76...) all-reduce(f32[768]{0:T(1024)S(1)} %add.330, ...), channel_id=2, replica_groups=mesh['fsdp'=32] {'fsdp'}, use_global_device_ids=true, to_apply=%region_32.33.clone | all-reduce | flops 9216 | bytes 73728
  707.1 12.7 %add_convert_fusion.2 = bf16[1024,768]{1,0:T(8,128)(2,1)S(1)} fusion(f32[1024,768]{1,0:T(8,128)} %copy-done.6, bf16[3072,768]{1,0:T(8,128)(2,1)} %all-gather.11.cloned.1.call-done, f32[768]{0:T(1024)S(1)} %convert_element_type.313, f32[1024,3072]{1,0:T(8,128)} %fusion.100, f32[3072]{0:T(1024)S(1)} %copy-done.82), kind=kOutput, calls=%fused_computation.159 | convolution fusion | flops 4865654784 | bytes 22035456 | tf_op jit(solution)/shard_map/dot_general | solution.py:196
  719.9 12.7 %add_convert_fusion.4 = bf16[1024,768]{1,0:T(8,128)(2,1)S(1)} fusion(f32[1024,768]{1,0:T(8,128)S(1)} %copy-done.5, bf16[3072,768]{1,0:T(8,128)(2,1)} %all-gather.11.cloned.1.call-done, f32[768]{0:T(1024)S(1)} %convert_element_type.313, f32[1024,3072]{1,0:T(8,128)} %fusion.99, f32[3072]{0:T(1024)S(1)} %copy-done.82), kind=kOutput, calls=%fused_computation.162 | convolution fusion | flops 4865654784 | bytes 22035456 | tf_op jit(solution)/shard_map/dot_general | solution.py:196
  741.9 108.9 %reduce-scatter.9.cloned.1.call-done = f32[24,3072]{1,0:T(8,128)} async-done(((f32[768,3072]{1,0:T(8,128)}), f32[24,3072]{1,0:T(8,128)}) %reduce-scatter.9.cloned.1.call-update) | async-done | bytes 294928 | tf_op jit(solution)/shard_map/reduce_scatter | solution.py:251
  850.8 142.2 %reduce-scatter.11.cloned.1.call-done = f32[96,768]{1,0:T(8,128)} async-done(((f32[3072,768]{1,0:T(8,128)}), f32[96,768]{1,0:T(8,128)}) %reduce-scatter.11.cloned.1.call-update) | async-done | bytes 294928 | tf_op jit(solution)/shard_map/reduce_scatter | solution.py:253
  (587 shorter events, 431.3 us)
Async XLA Ops:
  7.2 62.4 %copy-start = (bf16[2048,768]{1,0:T(8,128)(2,1)S(1)}, bf16[2048,768]{1,0:T(8,128)(2,1)}, u32[]{:S(2)}) copy-start(bf16[2048,768]{1,0:T(8,128)(2,1)} %param.24) | copy-start | bytes 9437188
  7.2 67.7 %all-gather.5.cloned.1.call-start = ((), (), s32[]{:S(2)}) async-start(), calls=%async_computation.4 | async-start | bytes 3649536 | tf_op jit(solution)/shard_map/all_gather | solution.py:107
  9.0 227.0 %all-gather.7.cloned.1.call-start = ((), (), s32[]{:S(2)}) async-start(), calls=%async_computation.5 | async-start | bytes 1216512 | tf_op jit(solution)/shard_map/all_gather | solution.py:110
  10.6 235.7 %all-gather.9.cloned.1.call-start = ((), (), s32[]{:S(2)}) async-start(), calls=%async_computation.6 | async-start | bytes 4866048 | tf_op jit(solution)/shard_map/all_gather | solution.py:114
  12.3 250.3 %all-gather.11.cloned.1.call-start = ((), (), s32[]{:S(2)}) async-start(), calls=%async_computation.7 | async-start | bytes 4866048 | tf_op jit(solution)/shard_map/all_gather | solution.py:116
  14.0 727.9 %reduce-scatter.7.cloned.1.call-start = ((), (), s32[]{:S(2)}) async-start(), calls=%async_computation.9 | async-start | bytes 2433024 | tf_op jit(solution)/shard_map/reduce_scatter | solution.py:247
  64.6 23.9 %copy-start.89 = (f32[768]{0:T(1024)}, f32[768]{0:T(1024)S(1)}, u32[]{:S(2)}) copy-start(f32[768]{0:T(1024)S(1)} %convert_element_type.287) | copy-start | bytes 9220
  64.6 23.9 %copy-start.67 = (f32[768]{0:T(1024)}, f32[768]{0:T(1024)S(1)}, u32[]{:S(2)}) copy-start(f32[768]{0:T(1024)S(1)} %convert_element_type.285) | copy-start | bytes 9220
  69.5 19.0 %copy-start.61 = (f32[1024]{0:T(1024)}, f32[1024]{0:T(1024)S(1)}, u32[]{:S(2)}) copy-start(f32[1024]{0:T(1024)S(1)} %get-tuple-element.451) | copy-start | bytes 12292
  70.9 17.6 %copy-start.69 = (f32[1024]{0:T(1024)}, f32[1024]{0:T(1024)S(1)}, u32[]{:S(2)}) copy-start(f32[1024]{0:T(1024)S(1)} %fusion.82) | copy-start | bytes 12292
  174.2 61.8 %copy-start.1 = (bf16[2048,768]{1,0:T(8,128)(2,1)S(1)}, bf16[2048,768]{1,0:T(8,128)(2,1)}, u32[]{:S(2)}) copy-start(bf16[2048,768]{1,0:T(8,128)(2,1)} %param.24) | copy-start | bytes 9437188
  174.2 61.8 %copy-start.91 = (f32[768]{0:T(1024)S(1)}, f32[768]{0:T(1024)}, u32[]{:S(2)}) copy-start(f32[768]{0:T(1024)} %convert_element_type.301) | copy-start | bytes 9220
  239.5 85.1 %copy-start.49 = (f32[1024]{0:T(1024)}, f32[1024]{0:T(1024)S(1)}, u32[]{:S(2)}) copy-start(f32[1024]{0:T(1024)S(1)} %broadcast_multiply_fusion.2) | copy-start | bytes 12292
  240.1 84.5 %copy-start.53 = (f32[1024]{0:T(1024)}, f32[1024]{0:T(1024)S(1)}, u32[]{:S(2)}) copy-start(f32[1024]{0:T(1024)S(1)} %fusion.83) | copy-start | bytes 12292
  244.1 80.5 %copy-start.51 = (f32[1024]{0:T(1024)}, f32[1024]{0:T(1024)S(1)}, u32[]{:S(2)}) copy-start(f32[1024]{0:T(1024)S(1)} %broadcast_multiply_fusion) | copy-start | bytes 12292
  246.3 78.4 %copy-start.55 = (f32[1024]{0:T(1024)}, f32[1024]{0:T(1024)S(1)}, u32[]{:S(2)}) copy-start(f32[1024]{0:T(1024)S(1)} %fusion.85) | copy-start | bytes 12292
  246.3 16.3 %copy-start.17 = (bf16[2048,768]{1,0:T(8,128)(2,1)S(1)}, bf16[2048,768]{1,0:T(8,128)(2,1)}, u32[]{:S(2)}) copy-start(bf16[2048,768]{1,0:T(8,128)(2,1)} %param.26) | copy-start | bytes 9437188
  246.3 16.3 %copy-start.81 = (f32[3072]{0:T(1024)S(1)}, f32[3072]{0:T(1024)}, u32[]{:S(2)}) copy-start(f32[3072]{0:T(1024)} %convert_element_type.309) | copy-start | bytes 36868
  296.1 15.7 %copy-start.7 = (f32[1024,768]{1,0:T(8,128)S(1)}, f32[1024,768]{1,0:T(8,128)}, u32[]{:S(2)}) copy-start(f32[1024,768]{1,0:T(8,128)} %copy-done.6) | copy-start | bytes 9437188
  452.5 289.4 %reduce-scatter.5.cloned.1.call-start = ((), (), s32[]{:S(2)}) async-start(), calls=%async_computation.8 | async-start | bytes 7299072 | tf_op jit(solution)/shard_map/reduce_scatter | solution.py:244
  462.0 115.1 %copy-start.2 = (bf16[2048,768]{1,0:T(8,128)(2,1)S(1)}, bf16[2048,768]{1,0:T(8,128)(2,1)}, u32[]{:S(2)}) copy-start(bf16[2048,768]{1,0:T(8,128)(2,1)} %param.24) | copy-start | bytes 9437188
  462.0 115.1 %copy-start.62 = (f32[1024]{0:T(1024)S(1)}, f32[1024]{0:T(1024)}, u32[]{:S(2)}) copy-start(f32[1024]{0:T(1024)} %copy-done.61) | copy-start | bytes 12292
  462.0 115.1 %copy-start.68 = (f32[768]{0:T(1024)S(1)}, f32[768]{0:T(1024)}, u32[]{:S(2)}) copy-start(f32[768]{0:T(1024)} %copy-done.67) | copy-start | bytes 9220
  462.0 115.1 %copy-start.70 = (f32[1024]{0:T(1024)S(1)}, f32[1024]{0:T(1024)}, u32[]{:S(2)}) copy-start(f32[1024]{0:T(1024)} %copy-done.69) | copy-start | bytes 12292
  462.0 115.1 %copy-start.90 = (f32[768]{0:T(1024)S(1)}, f32[768]{0:T(1024)}, u32[]{:S(2)}) copy-start(f32[768]{0:T(1024)} %copy-done.89) | copy-start | bytes 9220
  591.5 259.4 %reduce-scatter.9.cloned.1.call-start = ((), (), s32[]{:S(2)}) async-start(), calls=%async_computation.10 | async-start | bytes 9732096 | tf_op jit(solution)/shard_map/reduce_scatter | solution.py:251
  612.8 380.2 %reduce-scatter.11.cloned.1.call-start = ((), (), s32[]{:S(2)}) async-start(), calls=%async_computation.11 | async-start | bytes 9732096 | tf_op jit(solution)/shard_map/reduce_scatter | solution.py:253
  719.8 14.7 %copy-start.14 = (f32[1024,768]{1,0:T(8,128)S(1)}, f32[1024,768]{1,0:T(8,128)}, u32[]{:S(2)}) copy-start(f32[1024,768]{1,0:T(8,128)} %copy-done.13) | copy-start | bytes 9437188
  719.8 14.7 %copy-start.16 = (f32[1024,768]{1,0:T(8,128)S(1)}, f32[1024,768]{1,0:T(8,128)}, u32[]{:S(2)}) copy-start(f32[1024,768]{1,0:T(8,128)} %copy-done.15) | copy-start | bytes 9437188
  719.9 14.7 %copy-start.19 = (bf16[2048,768]{1,0:T(8,128)(2,1)S(1)}, bf16[2048,768]{1,0:T(8,128)(2,1)}, u32[]{:S(2)}) copy-start(bf16[2048,768]{1,0:T(8,128)(2,1)} %param.26) | copy-start | bytes 9437188
  719.9 14.7 %copy-start.74 = (f32[1024]{0:T(1024)S(1)}, f32[1024]{0:T(1024)}, u32[]{:S(2)}) copy-start(f32[1024]{0:T(1024)} %copy-done.73) | copy-start | bytes 12292
  719.9 14.7 %copy-start.76 = (f32[1024]{0:T(1024)S(1)}, f32[1024]{0:T(1024)}, u32[]{:S(2)}) copy-start(f32[1024]{0:T(1024)} %copy-done.75) | copy-start | bytes 12292
  (73 other events, 322.4 us)
Sparse Core Ops, SparseCore 0:
  11.5 63.3 all-gather.4
  77.8 52.8 all-gather.6
  134.1 62.5 all-gather.8
  200.1 62.4 all-gather.10
  452.6 97.8 reduce-scatter.6
  591.6 117.9 reduce-scatter.4
  716.1 134.7 reduce-scatter.8
  858.3 134.6 reduce-scatter.10
where the time goes:
time: 1010 us; the launch traced here: 1000 us
  matrix products  375 us (37%)
  waiting for transfers between devices  259 us (26%)
  local copies, waits for them, and re-layouts  147 us (15%)
  other arithmetic  117 us (12%)
  blocking collectives  84.4 us (8%)
  between operations  15.7 us (2%)
    reduce_scatter x1, waiting for transfers between devices, local(): lax.psum_scatter(accum[11], 'fsdp', scatter_dimension=0, tiled=True)  142 us
    reduce_scatter x1, waiting for transfers between devices, local(): lax.psum_scatter(accum[9], 'fsdp', scatter_dimension=0, tiled=True)  109 us
    unnamed x2, blocking collectives  84.4 us
    dynamic_slice x72, local copies, waits for them, and re-layouts, attention_forward(): lax.map(one_group, (heads_first(query), heads_first(keys), heads_first(va...  65.2 us
    dot_general x12, matrix products, one_group(): jnp.einsum('qhd,khd->hqk', d_pair, split_pair(v_block), preferred_element...  41.1 us
    dot_general x24, matrix products, masked_scores(): jnp.einsum('qhd,khd->hqk', q_pair, k_pair, preferred_element_type=jnp.flo...  38.4 us
    dot_general x12, matrix products, one_group(): jnp.einsum('hqk,khd->qhd', probs, split_pair(v_block), preferred_element_...  33.8 us
    convert_element_type x12, other arithmetic, one_group(): d_scores = (weights * (d_probs - delta)).astype(jnp.bfloat16)  32.4 us
  transfers between devices with their start and end apart: 8, of which 4 were waited for; matrix products, arithmetic and copies ran while one was open for 43% of the time, Pallas kernels for 0%

commit v1 on v0

v1 whole, which is shorter than its diff:
```python
import functools
import jax
import jax.numpy as jnp
from jax import lax
from jax.experimental import pallas as pl
from jax.experimental.pallas import tpu as pltpu
from jax.sharding import PartitionSpec as P

HD = 64
QB = 128
KB = 128
NEG = -1000000000.0
BF = jnp.bfloat16
F32 = jnp.float32
EPSILON = 1e-06
NT = (((1,), (1,)), ((), ()))


def mm(a, b):
    return jnp.dot(a, b, preferred_element_type=F32)


def mm_nt(a, b):
    return lax.dot_general(a, b, NT, preferred_element_type=F32)


def pair_diag(top, bottom):
    zero = jnp.zeros_like(top)
    return jnp.concatenate(
        [jnp.concatenate([top, zero], axis=1), jnp.concatenate([zero, bottom], axis=1)], axis=0
    )


SPANS = (2, 3, 4, 5, 6, 8)


def by_span(lo, hi, rows, run):
    need = hi - lo
    below = 0
    for span in SPANS:
        if below * KB >= rows:
            break
        size = min(span * KB, rows)
        last = size == rows

        @pl.when((need > below) & (last | (need <= span)))
        def _(size=size):
            run(pl.multiple_of(jnp.minimum(lo * KB, rows - size), KB), size)

        below = span


def chunks(k0, size):
    return [(pl.multiple_of(k0 + c, KB), min(2 * KB, size - c)) for c in range(0, size, 2 * KB)]


def terms(pieces):
    width = pieces[0].shape[1]
    row = lax.broadcasted_iota(jnp.int32, (8, width), 0)
    tail = jnp.zeros((8, width), F32)
    for i, piece in enumerate(pieces):
        tail = jnp.where(row == i, piece, tail)
    return tail


def three_parts(x):
    first = x.astype(BF).astype(F32)
    rest = x - first
    second = rest.astype(BF).astype(F32)
    return first, second, rest - second


def pair_rhs(feat, extra, p, qs):
    a = 128 * p
    block = pair_diag(feat[a : a + 64, qs], feat[a + 64 : a + 128, qs])
    rows = jnp.concatenate([extra[2 * p, :, qs], extra[2 * p + 1, :, qs]], axis=1)
    return block, jnp.concatenate([block, rows, jnp.zeros((112, 2 * QB), BF)], axis=0)


def attn_fwd_kernel(
    earlier, lo, hi, q_ref, k_ref, v_ref, oh_ref, mr_ref, *rest
):
    o_ref, ot_ref, lse_ref, qt, vt, extra, tops = rest[earlier:]
    seq = pl.program_id(0)
    rows = q_ref.shape[0]
    pairs = q_ref.shape[1] // 128
    heads = 2 * pairs
    vt[...] = v_ref[...].T
    qt[...] = (q_ref[...] * 0.125).astype(BF).T
    lane = lax.broadcasted_iota(jnp.int32, (8, heads * HD), 1) // HD
    pick = (lane == lax.broadcasted_iota(jnp.int32, (8, heads * HD), 0)).astype(BF)
    square = k_ref[...].astype(F32)
    norms = mm_nt(pick, (square * square).astype(BF))
    bound = jnp.sqrt(jnp.max(norms, axis=1, keepdims=True)) * 1.01
    for h in range(heads):
        qh = qt[64 * h : 64 * h + 64, :].astype(F32)
        length = jnp.sqrt(jnp.sum(qh * qh, axis=0, keepdims=True)) * 1.01
        m = (length * bound[h : h + 1, :]).astype(BF).astype(F32)
        tops[h : h + 1, :] = m
        extra[h, :, :] = jnp.concatenate([mr_ref[0], terms([-m])], axis=0).astype(BF)

    def keep(qs, p, l, full):
        a = 128 * p
        ot_ref[0, a : a + 64, qs] = full[0:64, 0:QB]
        ot_ref[0, a + 64 : a + 128, qs] = full[64:128, QB:]
        lse_ref[0, 0, 2 * p : 2 * p + 1, qs] = l[:, 0:QB]
        lse_ref[0, 0, 2 * p + 1 : 2 * p + 2, qs] = l[:, QB:]

    def q_step(qb, carry):
        qs = pl.ds(pl.multiple_of(qb * QB, QB), QB)

        def run(k0, size):
            rhs = [pair_rhs(qt, extra, p, qs)[1] for p in range(pairs)]
            l = [jnp.zeros((1, 2 * QB), F32)] * pairs
            acc = [None] * pairs
            for c0, cs in chunks(k0, size):
                ks = pl.ds(c0, cs)
                oh = oh_ref[ks, :]
                for p in range(pairs):
                    cols = slice(128 * p, 128 * p + 128)
                    w = jnp.exp(mm(jnp.concatenate([k_ref[ks, cols], oh], axis=1), rhs[p]))
                    l[p] = l[p] + jnp.sum(w, axis=0, keepdims=True)
                    part = mm(vt[cols, ks], w.astype(BF))
                    acc[p] = part if acc[p] is None else acc[p] + part
            for p in range(pairs):
                keep(qs, p, l[p], acc[p])

        by_span(lo[seq, qb], hi[seq, qb], rows, run)
        return carry

    lax.fori_loop(0, rows // QB, q_step, 0)

    @pl.when(jnp.min(lse_ref[0, 0]) < 1e-20)
    def _():
        for h in range(heads):
            extra[h, :, :] = jnp.concatenate([mr_ref[0], jnp.zeros_like(mr_ref[0])], axis=0).astype(BF)

        def q_again(qb, carry):
            qs = pl.ds(pl.multiple_of(qb * QB, QB), QB)
            for p in range(pairs):
                cols = slice(128 * p, 128 * p + 128)
                rhs = pair_rhs(qt, extra, p, qs)[1]

                def scores(kb):
                    ks = pl.ds(pl.multiple_of(kb * KB, KB), KB)
                    return ks, mm(jnp.concatenate([k_ref[ks, cols], oh_ref[ks, :]], axis=1), rhs)

                def top_step(kb, m):
                    return jnp.maximum(m, jnp.max(scores(kb)[1], axis=0, keepdims=True))

                blocks = rows // KB
                m = lax.fori_loop(0, blocks, top_step, jnp.full((1, 2 * QB), 2 * NEG, F32))

                def sum_step(kb, state):
                    ks, st = scores(kb)
                    w = jnp.exp(st - m)
                    return state[0] + jnp.sum(w, axis=0, keepdims=True), state[1] + mm(vt[cols, ks], w.astype(BF))

                start = (jnp.zeros((1, 2 * QB), F32), jnp.zeros((128, 2 * QB), F32))
                l, full = lax.fori_loop(0, blocks, sum_step, start)
                tops[2 * p : 2 * p + 1, qs] = m[:, 0:QB]
                tops[2 * p + 1 : 2 * p + 2, qs] = m[:, QB:]
                keep(qs, p, l, full)
            return carry

        lax.fori_loop(0, rows // QB, q_again, 0)

    for h in range(heads):
        l = lse_ref[0, 0, h : h + 1, :]
        hs = slice(64 * h, 64 * h + 64)
        ot_ref[0, hs, :] = ot_ref[0, hs, :] * (1.0 / l)
        lse_ref[0, 0, h : h + 1, :] = tops[h : h + 1, :] + jnp.log(l)
    o_ref[...] = ot_ref[0].astype(BF).T


def attn_bwd_kernel(
    lo, hi, part, q_ref, k_ref, v_ref, do_ref, ot_ref, lse_ref, oh_ref, mr_ref, dqkv_ref,
    qt, kt, dot, extra_q, extra_d, dqt, dkt, dvt,
):
    seq = pl.program_id(0)
    rows = q_ref.shape[0]
    pairs = q_ref.shape[1] // 128
    qt[...] = (q_ref[...] * 0.125).astype(BF).T
    kt[...] = k_ref[...].T
    dot[...] = do_ref[...].T
    for h in range(2 * pairs):
        r = slice(64 * h, 64 * h + 64)
        delta = jnp.sum(dot[r, :].astype(F32) * ot_ref[0, r, :], axis=0, keepdims=True)
        lse = lse_ref[0, 0, h : h + 1, :]
        extra_q[h, :, :] = jnp.concatenate([mr_ref[0], terms(three_parts(-lse))], axis=0).astype(BF)
        tail = terms(three_parts(-delta))
        extra_d[h, :, :] = jnp.concatenate([jnp.zeros_like(tail), tail], axis=0).astype(BF)
    dkt[...] = jnp.zeros_like(dkt)
    dvt[...] = jnp.zeros_like(dvt)

    def q_step(qb, carry):
        qs = pl.ds(pl.multiple_of(qb * QB, QB), QB)

        def run(k0, size):
            ks = pl.ds(k0, size)
            oh = oh_ref[ks, :]
            for p in range(pairs):
                a = 128 * p
                cols = slice(a, a + 128)
                qm, qx = pair_rhs(qt, extra_q, p, qs)
                dom, dx = pair_rhs(dot, extra_d, p, qs)
                w = jnp.exp(mm(jnp.concatenate([k_ref[ks, cols], oh], axis=1), qx))
                ds = (w * mm(jnp.concatenate([v_ref[ks, cols], oh], axis=1), dx)).astype(BF)
                dvt[cols, ks] += mm_nt(dom, w.astype(BF))
                dkt[cols, ks] += mm_nt(qm, ds)
                dq = mm(kt[cols, ks], ds)
                dqt[a : a + 64, qs] = dq[0:64, 0:QB]
                dqt[a + 64 : a + 128, qs] = dq[64:128, QB:]

        by_span(lo[seq, qb], hi[seq, qb], rows, run)
        return carry

    lax.fori_loop(0, rows // QB, q_step, 0)
    wide = dqt.shape[0]
    dqkv_ref[:, 0:wide] = (dqt[...] * 0.125).astype(BF).T
    dqkv_ref[:, wide : 2 * wide] = dkt[...].astype(BF).T
    dqkv_ref[:, 2 * wide :] = dvt[...].astype(BF).T


WIDE = 384
TILE = 512
VMEM_LIMIT = 60 * 1024 * 1024


def params(*semantics):
    return pltpu.CompilerParams(dimension_semantics=semantics or None, vmem_limit_bytes=VMEM_LIMIT)


def cost(flops, data):
    return pl.CostEstimate(flops=int(flops), bytes_accessed=int(data), transcendentals=0)


def whole(shape):
    zero = (0,) * len(shape)
    return pl.BlockSpec(shape, lambda *_: zero)


ANYWHERE = pl.BlockSpec(memory_space=pl.ANY)


def attention_tables(segs):
    order = jnp.where(segs == 0, 1 << 20, segs)
    seqs, length = segs.shape
    first = order[:, ::QB]
    last = order[:, QB - 1 :: QB]
    lo = jnp.sum((order[:, None, :] < first[:, :, None]).astype(jnp.int32), axis=2) // KB
    hi = (jnp.sum((order[:, None, :] <= last[:, :, None]).astype(jnp.int32), axis=2) + KB - 1) // KB
    ids = jnp.arange(128, dtype=jnp.int32)[None, :]
    onehot = (segs.reshape(-1)[:, None] == ids) | ((ids >= 8) & (ids < 16))
    differ = segs[:, None, :] != jnp.arange(8, dtype=jnp.int32)[None, :, None]
    return lo, hi, onehot.astype(BF), jnp.where(differ, NEG, 0.0)


def attention_fwd(qkv, lo, hi, onehot, miss, part, earlier=()):
    seqs = lo.shape[0]
    rows = qkv.shape[0] // seqs
    wide = WIDE
    width = qkv.shape[1] // 3
    col = lambda at: pl.BlockSpec((rows, wide), lambda s, *_: (s, at))
    return pl.pallas_call(
        functools.partial(attn_fwd_kernel, len(earlier)),
        grid_spec=pltpu.PrefetchScalarGridSpec(
            num_scalar_prefetch=2,
            grid=(seqs,),
            in_specs=[
                col(3 * part), col(3 * part + 1), col(3 * part + 2),
                pl.BlockSpec((rows, 128), lambda s, *_: (s, 0)),
                pl.BlockSpec((1, 8, rows), lambda s, *_: (s, 0, 0)),
            ]
            + [ANYWHERE] * len(earlier),
            out_specs=[
                col(part),
                pl.BlockSpec((1, wide, rows), lambda s, *_: (s, part, 0)),
                pl.BlockSpec((1, 1, wide // HD, rows), lambda s, *_: (s, part, 0, 0)),
            ],
            scratch_shapes=[
                pltpu.VMEM((wide, rows), BF),
                pltpu.VMEM((wide, rows), BF),
                pltpu.VMEM((wide // HD, 16, rows), BF),
                pltpu.VMEM((8, rows), F32),
            ],
        ),
        out_shape=[
            jax.ShapeDtypeStruct((qkv.shape[0], width), BF),
            jax.ShapeDtypeStruct((seqs, width, rows), F32),
            jax.ShapeDtypeStruct((seqs, width // wide, wide // HD, rows), F32),
        ],
        input_output_aliases={7 + i: i for i in range(len(earlier))},
        compiler_params=params("arbitrary"),
        cost_estimate=cost(12e9, 2e7),
        name="attention_forward",
    )(lo, hi, qkv, qkv, qkv, onehot, miss, *earlier)


def attention_bwd(qkv, d_attn, ot, lse, lo, hi, onehot, miss, part):
    seqs = lo.shape[0]
    rows = qkv.shape[0] // seqs
    wide = WIDE
    col = lambda at: pl.BlockSpec((rows, wide), lambda s, lo, hi, p: (s, 3 * p[0] + at))
    return pl.pallas_call(
        attn_bwd_kernel,
        grid_spec=pltpu.PrefetchScalarGridSpec(
            num_scalar_prefetch=3,
            grid=(seqs,),
            in_specs=[
                col(0), col(1), col(2),
                pl.BlockSpec((rows, wide), lambda s, lo, hi, p: (s, p[0])),
                pl.BlockSpec((1, wide, rows), lambda s, lo, hi, p: (s, p[0], 0)),
                pl.BlockSpec((1, 1, wide // HD, rows), lambda s, lo, hi, p: (s, p[0], 0, 0)),
                pl.BlockSpec((rows, 128), lambda s, *_: (s, 0)),
                pl.BlockSpec((1, 8, rows), lambda s, *_: (s, 0, 0)),
            ],
            out_specs=pl.BlockSpec((rows, 3 * wide), lambda s, *_: (s, 0)),
            scratch_shapes=[
                pltpu.VMEM((wide, rows), BF),
                pltpu.VMEM((wide, rows), BF),
                pltpu.VMEM((wide, rows), BF),
                pltpu.VMEM((wide // HD, 16, rows), BF),
                pltpu.VMEM((wide // HD, 16, rows), BF),
                pltpu.VMEM((wide, rows), F32),
                pltpu.VMEM((wide, rows), F32),
                pltpu.VMEM((wide, rows), F32),
            ],
        ),
        out_shape=jax.ShapeDtypeStruct((qkv.shape[0], 3 * wide), BF),
        compiler_params=params("arbitrary"),
        cost_estimate=cost(22e9, 2e7),
        name="attention_backward",
    )(lo, hi, part, qkv, qkv, qkv, d_attn, ot, lse, onehot, miss)


def normalized(x):
    mean = jnp.mean(x, axis=-1, keepdims=True)
    centered = x - mean
    scale = lax.rsqrt(jnp.mean(centered * centered, axis=-1, keepdims=True) + EPSILON)
    return centered * scale, scale


def norm_back(d, xhat, scale, gain):
    e = d * gain
    return scale * (e - jnp.mean(e, axis=-1, keepdims=True) - xhat * jnp.mean(e * xhat, axis=-1, keepdims=True))


def clear_first(*refs):
    @pl.when(pl.program_id(0) == 0)
    def _():
        for ref in refs:
            ref[...] = jnp.zeros_like(ref)


def add_row(ref, row, values):
    ref[row : row + 1, 0 : values.shape[1]] += jnp.sum(values, axis=0, keepdims=True)


def fetch(place, core, held, other, spots, outs, sems):
    for c in range(2):

        @pl.when(core[0] == c)
        def _(c=c):
            for h in range(2):
                src = held if h == c else other
                for chip in range(place.shape[1]):
                    for row, count, which, target in spots(h, chip):
                        pltpu.make_async_copy(
                            src.at[place[h, chip], pl.ds(row, count), :], outs[which].at[target], sems.at[which]
                        ).start()


def fetched(out, sem):
    pltpu.make_async_copy(out, out, sem).wait()


def qkv_kernel(spots, place, core, tok, vec, bias, held, other, n1, qkv, w, sem):
    if spots is not None:

        @pl.when(pl.program_id(0) == 0)
        def _():
            fetch(place, core, held, other, spots, [w], sem)

    xhat, _ = normalized(tok[...].astype(F32))
    n = (xhat * vec[0:1] + vec[1:2]).astype(BF)
    n1[...] = n
    if spots is not None:

        @pl.when(pl.program_id(0) == 0)
        def _():
            fetched(w, sem.at[0])

    qkv[...] = (mm(n, w[...] if spots is not None else held[...]) + bias[...]).astype(BF)


def project_qkv(tokens, vec, bias, held, other, place, core, spots):
    count, width = tokens.shape
    cols = 3 * width
    tile = lambda w: pl.BlockSpec((TILE, w), lambda i, *_: (i, 0))
    return pl.pallas_call(
        functools.partial(qkv_kernel, spots),
        grid_spec=pltpu.PrefetchScalarGridSpec(
            num_scalar_prefetch=2,
            grid=(count // TILE,),
            in_specs=[tile(width), whole(vec.shape), whole(bias.shape), ANYWHERE, ANYWHERE],
            out_specs=[tile(width), tile(cols), whole((width, cols))],
            scratch_shapes=[pltpu.SemaphoreType.DMA((1,))],
        ),
        out_shape=[
            jax.ShapeDtypeStruct((count, width), BF),
            jax.ShapeDtypeStruct((count, cols), BF),
            jax.ShapeDtypeStruct((width, cols), BF),
        ],
        compiler_params=params("arbitrary"),
        cost_estimate=cost(2 * count * width * cols, 2e7),
        name="norm_and_qkv",
    )(place, core, tokens, vec, bias, held, other)


STRIP = 256
CURVE = 0.7978845608028654
CUBIC = 0.044715


def up_kernel(spots, place, core, attn, tok, vec, b1, held, other, mid, n2, pre, act, wo, w1, sem):
    @pl.when(pl.program_id(0) == 0)
    def _():
        fetch(place, core, held, other, spots, [wo, w1], sem)
        fetched(wo, sem.at[0])

    x = tok[...].astype(F32) + mm(attn[...], wo[...]) + vec[2:3]
    mid[...] = x
    xhat, _ = normalized(x)
    n = (xhat * vec[0:1] + vec[1:2]).astype(BF)
    n2[...] = n

    @pl.when(pl.program_id(0) == 0)
    def _():
        fetched(w1, sem.at[1])

    width = STRIP
    for j in range(w1.shape[1] // width):
        cols = slice(j * width, (j + 1) * width)
        u = mm(n, w1[:, cols]) + b1[:, cols]
        pre[:, cols] = u
        th = jnp.tanh(u * (CURVE + (CURVE * CUBIC) * (u * u)))
        act[:, cols] = (u * (0.5 + 0.5 * th)).astype(BF)


def up_part(attn, tokens, vec, b1, held, other, place, core, spots):
    count, width = tokens.shape
    hidden = b1.shape[1]
    rows = TILE // 2
    tile = lambda w: pl.BlockSpec((rows, w), lambda i, *_: (i, 0))
    return pl.pallas_call(
        functools.partial(up_kernel, spots),
        grid_spec=pltpu.PrefetchScalarGridSpec(
            num_scalar_prefetch=2,
            grid=(count // rows,),
            in_specs=[tile(width), tile(width), whole(vec.shape), whole(b1.shape), ANYWHERE, ANYWHERE],
            out_specs=[
                tile(width), tile(width), tile(hidden), tile(hidden), whole((width, width)), whole((width, hidden)),
            ],
            scratch_shapes=[pltpu.SemaphoreType.DMA((2,))],
        ),
        out_shape=[
            jax.ShapeDtypeStruct((count, width), F32),
            jax.ShapeDtypeStruct((count, width), BF),
            jax.ShapeDtypeStruct((count, hidden), F32),
            jax.ShapeDtypeStruct((count, hidden), BF),
            jax.ShapeDtypeStruct((width, width), BF),
            jax.ShapeDtypeStruct((width, hidden), BF),
        ],
        compiler_params=params("arbitrary"),
        cost_estimate=cost(2 * count * width * (width + hidden), 6e7),
        name="out_and_up",
    )(place, core, attn, tokens, vec, b1, held, other)


def down_kernel(
    spots, place, core, act, mid, pre, cot, vec, w1, wo, held, other,
    out, d_pre, d_mid, d_branch, d_attn, sums, sum_up, w2, sem,
):
    @pl.when(pl.program_id(0) == 0)
    def _():
        fetch(place, core, held, other, spots, [w2], sem)
        fetched(w2, sem.at[0])

    clear_first(sums, sum_up)
    x = mid[...]
    width = x.shape[1]
    d_out = cot[...]
    d_n2 = None
    y = x + vec[3:4]
    for j in range(act.shape[1] // width):
        cols = slice(j * width, (j + 1) * width)
        d_act = mm_nt(d_out, w2[cols, :])
        y = y + mm(act[:, cols], w2[cols, :])
        u = pre[:, cols]
        square = u * u
        th = jnp.tanh(u * (CURVE + (CURVE * CUBIC) * square))
        slope = (0.5 + 0.5 * th) + (0.5 * u) * (1.0 - th * th) * (CURVE + (3.0 * CURVE * CUBIC) * square)
        low = (d_act * slope).astype(BF)
        d_pre[:, cols] = low
        sum_up[:, cols] += jnp.sum(low.astype(F32), axis=0, keepdims=True)
        part = mm_nt(low, w1[:, cols])
        d_n2 = part if d_n2 is None else d_n2 + part
    out[...] = y.astype(BF)
    xhat, scale = normalized(x)
    add_row(sums, 0, d_n2 * xhat)
    add_row(sums, 1, d_n2)
    g = d_out.astype(F32)
    add_row(sums, 3, g)
    d = g + norm_back(d_n2, xhat, scale, vec[0:1])
    d_mid[...] = d
    low = d.astype(BF)
    d_branch[...] = low
    add_row(sums, 2, low.astype(F32))
    d_attn[...] = mm_nt(low, wo[...]).astype(BF)


def down_part(act, mid, pre, cotangent, vec, w1, wo, held, other, place, core, spots):
    count, width = mid.shape
    hidden = act.shape[1]
    rows = TILE // 2
    tile = lambda w: pl.BlockSpec((rows, w), lambda i, *_: (i, 0))
    return pl.pallas_call(
        functools.partial(down_kernel, spots),
        grid_spec=pltpu.PrefetchScalarGridSpec(
            num_scalar_prefetch=2,
            grid=(count // rows,),
            in_specs=[
                tile(hidden), tile(width), tile(hidden), tile(width), whole(vec.shape), whole(w1.shape),
                whole(wo.shape), ANYWHERE, ANYWHERE,
            ],
            out_specs=[
                tile(width), tile(hidden), tile(width), tile(width), tile(width), whole((8, width)), whole((1, hidden)),
            ],
            scratch_shapes=[pltpu.VMEM((hidden, width), BF), pltpu.SemaphoreType.DMA((1,))],
        ),
        out_shape=[
            jax.ShapeDtypeStruct((count, width), BF),
            jax.ShapeDtypeStruct((count, hidden), BF),
            jax.ShapeDtypeStruct((count, width), F32),
            jax.ShapeDtypeStruct((count, width), BF),
            jax.ShapeDtypeStruct((count, width), BF),
            jax.ShapeDtypeStruct((8, width), F32),
            jax.ShapeDtypeStruct((1, hidden), F32),
        ],
        compiler_params=params("arbitrary"),
        cost_estimate=cost(2 * count * width * (width + 3 * hidden), 8e7),
        name="down_and_back",
    )(place, core, act, mid, pre, cotangent, vec, w1, wo, held, other)


def first_norm_kernel(parts, far, near, w_far, w_near, tok, d_mid, vec, out, sums):
    clear_first(sums)
    d = mm_nt(far[...], w_far[...]) + mm_nt(near[...], w_near[...])
    xhat, scale = normalized(tok[...].astype(F32))
    add_row(sums, 0, d * xhat)
    add_row(sums, 1, d)
    add_row(sums, 2, far[...].astype(F32))
    add_row(sums, 3, near[...].astype(F32))
    out[...] = (d_mid[...] + norm_back(d, xhat, scale, vec[0:1])).astype(BF)


def first_norm_back(far, near, w, tokens, d_mid, vec, parts):
    count, width = tokens.shape
    cols = far.shape[1]
    tile = lambda w: pl.BlockSpec((TILE, w), lambda i, p: (i, 0))
    return pl.pallas_call(
        first_norm_kernel,
        grid_spec=pltpu.PrefetchScalarGridSpec(
            num_scalar_prefetch=1,
            grid=(count // TILE,),
            in_specs=[
                tile(cols), tile(cols),
                pl.BlockSpec((width, cols), lambda i, p: (0, p[0])),
                pl.BlockSpec((width, cols), lambda i, p: (0, p[1])),
                tile(width), tile(width), whole(vec.shape),
            ],
            out_specs=[tile(width), whole((8, cols))],
        ),
        out_shape=[jax.ShapeDtypeStruct((count, width), BF), jax.ShapeDtypeStruct((8, cols), F32)],
        compiler_params=params("arbitrary"),
        cost_estimate=cost(4 * count * width * cols, 3e7),
        name="first_norm_back",
    )(parts, far, near, w, w, tokens, d_mid, vec)


def tn(a, b):
    return lax.dot_general(a, b, (((0,), (0,)), ((), ())), preferred_element_type=F32)


def spread_chunks(send_at, keep_at, acc, got, send, keep):
    def body(j, carry):
        for at, out in ((send_at, send), (keep_at, keep)):
            i = at[j]
            out[j] = (acc[i].astype(F32) + got[i].astype(F32)).astype(BF)
        return carry

    lax.fori_loop(0, send.shape[0], body, 0)


def grad_down_kernel(near, part, send_at, keep_at, cot, act, *refs):
    got, outs, (turned, acc) = (refs[0], refs[1:3], refs[3:]) if near else (None, refs[:1], (refs[1], refs[0]))
    step = pl.program_id(0)

    @pl.when(step == 0)
    def _():
        turned[...] = cot[...].T

    sums = mm(turned[...], act[...])
    chips, blocks, rows, _ = acc.shape
    some = chips // pl.num_programs(0)
    sums = (sums if near else sums.astype(BF)).T.reshape(act.shape[1] // (blocks * rows), blocks, rows, WIDE)
    acc[pl.ds(step * sums.shape[0], sums.shape[0])] = sums.astype(acc.dtype)
    if near:

        @pl.when(step == pl.num_programs(0) - 1)
        def _():
            spread_chunks(send_at, keep_at, acc, got, *outs)


def grad_cols_kernel(widths, near, part, send_at, keep_at, *refs):
    count = len(widths)
    ins, refs = refs[: 2 * count], refs[2 * count :]
    got, outs, acc = (refs[0], refs[1:3], refs[3]) if near else (None, refs[:1], refs[0])
    step = pl.program_id(0)
    chips, _, rows, _ = acc.shape
    at = base = 0
    for k, (blocks, steps) in enumerate(widths):
        for i in range(steps):

            @pl.when(step == at + i)
            def _(k=k, blocks=blocks, first=base + i * blocks):
                sums = tn(ins[2 * k][...], ins[2 * k + 1][...]).astype(acc.dtype)
                for b in range(blocks):
                    acc[:, first + b] = sums[:, b * WIDE : (b + 1) * WIDE].reshape(chips, rows, WIDE)

        at += steps
        base += steps * blocks
    if near:

        @pl.when(step == pl.num_programs(0) - 1)
        def _():
            spread_chunks(send_at, keep_at, acc, got, *outs)


def grad_call(kernel, steps, specs, arrays, shape, part, got, order, scratch, flops, name):
    near = got is not None
    chips = shape[0]
    out = jax.ShapeDtypeStruct(((chips // 2,) if near else (chips,)) + shape[1:], BF)
    spec = whole(out.shape)
    if near:
        specs, arrays = specs + [whole(got.shape)], arrays + [got]
        scratch = scratch + [pltpu.VMEM(shape, F32)]
    return pl.pallas_call(
        kernel,
        grid_spec=pltpu.PrefetchScalarGridSpec(
            num_scalar_prefetch=3,
            grid=(steps,),
            in_specs=specs,
            out_specs=[spec, spec] if near else spec,
            scratch_shapes=scratch,
        ),
        out_shape=[out, out] if near else out,
        compiler_params=params("arbitrary"),
        cost_estimate=cost(flops, 2e7),
        name=name,
    )(part, *(order or (part, part)), *arrays)


def grad_down(cot, act, part, chips, name, got=None, order=None):
    tokens, width = cot.shape
    hidden = act.shape[1]
    shape = (chips, 4, hidden // chips // 4, WIDE)
    specs = [
        pl.BlockSpec((tokens, WIDE), lambda i, p, *_: (0, p[0])),
        pl.BlockSpec((tokens, width), lambda i, *_: (0, i)),
    ]
    return grad_call(
        functools.partial(grad_down_kernel, got is not None), hidden // width, specs, [cot, act], shape, part, got,
        order, [pltpu.VMEM((WIDE, tokens), BF)], 2 * tokens * WIDE * hidden, name,
    )


def grad_cols(pairs, part, chips, name, got=None, order=None):
    tokens, width = pairs[0][0].shape
    specs, arrays, widths, at, flops = [], [], [], 0, 0
    for lhs, rhs, blocks, steps, by_part in pairs:
        def column(i, p, *_, at=at, steps=steps, by_part=by_part):
            j = jnp.clip(i - at, 0, steps - 1)
            return (0, p[0] * steps + j if by_part else j)

        specs += [pl.BlockSpec((tokens, width), lambda i, *_: (0, 0)), pl.BlockSpec((tokens, blocks * WIDE), column)]
        arrays += [lhs, rhs]
        widths.append((blocks, steps))
        at += steps
        flops += 2 * tokens * width * WIDE * blocks * steps
    shape = (chips, sum(b * s for b, s in widths), width // chips, WIDE)
    return grad_call(
        functools.partial(grad_cols_kernel, tuple(widths), got is not None), at, specs, arrays, shape, part, got,
        order, [], flops, name,
    )


def here():
    me = lax.axis_index("fsdp")
    return me // 8, (me // 4) % 2, (me // 2) % 2, me % 2


def pairs_of(devices, move):
    depth = devices // 8
    found = []
    for i in range(devices):
        z, y, x, c = move(i // 8, (i // 4) % 2, (i // 2) % 2, i % 2)
        found.append((i, (((z % depth) * 2 + y) * 2 + x) * 2 + c))
    return found


class Moves:
    def __init__(self, devices):
        self.depth = devices // 8
        self.chips = devices // 2
        self.core = pairs_of(devices, lambda z, y, x, c: (z, y, x, 1 - c))
        self.first = pairs_of(devices, lambda z, y, x, c: (z, 1 - y, x, c) if c == 0 else (z, y, 1 - x, c))
        self.second = pairs_of(devices, lambda z, y, x, c: (z, y, 1 - x, c) if c == 0 else (z, 1 - y, x, c))
        self.deep = [pairs_of(devices, lambda z, y, x, c, k=k: (z + k, y, x, c)) for k in range(self.depth)]


def swap(x, moves):
    return lax.ppermute(x, "fsdp", moves)


def of_two(pick_second, a, b):
    return jnp.where(pick_second, b, a)


def pair_kernel(blocks, core, own, got, chunk):
    for c in range(2):

        @pl.when(core[0] == c)
        def _(c=c):
            parts = (own, got) if c == 0 else (got, own)
            at = 0
            for size in blocks:
                for k in range(2):
                    chunk[0, 2 * at + k * size : 2 * at + (k + 1) * size, :] = parts[k][at : at + size, :]
                at += size


def pair_rows(own, got, blocks, core):
    shape = jax.ShapeDtypeStruct((1, 2 * own.shape[0], own.shape[1]), BF)
    return pl.pallas_call(
        functools.partial(pair_kernel, blocks),
        grid_spec=pltpu.PrefetchScalarGridSpec(
            num_scalar_prefetch=1,
            grid=(1,),
            in_specs=[whole(own.shape), whole(own.shape)],
            out_specs=whole(shape.shape),
        ),
        out_shape=shape,
        name="pair_rows",
    )(core, own, got)


def pack_kernel(core, *refs):
    (wqkv, small, wo, w1, w2), outs = refs[:5], refs[5:]
    width = wo.shape[1]
    for c in range(2):

        @pl.when(core[0] == c)
        def _(c=c):
            for h in range(2):
                first, second, third = outs[:3] if h == c else outs[3:]
                rows = wo.shape[0]
                for t in range(3):
                    first[rows * t : rows * (t + 1), :] = wqkv[:, t * width + h * WIDE : t * width + (h + 1) * WIDE].astype(BF)
                first[3 * rows :, :] = small[...].astype(BF)
                second[0:rows, :] = wo[:, h * WIDE : (h + 1) * WIDE].astype(BF)
                for b in range(4):
                    cols = slice((4 * h + b) * WIDE, (4 * h + b + 1) * WIDE)
                    second[rows * (1 + b) : rows * (2 + b), :] = w1[:, cols].astype(BF)
                third[...] = w2[:, h * WIDE : (h + 1) * WIDE].astype(BF)


def pack(wqkv, small, wo, w1, w2, core):
    rows = wo.shape[0]
    ins = (wqkv, small, wo, w1, w2)
    shapes = [(3 * rows + small.shape[0], WIDE), (5 * rows, WIDE), (w2.shape[0], WIDE)] * 2
    return pl.pallas_call(
        pack_kernel,
        grid_spec=pltpu.PrefetchScalarGridSpec(
            num_scalar_prefetch=1,
            grid=(1,),
            in_specs=[whole(x.shape) for x in ins],
            out_specs=[whole(s) for s in shapes],
        ),
        out_shape=[jax.ShapeDtypeStruct(s, BF) for s in shapes],
        name="pack_shards",
    )(core, *ins)


def gate(x, *after):
    return lax.optimization_barrier((x,) + after)[0]


def chunk_places(moves):
    z, y, x, c = here()
    chip = jnp.arange(moves.chips, dtype=jnp.int32)
    deep = (z - chip // 4) % moves.depth
    far_y, far_x = (chip // 2) % 2 ^ y, chip % 2 ^ x
    half0 = (far_x * 2 + far_y) * moves.depth + deep
    half1 = (far_y * 2 + far_x) * moves.depth + deep
    return jnp.stack([half0, half1]).astype(jnp.int32), c.astype(jnp.int32).reshape(1)


def fold_kernel(send_at, keep_at, a_send, b_send, a_keep, b_keep, send, keep):
    send[...] = (a_send[...].astype(F32) + b_send[...].astype(F32)).astype(BF)
    keep[...] = (a_keep[...].astype(F32) + b_keep[...].astype(F32)).astype(BF)


def fold(a, b, send_at, keep_at):
    count = send_at.shape[0]
    block = (1,) + a.shape[1:]
    none = (0,) * (a.ndim - 1)
    sent = pl.BlockSpec(block, lambda j, s, k: (s[j],) + none)
    kept = pl.BlockSpec(block, lambda j, s, k: (k[j],) + none)
    out = pl.BlockSpec(block, lambda j, s, k: (j,) + none)
    shape = jax.ShapeDtypeStruct((count,) + a.shape[1:], BF)
    return pl.pallas_call(
        fold_kernel,
        grid_spec=pltpu.PrefetchScalarGridSpec(
            num_scalar_prefetch=2, grid=(count,), in_specs=[sent, sent, kept, kept], out_specs=[out, out]
        ),
        out_shape=[shape, shape],
        cost_estimate=pl.CostEstimate(flops=0, bytes_accessed=3 * 2 * a.size, transcendentals=0),
        name="fold_sums",
    )(send_at, keep_at, a, b, a, b)


def fold_places(moves):
    z, y, x, c = here()
    plane = jnp.arange(2 * moves.depth, dtype=jnp.int32)
    deep, side = plane // 2, plane % 2
    bit = jnp.where(c == 0, x, y)

    def spread(b):
        return jnp.where(c == 0, deep * 4 + side * 2 + b, deep * 4 + b * 2 + side).astype(jnp.int32)

    level = jnp.arange(moves.depth, dtype=jnp.int32)
    turn = (z + level) % moves.depth
    mine = jnp.where(c == 0, y, x)
    return (
        (spread(1 - bit), spread(bit)),
        ((turn * 2 + 1 - mine).astype(jnp.int32), (turn * 2 + mine).astype(jnp.int32)),
    )


def level_kernel(keep, got, first, *rest):
    first[...] = keep[0].astype(F32) + got[0].astype(F32)
    for k, out in enumerate(rest):
        out[...] = (keep[k + 1].astype(F32) + got[k + 1].astype(F32)).astype(BF)


def level(keep, got):
    shape = keep.shape[1:]
    outs = [jax.ShapeDtypeStruct(shape, F32)] + [jax.ShapeDtypeStruct(shape, BF)] * (keep.shape[0] - 1)
    return pl.pallas_call(
        level_kernel,
        in_specs=[whole(keep.shape)] * 2,
        out_specs=[whole(shape)] * keep.shape[0],
        grid=(1,),
        out_shape=outs,
        compiler_params=params("arbitrary"),
        cost_estimate=cost(0, 4 * keep.size),
        name="level_sums",
    )(keep, got)


def scattered_small(sums, moves, places):
    c = here()[3]
    odd = c == 1
    part = of_two(odd, sums[:, 0], sums[:, 1]) + swap(of_two(odd, sums[:, 1], sums[:, 0]), moves.core)
    for (send_at, keep_at), move in zip(places, (moves.second, moves.first)):
        part = jnp.take(part, keep_at, axis=0) + swap(jnp.take(part, send_at, axis=0), move)
    total = part[0]
    for k in range(1, moves.depth):
        total = total + swap(part[k], moves.deep[k])
    return total


def halves(total, cores_axis, moves):
    odd = here()[3] == 1
    zero = lax.index_in_dim(total, 0, cores_axis, keepdims=False)
    one = lax.index_in_dim(total, 1, cores_axis, keepdims=False)
    mine = of_two(odd, zero, one)
    got = swap(of_two(odd, one, zero), moves.core)
    return jnp.stack([of_two(odd, mine, got), of_two(odd, got, mine)])


def by_neighbours(devices, width, hidden, count):
    rows = width // devices
    fits = rows * devices == width and rows % 8 == 0 and devices % 8 == 0
    return fits and width == 2 * WIDE and hidden == 4 * width and count % TILE == 0


def weight_halves(w):
    rows = w.shape[0]
    return w.reshape(rows, 3, 2, WIDE).transpose(0, 2, 1, 3).reshape(rows, -1)


def local(
    tokens, segments, cotangent, ln1_gain, ln1_shift, w_qkv, bias_q, bias_v, w_out, bias_out,
    ln2_gain, ln2_shift, w_up, bias_up, w_down, bias_down, *, seq,
):
    masters = (
        ln1_gain, ln1_shift, w_qkv, bias_q, bias_v, w_out, bias_out,
        ln2_gain, ln2_shift, w_up, bias_up, w_down, bias_down,
    )
    count, width = tokens.shape
    tables = attention_tables(segments.reshape(-1, seq))
    run = by_chips if by_neighbours(lax.axis_size("fsdp"), width, w_up.shape[1], count) else by_collectives
    return run(tokens, cotangent, tables, masters)


def by_collectives(tokens, cotangent, tables, masters):
    def norm(x, gain, shift):
        return normalized(x)[0] * gain + shift

    width = tokens.shape[1]
    full = [lax.all_gather(m.astype(BF), "fsdp", axis=0, tiled=True) for m in masters]
    g1, c1, wqkv, bq, bv, wo, bo, g2, c2, w1, b1, w2, b2 = [p.astype(F32) if p.ndim == 1 else p for p in full]
    wqkv = weight_halves(wqkv)
    rows = tokens.astype(F32)
    n1 = norm(rows, g1, c1).astype(BF)
    bias = weight_halves(jnp.concatenate([bq, jnp.zeros_like(bq), bv])[None])
    qkv = (mm(n1, wqkv) + bias).astype(BF)
    kept = attention_fwd(qkv, *tables, 0)
    attn, attn_t, lse = attention_fwd(qkv, *tables, 1, tuple(kept))
    middle = rows + mm(attn, wo) + bo
    n2 = norm(middle, g2, c2).astype(BF)
    act_value, gelu_pull = jax.vjp(functools.partial(jax.nn.gelu, approximate=True), mm(n2, w1) + b1)
    act = act_value.astype(BF)
    layer_out = (middle + mm(act, w2) + b2).astype(BF)
    d_out = cotangent.astype(F32)
    d_pre = gelu_pull(mm_nt(cotangent, w2))[0].astype(BF)
    _, pull = jax.vjp(norm, middle, g2, c2)
    d_mid, d_g2, d_c2 = pull(mm_nt(d_pre, w1))
    d_mid = d_out + d_mid
    d_branch = d_mid.astype(BF)
    d_attn = mm_nt(d_branch, wo).astype(BF)
    parts = [
        attention_bwd(qkv, d_attn, attn_t, lse, *tables, jnp.full((1,), h, jnp.int32)) for h in range(2)
    ]
    d_qkv = jnp.concatenate(parts, axis=1)
    _, pull = jax.vjp(norm, rows, g1, c1)
    d_rows, d_g1, d_c1 = pull(mm_nt(d_qkv, wqkv))
    input_grad = (d_mid + d_rows).astype(BF)
    total = lambda x: jnp.sum(x.astype(F32), axis=0)
    by_part = lambda x: x.reshape(-1, 2, 3, WIDE).transpose(0, 2, 1, 3).reshape(x.shape)
    sums = by_part(total(d_qkv)[None])[0]
    grads = (
        d_g1, d_c1, by_part(tn(n1, d_qkv)), sums[:width], sums[2 * width :], tn(attn, d_branch), total(d_branch),
        d_g2, d_c2, tn(n2, d_pre), total(d_pre), tn(act, cotangent), total(d_out),
    )
    return (layer_out, input_grad) + tuple(
        lax.psum_scatter(g, "fsdp", scatter_dimension=0, tiled=True) for g in grads
    )


def by_chips(tokens, cotangent, tables, masters):
    devices = lax.axis_size("fsdp")
    moves = Moves(devices)
    chips = moves.chips
    count, width = tokens.shape
    ln1_gain, ln1_shift, w_qkv, bias_q, bias_v, w_out, bias_out, ln2_gain, ln2_shift, w_up, bias_up, w_down, bias_down = masters
    part = width // devices
    two = 2 * part
    hidden = w_up.shape[1]
    places, core = chunk_places(moves)

    small = jnp.concatenate([ln1_gain, ln1_shift, bias_q, bias_v, bias_out, ln2_gain, ln2_shift, bias_down, bias_up])
    small = jnp.pad(small[None], ((0, 7), (0, WIDE - small.shape[0])))
    own1, own2, own3, oth1, oth2, oth3 = pack(w_qkv, small, w_out, w_up, w_down, core)

    def deep(chunk):
        return jnp.concatenate([chunk] + [swap(chunk, moves.deep[k]) for k in range(1, moves.depth)], axis=0)

    def along(held, move):
        return jnp.concatenate([held, swap(held, move)], axis=0)

    got1, got2, got3 = swap(oth1, moves.core), swap(oth2, moves.core), swap(oth3, moves.core)
    chunk1 = pair_rows(own1, got1, [part] * 3 + [8], core)
    chunk2 = pair_rows(own2, got2, [part] * 5, core)
    chunk3 = pair_rows(own3, got3, [4 * part], core)
    held1 = deep(chunk1)
    held1 = along(held1, moves.first)
    deep2 = [swap(gate(chunk2, held1), moves.deep[k]) for k in range(1, moves.depth)]
    held1 = along(held1, moves.second)
    other1 = swap(held1, moves.core)

    vecs = jnp.take(held1[:, 6 * part :: 8], of_two(core[0] == 1, places[0], places[1]), axis=0)
    vecs = vecs.reshape(devices, WIDE).astype(F32)
    g1, c1, bq, bv, bo, g2, c2, b2 = [vecs[:, i * part : (i + 1) * part].reshape(-1) for i in range(8)]
    b1 = vecs[:, 8 * part : 12 * part].reshape(1, -1)
    bias = weight_halves(jnp.concatenate([bq, jnp.zeros_like(bq), bv])[None])

    def spots_qkv(h, chip):
        return [
            (two * t, two, 0, (pl.ds(two * chip, two), pl.ds((3 * h + t) * WIDE, WIDE))) for t in range(3)
        ]

    def spots_up(h, chip):
        rows = pl.ds(two * chip, two)
        return [(0, two, 0, (rows, pl.ds(h * WIDE, WIDE)))] + [
            (two * (1 + b), two, 1, (rows, pl.ds((4 * h + b) * WIDE, WIDE))) for b in range(4)
        ]

    def spots_down(h, chip):
        return [(0, 4 * two, 0, (pl.ds(4 * two * chip, 4 * two), pl.ds(h * WIDE, WIDE)))]

    n1, qkv, wqkv = project_qkv(tokens, jnp.stack([g1, c1]), bias, held1, other1, places, core, spots_qkv)
    deep2 = lax.optimization_barrier(tuple(deep2) + (qkv,))[:-1]
    held2 = along(jnp.concatenate([chunk2, *deep2], axis=0), moves.first)
    deep3 = [swap(gate(chunk3, held2), moves.deep[k]) for k in range(1, moves.depth)]
    kept = attention_fwd(gate(qkv, held2), *tables, 0)
    more2 = swap(held2, moves.second)
    *deep3, more2 = lax.optimization_barrier(tuple(deep3) + (more2, kept[0]))[:-1]
    held2 = jnp.concatenate([held2, more2], axis=0)
    held3 = jnp.concatenate([chunk3, *deep3], axis=0)
    kept = lax.optimization_barrier(tuple(kept) + (held2, held3))[:3]
    other2 = swap(held2, moves.core)
    more3 = swap(held3, moves.first)
    attn, attn_t, lse = attention_fwd(qkv, *tables, 1, tuple(kept))
    held3 = jnp.concatenate([held3, gate(more3, attn)], axis=0)
    more3 = swap(held3, moves.second)
    mid, n2, pre, act, wo, w1 = up_part(
        gate(attn, held3), tokens, jnp.stack([g2, c2, bo]), b1, held2, gate(other2, attn), places, core, spots_up
    )
    held3 = jnp.concatenate([held3, gate(more3, act)], axis=0)
    other3 = swap(held3, moves.core)

    far, near = 1 - core, core
    orders = fold_places(moves)
    sent_down = grad_down(gate(cotangent, held3), act, far, chips, "grad_down_far")
    got_down = swap(sent_down, moves.core)
    layer_out, d_pre, d_mid, d_branch, d_attn, sums2, sum_up = down_part(
        gate(act, sent_down), mid, pre, cotangent, jnp.stack([g2, g2, g2, b2]), w1, wo, held3, gate(other3, sent_down),
        places, core, spots_down,
    )
    ups = lambda n2: [(n2, d_pre, 2, 2, True), (attn, d_branch, 1, 1, True)]
    sent_up = grad_cols(ups(n2), far, chips, "grad_up_out_far")
    got_up = swap(sent_up, moves.core)
    send_down, keep_down = grad_down(
        gate(cotangent, sent_up), act, near, chips, "grad_down_near", gate(got_down, d_pre), orders[0]
    )
    got_down = swap(send_down, moves.second)
    send_up, keep_up = grad_cols(
        ups(gate(n2, send_down)), near, chips, "grad_up_out_near", gate(got_up, send_down), orders[0]
    )
    got_up = swap(send_up, moves.second)
    d_qkv_far = attention_bwd(qkv, gate(d_attn, send_up), attn_t, lse, *tables, far)
    send_down, keep_down = fold(keep_down, gate(got_down, d_qkv_far), *orders[1])
    got_down = swap(send_down, moves.first)
    send_up, keep_up = fold(keep_up, gate(got_up, d_qkv_far), *orders[1])
    got_up = swap(send_up, moves.first)
    sent_qkv = grad_cols(
        [(gate(n1, send_up, send_down), d_qkv_far, 3, 1, False)], far, chips, "grad_qkv_far"
    )
    got_qkv = swap(sent_qkv, moves.core)
    d_qkv_near = attention_bwd(qkv, gate(d_attn, sent_qkv), attn_t, lse, *tables, near)

    def spread(others):
        return [swap(x, moves.deep[k + 1]) for k, x in enumerate(others)]

    def total_of(first, gots):
        return sum((g.astype(F32) for g in gots), first)

    first_down, *rest_down = level(keep_down, gate(got_down, d_qkv_near))
    first_up, *rest_up = level(keep_up, gate(got_up, d_qkv_near))
    gots_down, gots_up = spread(rest_down), spread(rest_up)
    send_qkv, keep_qkv = grad_cols(
        [(gate(n1, first_down, first_up), d_qkv_near, 3, 1, False)], near, chips, "grad_qkv_near",
        gate(got_qkv, d_qkv_near), orders[0],
    )
    got_qkv = swap(send_qkv, moves.second)
    input_grad, sums1 = first_norm_back(
        d_qkv_far, gate(d_qkv_near, send_qkv), wqkv, tokens, d_mid, g1[None], jnp.concatenate([far, near])
    )
    send_qkv, keep_qkv = fold(keep_qkv, gate(got_qkv, sums1), *orders[1])
    got_qkv = swap(send_qkv, moves.first)

    odd = core[0] == 1
    by_half = [of_two(odd, sums1[3], sums1[2]), of_two(odd, sums1[2], sums1[3])]
    d_bq = jnp.concatenate([s[:WIDE] for s in by_half])
    d_bv = jnp.concatenate([s[2 * WIDE :] for s in by_half])
    vecs = [sums1[0, :width], sums1[1, :width], d_bq, d_bv, sums2[2], sums2[0], sums2[1], sums2[3]]
    small = jnp.concatenate([v.reshape(devices, part) for v in vecs] + [sum_up.reshape(devices, 4 * part)], axis=1)
    small = jnp.pad(small, ((0, 0), (0, WIDE - small.shape[1]))).reshape(chips, 2, WIDE)
    small = scattered_small(small, moves, orders)
    s = [small[i * part : (i + 1) * part] for i in range(8)]
    s_b1 = small[8 * part : 12 * part]

    total_down = total_of(first_down, gots_down)
    both_halves = halves(total_down.reshape(2, 4 * part, WIDE), 0, moves)
    g_down = both_halves.transpose(1, 0, 2).reshape(4 * part, width)
    total_up = total_of(first_up, gots_up)
    both_halves = halves(total_up.reshape(5, 2, part, WIDE), 1, moves)
    g_up = both_halves[:, :4].transpose(2, 0, 1, 3).reshape(part, hidden)
    g_out = both_halves[:, 4].transpose(1, 0, 2).reshape(part, width)
    first_qkv, *rest_qkv = level(keep_qkv, got_qkv)
    total_qkv = total_of(first_qkv, spread(rest_qkv))
    both_halves = halves(total_qkv.reshape(3, 2, part, WIDE), 1, moves)
    g_qkv = both_halves.transpose(2, 1, 0, 3).reshape(part, 3 * width)
    return (
        layer_out, input_grad, s[0], s[1], g_qkv, s[2], s[3], g_out, s[4], s[5], s[6], g_up, s_b1, g_down, s[7],
    )


MICRO = 2


def solution(mesh):
    line, table = P("fsdp"), P("fsdp", None)
    weights = (line, line, table, line, line, table, line, line, line, table, line, table, line)

    def step(tokens, *rest):
        seq = tokens.shape[0] // (mesh.shape["fsdp"] * MICRO)
        return jax.shard_map(
            functools.partial(local, seq=seq),
            mesh=mesh,
            in_specs=(table, line, table) + weights,
            out_specs=(table, table) + weights,
            check_vma=False,
        )(tokens, *rest)

    return step
```

time: 1010 us -> 507 us (0.50)
  matrix products: 375 us -> 0 us
  Pallas kernels: 0 us -> 311 us
  waiting for transfers between devices: 259 us -> 75.5 us
  local copies, waits for them, and re-layouts: 147 us -> 40.1 us
  other arithmetic: 117 us -> 12.2 us
  blocking collectives: 84.4 us -> 0 us
  starting transfers between devices: 0.33 us -> 60.4 us
  between operations: 15.7 us -> 1.84 us
    dot_general x108 -> x0, matrix products: 375 us -> none  [the longest x12 41.1 us: one_group(): jnp.einsum('qhd,khd->hqk', d_pair, split_pair(v_block), preferred_element...]
    pallas_call x0 -> x24, Pallas kernels: none -> 311 us  [the longest x6 71.6 us: grad_call(): pl.pallas_call(kernel, grid_spec=pltpu.PrefetchScalarGridSpec(num_scalar_...]
    reduce_scatter x4 -> x0, waiting for transfers between devices: 251 us -> none  [the longest x1 142 us: local(): lax.psum_scatter(accum[11], 'fsdp', scatter_dimension=0, tiled=True)]
    unnamed x2 -> x0, blocking collectives: 84.4 us -> none
    ppermute x0 -> x48, waiting for transfers between devices: none -> 75.5 us  [swap(): return lax.ppermute(x, 'fsdp', moves)]
    dynamic_slice x72 -> x0, local copies, waits for them, and re-layouts: 65.2 us -> none  [attention_forward(): lax.map(one_group, (heads_first(query), heads_first(keys), heads_first(va...]
    ppermute x0 -> x48, starting transfers between devices: none -> 60.4 us  [swap(): return lax.ppermute(x, 'fsdp', moves)]
    convert_element_type x36 -> x2, other arithmetic: 57.6 us -> 1.23 us  [the longest x1 1.16 us: attention_tables(): return (lo, hi, onehot.astype(BF), jnp.where(differ, NEG, 0.0))]
  transfers between devices with their start and end apart: 8 -> 48, of which waited for: 4 -> 16; matrix products, arithmetic and copies ran while one was open for 43% -> 6% of each run, Pallas kernels for 0% -> 42%
where the time goes in v1:
time: 507 us; the launch traced here: 501 us
  Pallas kernels  311 us (61%)
  waiting for transfers between devices  75.5 us (15%)
  starting transfers between devices  60.4 us (12%)
  local copies, waits for them, and re-layouts  40.1 us (8%)
  other arithmetic  12.2 us (2%)
    ppermute x48, waiting for transfers between devices, swap(): return lax.ppermute(x, 'fsdp', moves)  75.5 us
    pallas_call x6, Pallas kernels, grad_call(): pl.pallas_call(kernel, grid_spec=pltpu.PrefetchScalarGridSpec(num_scalar_...  71.6 us
    ppermute x48, starting transfers between devices, swap(): return lax.ppermute(x, 'fsdp', moves)  60.4 us
    pallas_call x2, Pallas kernels, attention_bwd(): pl.pallas_call(attn_bwd_kernel, grid_spec=pltpu.PrefetchScalarGridSpec(nu...  58.7 us
    pallas_call x1, Pallas kernels, down_part(): pl.pallas_call(functools.partial(down_kernel, spots), grid_spec=pltpu.Pre...  53.1 us
    pallas_call x2, Pallas kernels, attention_fwd(): pl.pallas_call(functools.partial(attn_fwd_kernel, len(earlier)), grid_spe...  37.5 us
    pallas_call x1, Pallas kernels, up_part(): pl.pallas_call(functools.partial(up_kernel, spots), grid_spec=pltpu.Prefe...  30.2 us
    unnamed x62, local copies, waits for them, and re-layouts  20.9 us
  transfers between devices with their start and end apart: 48, of which 16 were waited for; matrix products, arithmetic and copies ran while one was open for 6% of the time, Pallas kernels for 42%

profile of v1, /device:TPU:0, one launch (start us, length us, event | category | flops | bytes accessed | tf_op | source)
XLA Modules:
  0.0 500.9 jit_solution(15454577642171904261)
XLA Ops:
  17.2 4.8 collective-permute-done.2
  28.2 3.7 collective-permute-done.4
  34.2 12.6 %collective-permute-done.5 = bf16[8,160,384]{2,1,0:T(8,128)(2,1)S(1)} collective-permute-done((bf16[8,160,384]{2,1,0:T(8,128)(2,1)S(1)}, bf16[8,160,384]{2,1,0:T(8,128)(2,1)S(1)}, u32[]{:S(2)}, u32[]{:S(2)}) %collective-permute-start.5) | collective-permute-done | bytes 983072 | tf_op jit(solution)/shard_map/ppermute | solution.py:734
  53.9 4.2 collective-permute-start.10
  62.1 15.2 %norm_and_qkv.1 = (bf16[2048,768]{1,0:T(8,128)(2,1)}, bf16[2048,2304]{1,0:T(8,128)(2,1)}, bf16[768,2304]{1,0:T(8,128)(2,1)}) custom-call(s32[2,16]{1,0:T(2,128)} %pad_add_fusion.place, s32[1]{0:T(128)} %bitcast.core.part, bf16[2048,768]{1,0:T(8,128)(2,1)} %tok.5, f32[2,768]{1,0:T(2,128)} %pad_maximum_fusion.9.vec, f32[1,2304]{1,0:T(1,128)} %reshape.530.bias, ...), custom_call_target="tpu_custom_call" | custom-call | flops 7247757312 | bytes 20000000 | tf_op jit(solution)/shard_map/norm_and_qkv/pallas_call | solution.py:401
  83.9 5.2 %collective-permute-done.11 = bf16[4,240,384]{2,1,0:T(8,128)(2,1)S(1)} collective-permute-done((bf16[4,240,384]{2,1,0:T(8,128)(2,1)S(1)}, bf16[4,240,384]{2,1,0:T(8,128)(2,1)S(1)}, u32[]{:S(2)}, u32[]{:S(2)}) %collective-permute-start.11) | collective-permute-done | bytes 737312 | tf_op jit(solution)/shard_map/ppermute | solution.py:734
  96.4 3.8 collective-permute-start.13
  102.8 18.8 %attention_forward.2 = (bf16[2048,768]{1,0:T(8,128)(2,1)}, f32[2,768,1024]{2,1,0:T(8,128)}, f32[2,2,6,1024]{3,2,1,0:T(8,128)}) custom-call(s32[2,8]{1,0:T(2,128)} %get-tuple-element.282.lo, s32[2,8]{1,0:T(2,128)} %get-tuple-element.281.hi, bf16[2048,2304]{1,0:T(8,128)(2,1)} %get-tuple-element.115.q_ref.k_ref.v_ref, ...), custom_call_target="tpu_custom_call" | custom-call | flops 12000000000 | bytes 20000000 | tf_op jit(solution)/shard_map/attention_forward/pallas_call | solution.py:265
  125.1 18.7 %attention_forward.3 = (bf16[2048,768]{1,0:T(8,128)(2,1)}, f32[2,768,1024]{2,1,0:T(8,128)}, f32[2,2,6,1024]{3,2,1,0:T(8,128)}) custom-call(s32[2,8]{1,0:T(2,128)} %get-tuple-element.282.lo, s32[2,8]{1,0:T(2,128)} %get-tuple-element.281.hi, ...), custom_call_target="tpu_custom_call", output_to_operand_aliasing={{0}: (7, {}), {1}: (8, {}), {2}: (9, {})} | custom-call | flops 12000000000 | bytes 20000000 | tf_op jit(solution)/shard_map/attention_forward/pallas_call | solution.py:265
  148.6 30.2 %out_and_up.1 = (f32[2048,768]{1,0:T(8,128)}, bf16[2048,768]{1,0:T(8,128)(2,1)}, f32[2048,3072]{1,0:T(8,128)}, bf16[2048,3072]{1,0:T(8,128)(2,1)}, bf16[768,768]{1,0:T(8,128)(2,1)}, /*index=5*/bf16[768,3072]{1,0:T(8,128)(2,1)}) custom-call(s32[2,16]{1,0:T(2,128)} %pad_add_fusion.place, s32[1]{0:T(128)} %bitcast.core.part, ...), custom_call_target="tpu_custom_call" | custom-call | flops 12079595520 | bytes 60000000 | tf_op jit(solution)/shard_map/out_and_up/pallas_call | solution.py:456
  181.9 10.7 %grad_down_far.1 = bf16[16,4,48,384]{3,2,1,0:T(8,128)(2,1)} custom-call(s32[1]{0:T(128)S(6)} %sub.112.part.send_at.keep_at, s32[1]{0:T(128)S(6)} %sub.112.part.send_at.keep_at, s32[1]{0:T(128)S(6)} %sub.112.part.send_at.keep_at, bf16[2048,768]{1,0:T(8,128)(2,1)} %cot.3, bf16[2048,3072]{1,0:T(8,128)(2,1)} %get-tuple-element.136.act), custom_call_target="tpu_custom_call" | custom-call | flops 4831838208 | bytes 20000000 | tf_op jit(solution)/shard_map/grad_down_far/pallas_call | solution.py:659
  192.6 53.1 %down_and_back.1 = (bf16[2048,768]{1,0:T(8,128)(2,1)}, bf16[2048,3072]{1,0:T(8,128)(2,1)}, f32[2048,768]{1,0:T(8,128)}, bf16[2048,768]{1,0:T(8,128)(2,1)}, bf16[...) custom-call(s32[2,16]{1,0:T(2,128)} %pad_add_fusion.place, s32[1]{0:T(128)} %bitcast.core.part, ...), custom_call_target="tpu_custom_call" | custom-call | flops 31406948352 | bytes 80000000 | tf_op jit(solution)/shard_map/down_and_back/pallas_call | solution.py:528
  245.7 13.7 %grad_up_out_far.1 = bf16[16,5,48,384]{3,2,1,0:T(8,128)(2,1)} custom-call(s32[1]{0:T(128)S(6)} %sub.112.part.send_at.keep_at, s32[1]{0:T(128)S(6)} %sub.112.part.send_at.keep_at, s32[1]{0:T(128)S(6)} %sub.112.part.send_at.keep_at, bf16[2048,768]{1,0:T(8,128)(2,1)} %get-tuple-element.150.refs_0_, bf16[2048,3072]{1,0:T(8,128)(2,1)} %get-tuple-element.145.refs_1_, ...), custom_call_target="tpu_custom_call" | custom-call | flops 6039797760 | bytes 20000000 | tf_op jit(solution)/shard_map/grad_up_out_far/pallas_call | solution.py:659
  260.1 8.1 %collective-permute-done.21.refs_0_ = bf16[16,4,48,384]{3,2,1,0:T(8,128)(2,1)} collective-permute-done((bf16[16,4,48,384]{3,2,1,0:T(8,128)(2,1)S(1)}, bf16[16,4,48,384]{3,2,1,0:T(8,128)(2,1)}, u32[]{:S(2)}, u32[]{:S(2)}) %collective-permute-start.21) | collective-permute-done | bytes 2359328 | tf_op jit(solution)/shard_map/ppermute | solution.py:734
  268.2 12.9 %grad_down_near.1 = (bf16[8,4,48,384]{3,2,1,0:T(8,128)(2,1)}, bf16[8,4,48,384]{3,2,1,0:T(8,128)(2,1)}) custom-call(s32[1]{0:T(128)} %bitcast.core.part, s32[8]{0:T(128)} %copy-done.19, s32[8]{0:T(128)} %copy-done.20, bf16[2048,768]{1,0:T(8,128)(2,1)} %cot.3, bf16[2048,3072]{1,0:T(8,128)(2,1)} %get-tuple-element.136.act, ...), custom_call_target="tpu_custom_call" | custom-call | flops 4831838208 | bytes 20000000 | tf_op jit(solution)/shard_map/grad_down_near/pallas_call | solution.py:659
  281.9 15.2 %grad_up_out_near.1 = (bf16[8,5,48,384]{3,2,1,0:T(8,128)(2,1)}, bf16[8,5,48,384]{3,2,1,0:T(8,128)(2,1)}) custom-call(s32[1]{0:T(128)} %bitcast.core.part, s32[8]{0:T(128)} %copy-done.19, s32[8]{0:T(128)} %copy-done.20, bf16[2048,768]{1,0:T(8,128)(2,1)} %get-tuple-element.150.refs_0_, bf16[2048,3072]{1,0:T(8,128)(2,1)} %get-tuple-element.145.refs_1_, ...), custom_call_target="tpu_custom_call" | custom-call | flops 6039797760 | bytes 20000000 | tf_op jit(solution)/shard_map/grad_up_out_near/pallas_call | solution.py:659
  298.4 29.3 %attention_backward.2.refs_1_.far = bf16[2048,1152]{1,0:T(8,128)(2,1)} custom-call(s32[2,8]{1,0:T(2,128)} %get-tuple-element.282.lo, s32[2,8]{1,0:T(2,128)} %get-tuple-element.281.hi, s32[1]{0:T(128)S(6)} %sub.112.part.send_at.keep_at, bf16[2048,2304]{1,0:T(8,128)(2,1)} %get-tuple-element.115.q_ref.k_ref.v_ref, ...), custom_call_target="tpu_custom_call" | custom-call | flops 22000001024 | bytes 20000000 | tf_op jit(solution)/shard_map/attention_backward/pallas_call | solution.py:305
  328.8 4.4 fold_sums.4
  334.4 4.8 fold_sums.3
  339.3 8.8 %grad_qkv_far.1 = bf16[16,3,48,384]{3,2,1,0:T(8,128)(2,1)} custom-call(s32[1]{0:T(128)S(6)} %sub.112.part.send_at.keep_at, s32[1]{0:T(128)S(6)} %sub.112.part.send_at.keep_at, s32[1]{0:T(128)S(6)} %sub.112.part.send_at.keep_at, bf16[2048,768]{1,0:T(8,128)(2,1)} %get-tuple-element.171.refs_0_, bf16[2048,1152]{1,0:T(8,128)(2,1)} %attention_backward.2.refs_1_.far), custom_call_target="tpu_custom_call" | custom-call | flops 3623878656 | bytes 20000000 | tf_op jit(solution)/shard_map/grad_qkv_far/pallas_call | solution.py:659
  348.1 29.3 %attention_backward.3.refs_1_.near = bf16[2048,1152]{1,0:T(8,128)(2,1)} custom-call(s32[2,8]{1,0:T(2,128)} %get-tuple-element.282.lo, s32[2,8]{1,0:T(2,128)} %get-tuple-element.281.hi, s32[1]{0:T(128)} %bitcast.core.part, bf16[2048,2304]{1,0:T(8,128)(2,1)} %get-tuple-element.115.q_ref.k_ref.v_ref, bf16[2048,2304]{1,0:T(8,128)(2,1)} %get-tuple-element.115.q_ref.k_ref.v_ref, ...), custom_call_target="tpu_custom_call" | custom-call | flops 22000001024 | bytes 20000000 | tf_op jit(solution)/shard_map/attention_backward/pallas_call | solution.py:305
  389.4 5.0 %collective-permute-done.45 = bf16[4,48,384]{2,1,0:T(8,128)(2,1)S(1)} collective-permute-done((bf16[4,48,384]{2,1,0:T(8,128)(2,1)}, bf16[4,48,384]{2,1,0:T(8,128)(2,1)S(1)}, u32[]{:S(2)}, u32[]{:S(2)}) %collective-permute-start.45) | collective-permute-done | bytes 147488 | tf_op jit(solution)/shard_map/ppermute | solution.py:734
  401.0 3.2 collective-permute-start.40
  407.3 3.3 collective-permute-done.40
  410.6 7.5 %collective-permute-done.41 = bf16[5,48,384]{2,1,0:T(8,128)(2,1)S(1)} collective-permute-done((bf16[5,48,384]{2,1,0:T(8,128)(2,1)}, bf16[5,48,384]{2,1,0:T(8,128)(2,1)S(1)}, u32[]{:S(2)}, u32[]{:S(2)}) %collective-permute-start.41) | collective-permute-done | bytes 184352 | tf_op jit(solution)/shard_map/ppermute | solution.py:734
  419.2 10.3 %grad_qkv_near.1 = (bf16[8,3,48,384]{3,2,1,0:T(8,128)(2,1)}, bf16[8,3,48,384]{3,2,1,0:T(8,128)(2,1)}) custom-call(s32[1]{0:T(128)} %bitcast.core.part, s32[8]{0:T(128)} %copy-done.19, s32[8]{0:T(128)} %copy-done.20, bf16[2048,768]{1,0:T(8,128)(2,1)} %get-tuple-element.171.refs_0_, bf16[2048,1152]{1,0:T(8,128)(2,1)} %attention_backward.3.refs_1_.near, ...), custom_call_target="tpu_custom_call" | custom-call | flops 3623878656 | bytes 20000000 | tf_op jit(solution)/shard_map/grad_qkv_near/pallas_call | solution.py:659
  429.5 18.0 %first_norm_back.1 = (bf16[2048,768]{1,0:T(8,128)(2,1)}, f32[8,1152]{1,0:T(8,128)}) custom-call(s32[2]{0:T(128)} %pad_add_fusion.1.parts, bf16[2048,1152]{1,0:T(8,128)(2,1)} %attention_backward.2.refs_1_.far, bf16[2048,1152]{1,0:T(8,128)(2,1)} %attention_backward.3.refs_1_.near, bf16[768,2304]{1,0:T(8,128)(2,1)} %get-tuple-element.175.w_far.w_near, ...), custom_call_target="tpu_custom_call" | custom-call | flops 7247757312 | bytes 30000000 | tf_op jit(solution)/shard_map/first_norm_back/pallas_call | solution.py:572
  454.0 10.1 %collective-permute-done.29 = f32[8,384]{1,0:T(8,128)S(1)} collective-permute-done((f32[8,384]{1,0:T(8,128)S(1)}, f32[8,384]{1,0:T(8,128)S(1)}, u32[]{:S(2)}, u32[]{:S(2)}) %collective-permute-start.29) | collective-permute-done | bytes 12320 | tf_op jit(solution)/shard_map/ppermute | solution.py:734
  468.9 4.2 fold_sums.5
  473.2 4.5 collective-permute-start.31
  484.4 4.3 collective-permute-start.36
  493.5 3.5 collective-permute-done.37
  (267 shorter events, 117.5 us)
Async XLA Ops:
  10.8 11.2 %collective-permute-start.2 = (bf16[1,160,384]{2,1,0:T(8,128)(2,1)}, bf16[1,160,384]{2,1,0:T(8,128)(2,1)S(1)}, u32[]{:S(2)}, u32[]{:S(2)}) collective-permute-start(bf16[1,160,384]{2,1,0:T(8,128)(2,1)} %pair_rows.3), channel_id=1, source_target_pairs={{0,16},{1,17},{2,18},{3,19},{4,20},{5,21},{6,22},{7,23},{8,24},{9,... | collective-permute-start | bytes 368648 | tf_op jit(solution)/shard_map/ppermute | solution.py:734
  32.8 14.1 %collective-permute-start.5 = (bf16[8,160,384]{2,1,0:T(8,128)(2,1)S(1)}, bf16[8,160,384]{2,1,0:T(8,128)(2,1)S(1)}, u32[]{:S(2)}, u32[]{:S(2)}) collective-permute-start(bf16[8,160,384]{2,1,0:T(8,128)(2,1)S(1)} %get-tuple-element.225), channel_id=1, source_target_pairs={{0,2},{1,5},{2,0},{3,7},{4,6},{5,1},{6,4},{7,3},{8,10},{9,13},{10,... | collective-permute-start | bytes 2949128 | tf_op jit(solution)/shard_map/ppermute | solution.py:734
  47.9 14.2 %collective-permute-start.6 = (bf16[16,160,384]{2,1,0:T(8,128)(2,1)}, bf16[16,160,384]{2,1,0:T(8,128)(2,1)}, u32[]{:S(2)}, u32[]{:S(2)}) collective-permute-start(bf16[16,160,384]{2,1,0:T(8,128)(2,1)} %constant_dynamic-update-slice_fusion.5.held), channel_id=1, source_target_pairs={{0,1},{1,0},{2,3},{3,2},{4,5},{5,4},{6,7},{7,6},{8,9},{9,8},{10,11... | collective-permute-start | bytes 5898248 | tf_op jit(solution)/shard_map/ppermute | solution.py:734
  48.4 45.8 %collective-permute-start.12 = (bf16[96,384]{1,0:T(8,128)(2,1)S(1)}, bf16[96,384]{1,0:T(8,128)(2,1)S(1)}, u32[]{:S(2)}, u32[]{:S(2)}) collective-permute-start(bf16[96,384]{1,0:T(8,128)(2,1)S(1)} %copy-done.23), channel_id=1, source_target_pairs={{0,1},{1,0},{2,3},{3,2},{4,5},{5,4},{6,7},{7,6},{8,9},{9,8},{10,11... | collective-permute-start | bytes 221192 | tf_op jit(solution)/shard_map/ppermute | solution.py:734
  53.9 23.5 %collective-permute-start.10 = (bf16[1,240,384]{2,1,0:T(8,128)(2,1)}, bf16[1,240,384]{2,1,0:T(8,128)(2,1)S(1)}, u32[]{:S(2)}, u32[]{:S(2)}) collective-permute-start(bf16[1,240,384]{2,1,0:T(8,128)(2,1)} %pair_rows.4), channel_id=1, source_target_pairs={{0,24},{1,25},{2,26},{3,27},{4,28},{5,29},{6,30},{7,31},{8,0},{9,1... | collective-permute-start | bytes 552968 | tf_op jit(solution)/shard_map/ppermute | solution.py:734
  58.1 19.3 %collective-permute-start.8 = (bf16[1,240,384]{2,1,0:T(8,128)(2,1)}, bf16[1,240,384]{2,1,0:T(8,128)(2,1)S(1)}, u32[]{:S(2)}, u32[]{:S(2)}) collective-permute-start(bf16[1,240,384]{2,1,0:T(8,128)(2,1)} %pair_rows.4), channel_id=1, source_target_pairs={{0,8},{1,9},{2,10},{3,11},{4,12},{5,13},{6,14},{7,15},{8,16},{9,17... | collective-permute-start | bytes 552968 | tf_op jit(solution)/shard_map/ppermute | solution.py:734
  58.1 19.3 %collective-permute-start.9 = (bf16[1,240,384]{2,1,0:T(8,128)(2,1)}, bf16[1,240,384]{2,1,0:T(8,128)(2,1)S(1)}, u32[]{:S(2)}, u32[]{:S(2)}) collective-permute-start(bf16[1,240,384]{2,1,0:T(8,128)(2,1)} %pair_rows.4), channel_id=1, source_target_pairs={{0,16},{1,17},{2,18},{3,19},{4,20},{5,21},{6,22},{7,23},{8,24},{9,... | collective-permute-start | bytes 552968 | tf_op jit(solution)/shard_map/ppermute | solution.py:734
  77.6 11.5 %collective-permute-start.11 = (bf16[4,240,384]{2,1,0:T(8,128)(2,1)S(1)}, bf16[4,240,384]{2,1,0:T(8,128)(2,1)S(1)}, u32[]{:S(2)}, u32[]{:S(2)}) collective-permute-start(bf16[4,240,384]{2,1,0:T(8,128)(2,1)S(1)} %pad_maximum_fusion), channel_id=1, source_target_pairs={{0,4},{1,3},{2,6},{3,1},{4,0},{5,7},{6,2},{7,5},{8,12},{9,11},{10,... | collective-permute-start | bytes 2211848 | tf_op jit(solution)/shard_map/ppermute | solution.py:734
  91.7 29.9 %collective-permute-start.16 = (bf16[8,240,384]{2,1,0:T(8,128)(2,1)}, bf16[8,240,384]{2,1,0:T(8,128)(2,1)S(1)}, u32[]{:S(2)}, u32[]{:S(2)}) collective-permute-start(bf16[8,240,384]{2,1,0:T(8,128)(2,1)} %get-tuple-element.220), channel_id=1, source_target_pairs={{0,2},{1,5},{2,0},{3,7},{4,6},{5,1},{6,4},{7,3},{8,10},{9,13},{10,... | collective-permute-start | bytes 4423688 | tf_op jit(solution)/shard_map/ppermute | solution.py:734
  96.4 25.1 %collective-permute-start.13 = (bf16[1,192,384]{2,1,0:T(8,128)(2,1)}, bf16[1,192,384]{2,1,0:T(8,128)(2,1)S(1)}, u32[]{:S(2)}, u32[]{:S(2)}) collective-permute-start(bf16[1,192,384]{2,1,0:T(8,128)(2,1)} %pair_rows.5), channel_id=1, source_target_pairs={{0,8},{1,9},{2,10},{3,11},{4,12},{5,13},{6,14},{7,15},{8,16},{9,17... | collective-permute-start | bytes 442376 | tf_op jit(solution)/shard_map/ppermute | solution.py:734
  100.3 21.3 %collective-permute-start.14 = (bf16[1,192,384]{2,1,0:T(8,128)(2,1)}, bf16[1,192,384]{2,1,0:T(8,128)(2,1)S(1)}, u32[]{:S(2)}, u32[]{:S(2)}) collective-permute-start(bf16[1,192,384]{2,1,0:T(8,128)(2,1)} %pair_rows.5), channel_id=1, source_target_pairs={{0,16},{1,17},{2,18},{3,19},{4,20},{5,21},{6,22},{7,23},{8,24},{9,... | collective-permute-start | bytes 442376 | tf_op jit(solution)/shard_map/ppermute | solution.py:734
  100.3 21.3 %collective-permute-start.15 = (bf16[1,192,384]{2,1,0:T(8,128)(2,1)}, bf16[1,192,384]{2,1,0:T(8,128)(2,1)S(1)}, u32[]{:S(2)}, u32[]{:S(2)}) collective-permute-start(bf16[1,192,384]{2,1,0:T(8,128)(2,1)} %pair_rows.5), channel_id=1, source_target_pairs={{0,24},{1,25},{2,26},{3,27},{4,28},{5,29},{6,30},{7,31},{8,0},{9,1... | collective-permute-start | bytes 442376 | tf_op jit(solution)/shard_map/ppermute | solution.py:734
  122.8 25.8 %collective-permute-start.18 = (bf16[16,240,384]{2,1,0:T(8,128)(2,1)}, bf16[16,240,384]{2,1,0:T(8,128)(2,1)}, u32[]{:S(2)}, u32[]{:S(2)}) collective-permute-start(bf16[16,240,384]{2,1,0:T(8,128)(2,1)} %constant_dynamic-update-slice_fusion.16.held), channel_id=1, source_target_pairs={{0,1},{1,0},{2,3},{3,2},{4,5},{5,4},{6,7},{7,6},{8,9},{9,8},{10,11... | collective-permute-start | bytes 8847368 | tf_op jit(solution)/shard_map/ppermute | solution.py:734
  124.0 22.1 %collective-permute-start.17 = (bf16[4,192,384]{2,1,0:T(8,128)(2,1)S(1)}, bf16[4,192,384]{2,1,0:T(8,128)(2,1)S(1)}, u32[]{:S(2)}, u32[]{:S(2)}) collective-permute-start(bf16[4,192,384]{2,1,0:T(8,128)(2,1)S(1)} %pad_maximum_fusion.1), channel_id=1, source_target_pairs={{0,4},{1,3},{2,6},{3,1},{4,0},{5,7},{6,2},{7,5},{8,12},{9,11},{10,... | collective-permute-start | bytes 1769480 | tf_op jit(solution)/shard_map/ppermute | solution.py:734
  147.2 31.6 %collective-permute-start.19 = (bf16[8,192,384]{2,1,0:T(8,128)(2,1)}, bf16[8,192,384]{2,1,0:T(8,128)(2,1)S(1)}, u32[]{:S(2)}, u32[]{:S(2)}) collective-permute-start(bf16[8,192,384]{2,1,0:T(8,128)(2,1)} %get-tuple-element.222), channel_id=1, source_target_pairs={{0,2},{1,5},{2,0},{3,7},{4,6},{5,1},{6,4},{7,3},{8,10},{9,13},{10,... | collective-permute-start | bytes 3538952 | tf_op jit(solution)/shard_map/ppermute | solution.py:734
  180.0 12.6 %collective-permute-start.20 = (bf16[16,192,384]{2,1,0:T(8,128)(2,1)}, bf16[16,192,384]{2,1,0:T(8,128)(2,1)}, u32[]{:S(2)}, u32[]{:S(2)}) collective-permute-start(bf16[16,192,384]{2,1,0:T(8,128)(2,1)} %constant_dynamic-update-slice_fusion.27.held), channel_id=1, source_target_pairs={{0,1},{1,0},{2,3},{3,2},{4,5},{5,4},{6,7},{7,6},{8,9},{9,8},{10,11... | collective-permute-start | bytes 7077896 | tf_op jit(solution)/shard_map/ppermute | solution.py:734
  259.4 22.6 %collective-permute-start.22 = (bf16[16,5,48,384]{3,2,1,0:T(8,128)(2,1)}, bf16[16,5,48,384]{3,2,1,0:T(8,128)(2,1)}, u32[]{:S(2)}, u32[]{:S(2)}) collective-permute-start(bf16[16,5,48,384]{3,2,1,0:T(8,128)(2,1)} %grad_up_out_far.1), channel_id=1, source_target_pairs={{0,1},{1,0},{2,3},{3,2},{4,5},{5,4},{6,7},{7,6},{8,9},{9,8},{10,11... | collective-permute-start | bytes 8847368 | tf_op jit(solution)/shard_map/ppermute | solution.py:734
  281.0 46.7 %collective-permute-start.24 = (bf16[8,4,48,384]{3,2,1,0:T(8,128)(2,1)}, bf16[8,4,48,384]{3,2,1,0:T(8,128)(2,1)S(1)}, u32[]{:S(2)}, u32[]{:S(2)}) collective-permute-start(bf16[8,4,48,384]{3,2,1,0:T(8,128)(2,1)} %get-tuple-element.149), channel_id=1, source_target_pairs={{0,2},{1,5},{2,0},{3,7},{4,6},{5,1},{6,4},{7,3},{8,10},{9,13},{10,... | collective-permute-start | bytes 3538952 | tf_op jit(solution)/shard_map/ppermute | solution.py:734
  297.2 36.1 %collective-permute-start.23 = (bf16[8,5,48,384]{3,2,1,0:T(8,128)(2,1)}, bf16[8,5,48,384]{3,2,1,0:T(8,128)(2,1)S(1)}, u32[]{:S(2)}, u32[]{:S(2)}) collective-permute-start(bf16[8,5,48,384]{3,2,1,0:T(8,128)(2,1)} %get-tuple-element.152), channel_id=1, source_target_pairs={{0,2},{1,5},{2,0},{3,7},{4,6},{5,1},{6,4},{7,3},{8,10},{9,13},{10,... | collective-permute-start | bytes 4423688 | tf_op jit(solution)/shard_map/ppermute | solution.py:734
  333.3 44.1 %collective-permute-start.25 = (bf16[4,4,48,384]{3,2,1,0:T(8,128)(2,1)}, bf16[4,4,48,384]{3,2,1,0:T(8,128)(2,1)S(1)}, u32[]{:S(2)}, u32[]{:S(2)}) collective-permute-start(bf16[4,4,48,384]{3,2,1,0:T(8,128)(2,1)} %get-tuple-element.162), channel_id=1, source_target_pairs={{0,4},{1,3},{2,6},{3,1},{4,0},{5,7},{6,2},{7,5},{8,12},{9,11},{10,... | collective-permute-start | bytes 1769480 | tf_op jit(solution)/shard_map/ppermute | solution.py:734
  348.1 71.1 %collective-permute-start.27 = (bf16[16,3,48,384]{3,2,1,0:T(8,128)(2,1)}, bf16[16,3,48,384]{3,2,1,0:T(8,128)(2,1)}, u32[]{:S(2)}, u32[]{:S(2)}) collective-permute-start(bf16[16,3,48,384]{3,2,1,0:T(8,128)(2,1)} %grad_qkv_far.1), channel_id=1, source_target_pairs={{0,1},{1,0},{2,3},{3,2},{4,5},{5,4},{6,7},{7,6},{8,9},{9,8},{10,11... | collective-permute-start | bytes 5308424 | tf_op jit(solution)/shard_map/ppermute | solution.py:734
  380.8 13.7 %collective-permute-start.45 = (bf16[4,48,384]{2,1,0:T(8,128)(2,1)}, bf16[4,48,384]{2,1,0:T(8,128)(2,1)S(1)}, u32[]{:S(2)}, u32[]{:S(2)}) collective-permute-start(bf16[4,48,384]{2,1,0:T(8,128)(2,1)} %get-tuple-element.193), channel_id=1, source_target_pairs={{0,16},{1,17},{2,18},{3,19},{4,20},{5,21},{6,22},{7,23},{8,24},{9,... | collective-permute-start | bytes 442376 | tf_op jit(solution)/shard_map/ppermute | solution.py:734
  383.5 11.0 %collective-permute-start.46 = (bf16[4,48,384]{2,1,0:T(8,128)(2,1)}, bf16[4,48,384]{2,1,0:T(8,128)(2,1)S(1)}, u32[]{:S(2)}, u32[]{:S(2)}) collective-permute-start(bf16[4,48,384]{2,1,0:T(8,128)(2,1)} %get-tuple-element.194), channel_id=1, source_target_pairs={{0,24},{1,25},{2,26},{3,27},{4,28},{5,29},{6,30},{7,31},{8,0},{9,1... | collective-permute-start | bytes 442376 | tf_op jit(solution)/shard_map/ppermute | solution.py:734
  384.8 13.0 %collective-permute-start.26 = (bf16[4,5,48,384]{3,2,1,0:T(8,128)(2,1)S(1)}, bf16[4,5,48,384]{3,2,1,0:T(8,128)(2,1)S(1)}, u32[]{:S(2)}, u32[]{:S(2)}) collective-permute-start(bf16[4,5,48,384]{3,2,1,0:T(8,128)(2,1)S(1)} %copy-done.21), channel_id=1, source_target_pairs={{0,4},{1,3},{2,6},{3,1},{4,0},{5,7},{6,2},{7,5},{8,12},{9,11},{10,... | collective-permute-start | bytes 2211848 | tf_op jit(solution)/shard_map/ppermute | solution.py:734
  395.5 11.1 %collective-permute-start.47 = (f32[96,384]{1,0:T(8,128)S(1)}, f32[96,384]{1,0:T(8,128)S(1)}, u32[]{:S(2)}, u32[]{:S(2)}) collective-permute-start(f32[96,384]{1,0:T(8,128)S(1)} %bitcast.91), channel_id=1, source_target_pairs={{0,1},{1,0},{2,3},{3,2},{4,5},{5,4},{6,7},{7,6},{8,9},{9,8},{10,11... | collective-permute-start | bytes 442376 | tf_op jit(solution)/shard_map/ppermute | solution.py:734
  404.2 13.9 %collective-permute-start.41 = (bf16[5,48,384]{2,1,0:T(8,128)(2,1)}, bf16[5,48,384]{2,1,0:T(8,128)(2,1)S(1)}, u32[]{:S(2)}, u32[]{:S(2)}) collective-permute-start(bf16[5,48,384]{2,1,0:T(8,128)(2,1)} %get-tuple-element.190), channel_id=1, source_target_pairs={{0,16},{1,17},{2,18},{3,19},{4,20},{5,21},{6,22},{7,23},{8,24},{9,... | collective-permute-start | bytes 552968 | tf_op jit(solution)/shard_map/ppermute | solution.py:734
  404.8 13.3 %collective-permute-start.42 = (bf16[5,48,384]{2,1,0:T(8,128)(2,1)}, bf16[5,48,384]{2,1,0:T(8,128)(2,1)S(1)}, u32[]{:S(2)}, u32[]{:S(2)}) collective-permute-start(bf16[5,48,384]{2,1,0:T(8,128)(2,1)} %get-tuple-element.191), channel_id=1, source_target_pairs={{0,24},{1,25},{2,26},{3,27},{4,28},{5,29},{6,30},{7,31},{8,0},{9,1... | collective-permute-start | bytes 552968 | tf_op jit(solution)/shard_map/ppermute | solution.py:734
  450.7 17.1 %collective-permute-start.34 = (bf16[8,3,48,384]{3,2,1,0:T(8,128)(2,1)}, bf16[8,3,48,384]{3,2,1,0:T(8,128)(2,1)S(1)}, u32[]{:S(2)}, u32[]{:S(2)}) collective-permute-start(bf16[8,3,48,384]{3,2,1,0:T(8,128)(2,1)} %get-tuple-element.173), channel_id=1, source_target_pairs={{0,2},{1,5},{2,0},{3,7},{4,6},{5,1},{6,4},{7,3},{8,10},{9,13},{10,... | collective-permute-start | bytes 2654216 | tf_op jit(solution)/shard_map/ppermute | solution.py:734
  452.7 11.4 %collective-permute-start.29 = (f32[8,384]{1,0:T(8,128)S(1)}, f32[8,384]{1,0:T(8,128)S(1)}, u32[]{:S(2)}, u32[]{:S(2)}) collective-permute-start(f32[8,384]{1,0:T(8,128)S(1)} %broadcast_select_fusion.2), channel_id=1, source_target_pairs={{0,2},{1,5},{2,0},{3,7},{4,6},{5,1},{6,4},{7,3},{8,10},{9,13},{10,... | collective-permute-start | bytes 36872 | tf_op jit(solution)/shard_map/ppermute | solution.py:734
  473.2 17.1 %collective-permute-start.31 = (f32[384]{0:T(512)S(1)}, f32[384]{0:T(512)S(1)}, u32[]{:S(2)}, u32[]{:S(2)}) collective-permute-start(f32[384]{0:T(512)S(1)} %get-tuple-element.203), channel_id=1, source_target_pairs={{0,8},{1,9},{2,10},{3,11},{4,12},{5,13},{6,14},{7,15},{8,16},{9,17... | collective-permute-start | bytes 4616 | tf_op jit(solution)/shard_map/ppermute | solution.py:734
  477.7 13.4 %collective-permute-start.32 = (f32[384]{0:T(512)S(1)}, f32[384]{0:T(512)S(1)}, u32[]{:S(2)}, u32[]{:S(2)}) collective-permute-start(f32[384]{0:T(512)S(1)} %get-tuple-element.205), channel_id=1, source_target_pairs={{0,16},{1,17},{2,18},{3,19},{4,20},{5,21},{6,22},{7,23},{8,24},{9,... | collective-permute-start | bytes 4616 | tf_op jit(solution)/shard_map/ppermute | solution.py:734
  479.2 11.9 %collective-permute-start.33 = (f32[384]{0:T(512)S(1)}, f32[384]{0:T(512)S(1)}, u32[]{:S(2)}, u32[]{:S(2)}) collective-permute-start(f32[384]{0:T(512)S(1)} %get-tuple-element.204), channel_id=1, source_target_pairs={{0,24},{1,25},{2,26},{3,27},{4,28},{5,29},{6,30},{7,31},{8,0},{9,1... | collective-permute-start | bytes 4616 | tf_op jit(solution)/shard_map/ppermute | solution.py:734
  (40 other events, 357.6 us)

commit v2 on v1

--- a/solution.py
+++ b/solution.py
@@ -78,9 +78,8 @@
 
 
 def attn_fwd_kernel(
-    earlier, lo, hi, q_ref, k_ref, v_ref, oh_ref, mr_ref, *rest
+    lo, hi, q_ref, k_ref, v_ref, oh_ref, mr_ref, o_ref, ot_ref, lse_ref, qt, vt, extra, tops
 ):
-    o_ref, ot_ref, lse_ref, qt, vt, extra, tops = rest[earlier:]
     seq = pl.program_id(0)
     rows = q_ref.shape[0]
     pairs = q_ref.shape[1] // 128
@@ -256,27 +255,27 @@
     return lo, hi, onehot.astype(BF), jnp.where(differ, NEG, 0.0)
 
 
-def attention_fwd(qkv, lo, hi, onehot, miss, part, earlier=()):
+def attention_fwd(qkv, lo, hi, onehot, miss):
     seqs = lo.shape[0]
     rows = qkv.shape[0] // seqs
     wide = WIDE
     width = qkv.shape[1] // 3
-    col = lambda at: pl.BlockSpec((rows, wide), lambda s, *_: (s, at))
+    parts = width // wide
+    col = lambda at: pl.BlockSpec((rows, wide), lambda s, j, *_: (s, 3 * j + at))
     return pl.pallas_call(
-        functools.partial(attn_fwd_kernel, len(earlier)),
+        attn_fwd_kernel,
         grid_spec=pltpu.PrefetchScalarGridSpec(
             num_scalar_prefetch=2,
-            grid=(seqs,),
+            grid=(seqs, parts),
             in_specs=[
-                col(3 * part), col(3 * part + 1), col(3 * part + 2),
+                col(0), col(1), col(2),
                 pl.BlockSpec((rows, 128), lambda s, *_: (s, 0)),
                 pl.BlockSpec((1, 8, rows), lambda s, *_: (s, 0, 0)),
-            ]
-            + [ANYWHERE] * len(earlier),
+            ],
             out_specs=[
-                col(part),
-                pl.BlockSpec((1, wide, rows), lambda s, *_: (s, part, 0)),
-                pl.BlockSpec((1, 1, wide // HD, rows), lambda s, *_: (s, part, 0, 0)),
+                pl.BlockSpec((rows, wide), lambda s, j, *_: (s, j)),
+                pl.BlockSpec((1, wide, rows), lambda s, j, *_: (s, j, 0)),
+                pl.BlockSpec((1, 1, wide // HD, rows), lambda s, j, *_: (s, j, 0, 0)),
             ],
             scratch_shapes=[
                 pltpu.VMEM((wide, rows), BF),
@@ -288,13 +287,12 @@
         out_shape=[
             jax.ShapeDtypeStruct((qkv.shape[0], width), BF),
             jax.ShapeDtypeStruct((seqs, width, rows), F32),
-            jax.ShapeDtypeStruct((seqs, width // wide, wide // HD, rows), F32),
+            jax.ShapeDtypeStruct((seqs, parts, wide // HD, rows), F32),
         ],
-        input_output_aliases={7 + i: i for i in range(len(earlier))},
-        compiler_params=params("arbitrary"),
-        cost_estimate=cost(12e9, 2e7),
+        compiler_params=params("arbitrary", "arbitrary"),
+        cost_estimate=cost(24e9, 2e7),
         name="attention_forward",
-    )(lo, hi, qkv, qkv, qkv, onehot, miss, *earlier)
+    )(lo, hi, qkv, qkv, qkv, onehot, miss)
 
 
 def attention_bwd(qkv, d_attn, ot, lse, lo, hi, onehot, miss, part):
@@ -357,56 +355,45 @@
     ref[row : row + 1, 0 : values.shape[1]] += jnp.sum(values, axis=0, keepdims=True)
 
 
-def fetch(place, core, held, other, spots, outs, sems):
-    for c in range(2):
-
-        @pl.when(core[0] == c)
-        def _(c=c):
-            for h in range(2):
-                src = held if h == c else other
-                for chip in range(place.shape[1]):
-                    for row, count, which, target in spots(h, chip):
-                        pltpu.make_async_copy(
-                            src.at[place[h, chip], pl.ds(row, count), :], outs[which].at[target], sems.at[which]
-                        ).start()
+def fetch(chunks, spots, outs, sems):
+    for h in range(2):
+        for chip in range(chunks.shape[1]):
+            for row, count, which, target in spots(h, chip):
+                pltpu.make_async_copy(
+                    chunks.at[h, chip, pl.ds(row, count), :], outs[which].at[target], sems.at[which]
+                ).start()
 
 
 def fetched(out, sem):
     pltpu.make_async_copy(out, out, sem).wait()
 
 
-def qkv_kernel(spots, place, core, tok, vec, bias, held, other, n1, qkv, w, sem):
-    if spots is not None:
-
-        @pl.when(pl.program_id(0) == 0)
-        def _():
-            fetch(place, core, held, other, spots, [w], sem)
+def qkv_kernel(spots, tok, vec, bias, chunks, n1, qkv, w, sem):
+    @pl.when(pl.program_id(0) == 0)
+    def _():
+        fetch(chunks, spots, [w], sem)
 
     xhat, _ = normalized(tok[...].astype(F32))
     n = (xhat * vec[0:1] + vec[1:2]).astype(BF)
     n1[...] = n
-    if spots is not None:
-
-        @pl.when(pl.program_id(0) == 0)
-        def _():
-            fetched(w, sem.at[0])
-
-    qkv[...] = (mm(n, w[...] if spots is not None else held[...]) + bias[...]).astype(BF)
-
-
-def project_qkv(tokens, vec, bias, held, other, place, core, spots):
+
+    @pl.when(pl.program_id(0) == 0)
+    def _():
+        fetched(w, sem.at[0])
+
+    qkv[...] = (mm(n, w[...]) + bias[...]).astype(BF)
+
+
+def project_qkv(tokens, vec, bias, chunks, spots):
     count, width = tokens.shape
     cols = 3 * width
-    tile = lambda w: pl.BlockSpec((TILE, w), lambda i, *_: (i, 0))
+    tile = lambda w: pl.BlockSpec((TILE, w), lambda i: (i, 0))
     return pl.pallas_call(
         functools.partial(qkv_kernel, spots),
-        grid_spec=pltpu.PrefetchScalarGridSpec(
-            num_scalar_prefetch=2,
-            grid=(count // TILE,),
-            in_specs=[tile(width), whole(vec.shape), whole(bias.shape), ANYWHERE, ANYWHERE],
-            out_specs=[tile(width), tile(cols), whole((width, cols))],
-            scratch_shapes=[pltpu.SemaphoreType.DMA((1,))],
-        ),
+        grid=(count // TILE,),
+        in_specs=[tile(width), whole(vec.shape), whole(bias.shape), ANYWHERE],
+        out_specs=[tile(width), tile(cols), whole((width, cols))],
+        scratch_shapes=[pltpu.SemaphoreType.DMA((1,))],
         out_shape=[
             jax.ShapeDtypeStruct((count, width), BF),
             jax.ShapeDtypeStruct((count, cols), BF),
@@ -415,99 +402,51 @@
         compiler_params=params("arbitrary"),
         cost_estimate=cost(2 * count * width * cols, 2e7),
         name="norm_and_qkv",
-    )(place, core, tokens, vec, bias, held, other)
-
-
-STRIP = 256
+    )(tokens, vec, bias, chunks)
+
+
+STRIP = 768
 CURVE = 0.7978845608028654
 CUBIC = 0.044715
 
 
-def up_kernel(spots, place, core, attn, tok, vec, b1, held, other, mid, n2, pre, act, wo, w1, sem):
-    @pl.when(pl.program_id(0) == 0)
-    def _():
-        fetch(place, core, held, other, spots, [wo, w1], sem)
-        fetched(wo, sem.at[0])
-
-    x = tok[...].astype(F32) + mm(attn[...], wo[...]) + vec[2:3]
-    mid[...] = x
-    xhat, _ = normalized(x)
-    n = (xhat * vec[0:1] + vec[1:2]).astype(BF)
-    n2[...] = n
-
-    @pl.when(pl.program_id(0) == 0)
-    def _():
-        fetched(w1, sem.at[1])
-
-    width = STRIP
-    for j in range(w1.shape[1] // width):
-        cols = slice(j * width, (j + 1) * width)
-        u = mm(n, w1[:, cols]) + b1[:, cols]
-        pre[:, cols] = u
-        th = jnp.tanh(u * (CURVE + (CURVE * CUBIC) * (u * u)))
-        act[:, cols] = (u * (0.5 + 0.5 * th)).astype(BF)
-
-
-def up_part(attn, tokens, vec, b1, held, other, place, core, spots):
-    count, width = tokens.shape
-    hidden = b1.shape[1]
-    rows = TILE // 2
-    tile = lambda w: pl.BlockSpec((rows, w), lambda i, *_: (i, 0))
-    return pl.pallas_call(
-        functools.partial(up_kernel, spots),
-        grid_spec=pltpu.PrefetchScalarGridSpec(
-            num_scalar_prefetch=2,
-            grid=(count // rows,),
-            in_specs=[tile(width), tile(width), whole(vec.shape), whole(b1.shape), ANYWHERE, ANYWHERE],
-            out_specs=[
-                tile(width), tile(width), tile(hidden), tile(hidden), whole((width, width)), whole((width, hidden)),
-            ],
-            scratch_shapes=[pltpu.SemaphoreType.DMA((2,))],
-        ),
-        out_shape=[
-            jax.ShapeDtypeStruct((count, width), F32),
-            jax.ShapeDtypeStruct((count, width), BF),
-            jax.ShapeDtypeStruct((count, hidden), F32),
-            jax.ShapeDtypeStruct((count, hidden), BF),
-            jax.ShapeDtypeStruct((width, width), BF),
-            jax.ShapeDtypeStruct((width, hidden), BF),
-        ],
-        compiler_params=params("arbitrary"),
-        cost_estimate=cost(2 * count * width * (width + hidden), 6e7),
-        name="out_and_up",
-    )(place, core, attn, tokens, vec, b1, held, other)
-
-
-def down_kernel(
-    spots, place, core, act, mid, pre, cot, vec, w1, wo, held, other,
-    out, d_pre, d_mid, d_branch, d_attn, sums, sum_up, w2, sem,
+def middle_kernel(
+    spots, attn, tok, cot, vec, b1, chunks2, chunks3,
+    out, n2, act, d_pre, d_mid, d_branch, d_attn, sums, sum_up, wo, w1, w2, sem,
 ):
     @pl.when(pl.program_id(0) == 0)
     def _():
-        fetch(place, core, held, other, spots, [w2], sem)
-        fetched(w2, sem.at[0])
-
-    clear_first(sums, sum_up)
-    x = mid[...]
-    width = x.shape[1]
+        fetch(chunks2, spots[0], [wo, w1], sem)
+        fetch(chunks3, spots[1], [w2], sem.at[pl.ds(2, 1)])
+        for ref in (sums, sum_up):
+            ref[...] = jnp.zeros_like(ref)
+        for k, ref in enumerate((wo, w1, w2)):
+            fetched(ref, sem.at[k])
+
+    x = tok[...].astype(F32) + mm(attn[...], wo[...]) + vec[2:3]
+    xhat, scale = normalized(x)
+    n = (xhat * vec[0:1] + vec[1:2]).astype(BF)
+    n2[...] = n
     d_out = cot[...]
+    y = x + vec[3:4]
     d_n2 = None
-    y = x + vec[3:4]
-    for j in range(act.shape[1] // width):
-        cols = slice(j * width, (j + 1) * width)
+    for j in range(w1.shape[1] // STRIP):
+        cols = slice(j * STRIP, (j + 1) * STRIP)
+        u = mm(n, w1[:, cols]) + b1[:, cols]
         d_act = mm_nt(d_out, w2[cols, :])
-        y = y + mm(act[:, cols], w2[cols, :])
-        u = pre[:, cols]
         square = u * u
         th = jnp.tanh(u * (CURVE + (CURVE * CUBIC) * square))
-        slope = (0.5 + 0.5 * th) + (0.5 * u) * (1.0 - th * th) * (CURVE + (3.0 * CURVE * CUBIC) * square)
+        half = 0.5 * u
+        hidden = (half + half * th).astype(BF)
+        act[:, cols] = hidden
+        y = y + mm(hidden, w2[cols, :])
+        slope = (0.5 + 0.5 * th) + half * (1.0 - th * th) * (CURVE + (3.0 * CURVE * CUBIC) * square)
         low = (d_act * slope).astype(BF)
         d_pre[:, cols] = low
         sum_up[:, cols] += jnp.sum(low.astype(F32), axis=0, keepdims=True)
         part = mm_nt(low, w1[:, cols])
         d_n2 = part if d_n2 is None else d_n2 + part
     out[...] = y.astype(BF)
-    xhat, scale = normalized(x)
     add_row(sums, 0, d_n2 * xhat)
     add_row(sums, 1, d_n2)
     g = d_out.astype(F32)
@@ -520,38 +459,34 @@
     d_attn[...] = mm_nt(low, wo[...]).astype(BF)
 
 
-def down_part(act, mid, pre, cotangent, vec, w1, wo, held, other, place, core, spots):
-    count, width = mid.shape
-    hidden = act.shape[1]
+def middle_part(attn, tokens, cotangent, vec, b1, gathered, spots):
+    count, width = tokens.shape
+    hidden = b1.shape[1]
     rows = TILE // 2
-    tile = lambda w: pl.BlockSpec((rows, w), lambda i, *_: (i, 0))
+    tile = lambda w: pl.BlockSpec((rows, w), lambda i: (i, 0))
+    row = lambda w, kind: jax.ShapeDtypeStruct((count, w), kind)
     return pl.pallas_call(
-        functools.partial(down_kernel, spots),
-        grid_spec=pltpu.PrefetchScalarGridSpec(
-            num_scalar_prefetch=2,
-            grid=(count // rows,),
-            in_specs=[
-                tile(hidden), tile(width), tile(hidden), tile(width), whole(vec.shape), whole(w1.shape),
-                whole(wo.shape), ANYWHERE, ANYWHERE,
-            ],
-            out_specs=[
-                tile(width), tile(hidden), tile(width), tile(width), tile(width), whole((8, width)), whole((1, hidden)),
-            ],
-            scratch_shapes=[pltpu.VMEM((hidden, width), BF), pltpu.SemaphoreType.DMA((1,))],
-        ),
+        functools.partial(middle_kernel, spots),
+        grid=(count // rows,),
+        in_specs=[tile(width), tile(width), tile(width), whole(vec.shape), whole(b1.shape)] + [ANYWHERE] * 2,
+        out_specs=[
+            tile(width), tile(width), tile(hidden), tile(hidden), tile(width), tile(width), tile(width),
+            whole((8, width)), whole((1, hidden)),
+        ],
+        scratch_shapes=[
+            pltpu.VMEM((width, width), BF),
+            pltpu.VMEM((width, hidden), BF),
+            pltpu.VMEM((hidden, width), BF),
+            pltpu.SemaphoreType.DMA((3,)),
+        ],
         out_shape=[
-            jax.ShapeDtypeStruct((count, width), BF),
-            jax.ShapeDtypeStruct((count, hidden), BF),
-            jax.ShapeDtypeStruct((count, width), F32),
-            jax.ShapeDtypeStruct((count, width), BF),
-            jax.ShapeDtypeStruct((count, width), BF),
-            jax.ShapeDtypeStruct((8, width), F32),
-            jax.ShapeDtypeStruct((1, hidden), F32),
+            row(width, BF), row(width, BF), row(hidden, BF), row(hidden, BF), row(width, F32), row(width, BF),
+            row(width, BF), jax.ShapeDtypeStruct((8, width), F32), jax.ShapeDtypeStruct((1, hidden), F32),
         ],
         compiler_params=params("arbitrary"),
-        cost_estimate=cost(2 * count * width * (width + 3 * hidden), 8e7),
-        name="down_and_back",
-    )(place, core, act, mid, pre, cotangent, vec, w1, wo, held, other)
+        cost_estimate=cost(4 * count * width * (width + 2 * hidden), 6e7),
+        name="middle",
+    )(attn, tokens, cotangent, vec, b1, *gathered)
 
 
 def first_norm_kernel(parts, far, near, w_far, w_near, tok, d_mid, vec, out, sums):
@@ -593,74 +528,76 @@
     return lax.dot_general(a, b, (((0,), (0,)), ((), ())), preferred_element_type=F32)
 
 
-def spread_chunks(send_at, keep_at, acc, got, send, keep):
-    def body(j, carry):
-        for at, out in ((send_at, send), (keep_at, keep)):
-            i = at[j]
-            out[j] = (acc[i].astype(F32) + got[i].astype(F32)).astype(BF)
-        return carry
-
-    lax.fori_loop(0, send.shape[0], body, 0)
-
-
-def grad_down_kernel(near, part, send_at, keep_at, cot, act, *refs):
-    got, outs, (turned, acc) = (refs[0], refs[1:3], refs[3:]) if near else (None, refs[:1], (refs[1], refs[0]))
+def grad_kernel(layout, near, part, send_at, keep_at, *refs):
+    count = len(layout)
+    ins, refs = refs[: 2 * count], refs[2 * count :]
+    if near:
+        got, (send, keep), (sums, total, held, sem) = refs[0], refs[1:3], (refs[3 : 3 + count], *refs[3 + count :])
+    else:
+        out, sums = refs[0], refs[1 : 1 + count]
     step = pl.program_id(0)
+    arrival = pltpu.make_async_copy(got, held, sem.at[0]) if near else None
 
     @pl.when(step == 0)
     def _():
-        turned[...] = cot[...].T
-
-    sums = mm(turned[...], act[...])
-    chips, blocks, rows, _ = acc.shape
-    some = chips // pl.num_programs(0)
-    sums = (sums if near else sums.astype(BF)).T.reshape(act.shape[1] // (blocks * rows), blocks, rows, WIDE)
-    acc[pl.ds(step * sums.shape[0], sums.shape[0])] = sums.astype(acc.dtype)
-    if near:
-
-        @pl.when(step == pl.num_programs(0) - 1)
-        def _():
-            spread_chunks(send_at, keep_at, acc, got, *outs)
-
-
-def grad_cols_kernel(widths, near, part, send_at, keep_at, *refs):
-    count = len(widths)
-    ins, refs = refs[: 2 * count], refs[2 * count :]
-    got, outs, acc = (refs[0], refs[1:3], refs[3]) if near else (None, refs[:1], refs[0])
-    step = pl.program_id(0)
-    chips, _, rows, _ = acc.shape
-    at = base = 0
-    for k, (blocks, steps) in enumerate(widths):
-        for i in range(steps):
-
-            @pl.when(step == at + i)
-            def _(k=k, blocks=blocks, first=base + i * blocks):
-                sums = tn(ins[2 * k][...], ins[2 * k + 1][...]).astype(acc.dtype)
-                for b in range(blocks):
-                    acc[:, first + b] = sums[:, b * WIDE : (b + 1) * WIDE].reshape(chips, rows, WIDE)
-
-        at += steps
-        base += steps * blocks
-    if near:
-
-        @pl.when(step == pl.num_programs(0) - 1)
-        def _():
-            spread_chunks(send_at, keep_at, acc, got, *outs)
-
-
-def grad_call(kernel, steps, specs, arrays, shape, part, got, order, scratch, flops, name):
+        if near:
+            arrival.start()
+        for acc in sums:
+            acc[...] = jnp.zeros_like(acc)
+
+    for k in range(count):
+        sums[k][...] += tn(ins[2 * k][...], ins[2 * k + 1][...])
+
+    @pl.when(step == pl.num_programs(0) - 1)
+    def _():
+        target = total if near else out
+        chips, _, rows, _ = target.shape
+        kind = target.dtype
+        base = 0
+        for k, blocks in enumerate(layout):
+            if blocks == 0:
+                target[...] = sums[k][...].astype(kind).T.reshape(target.shape)
+            for b in range(blocks):
+                cols = slice(b * WIDE, (b + 1) * WIDE)
+                target[:, base + b] = sums[k][:, cols].astype(kind).reshape(chips, rows, WIDE)
+            base += blocks
+        if near:
+            arrival.wait()
+
+            def body(j, carry):
+                for at, ref in ((send_at, send), (keep_at, keep)):
+                    i = at[j]
+                    ref[j] = (total[i] + held[i].astype(F32)).astype(BF)
+                return carry
+
+            lax.fori_loop(0, chips // 2, body, 0)
+
+
+def grad_part(pairs, part, chips, name, got=None, order=None):
+    tokens = pairs[0][0].shape[0]
     near = got is not None
-    chips = shape[0]
-    out = jax.ShapeDtypeStruct(((chips // 2,) if near else (chips,)) + shape[1:], BF)
+    specs, arrays, scratch, layout, flops = [], [], [], [], 0
+    for lhs, tall, lhs_part, rhs, wide, rhs_part in pairs:
+        for x, cols, by_part in ((lhs, tall, lhs_part), (rhs, wide, rhs_part)):
+            specs.append(pl.BlockSpec((TILE, cols), lambda i, p, *_, by_part=by_part: (i, p[0] if by_part else 0)))
+            arrays.append(x)
+        scratch.append(pltpu.VMEM((tall, wide), F32))
+        layout.append(0 if tall == WIDE else wide // WIDE)
+        flops += 2 * tokens * tall * wide
+    if layout[0] == 0:
+        shape = (chips, 4, pairs[0][4] // chips // 4, WIDE)
+    else:
+        shape = (chips, sum(layout), pairs[0][1] // chips, WIDE)
+    out = jax.ShapeDtypeStruct((chips // 2 if near else chips,) + shape[1:], BF)
     spec = whole(out.shape)
     if near:
-        specs, arrays = specs + [whole(got.shape)], arrays + [got]
-        scratch = scratch + [pltpu.VMEM(shape, F32)]
+        specs, arrays = specs + [ANYWHERE], arrays + [got]
+        scratch += [pltpu.VMEM(shape, F32), pltpu.VMEM(shape, BF), pltpu.SemaphoreType.DMA((1,))]
     return pl.pallas_call(
-        kernel,
+        functools.partial(grad_kernel, tuple(layout), near),
         grid_spec=pltpu.PrefetchScalarGridSpec(
             num_scalar_prefetch=3,
-            grid=(steps,),
+            grid=(tokens // TILE,),
             in_specs=specs,
             out_specs=[spec, spec] if near else spec,
             scratch_shapes=scratch,
@@ -672,40 +609,6 @@
     )(part, *(order or (part, part)), *arrays)
 
 
-def grad_down(cot, act, part, chips, name, got=None, order=None):
-    tokens, width = cot.shape
-    hidden = act.shape[1]
-    shape = (chips, 4, hidden // chips // 4, WIDE)
-    specs = [
-        pl.BlockSpec((tokens, WIDE), lambda i, p, *_: (0, p[0])),
-        pl.BlockSpec((tokens, width), lambda i, *_: (0, i)),
-    ]
-    return grad_call(
-        functools.partial(grad_down_kernel, got is not None), hidden // width, specs, [cot, act], shape, part, got,
-        order, [pltpu.VMEM((WIDE, tokens), BF)], 2 * tokens * WIDE * hidden, name,
-    )
-
-
-def grad_cols(pairs, part, chips, name, got=None, order=None):
-    tokens, width = pairs[0][0].shape
-    specs, arrays, widths, at, flops = [], [], [], 0, 0
-    for lhs, rhs, blocks, steps, by_part in pairs:
-        def column(i, p, *_, at=at, steps=steps, by_part=by_part):
-            j = jnp.clip(i - at, 0, steps - 1)
-            return (0, p[0] * steps + j if by_part else j)
-
-        specs += [pl.BlockSpec((tokens, width), lambda i, *_: (0, 0)), pl.BlockSpec((tokens, blocks * WIDE), column)]
-        arrays += [lhs, rhs]
-        widths.append((blocks, steps))
-        at += steps
-        flops += 2 * tokens * width * WIDE * blocks * steps
-    shape = (chips, sum(b * s for b, s in widths), width // chips, WIDE)
-    return grad_call(
-        functools.partial(grad_cols_kernel, tuple(widths), got is not None), at, specs, arrays, shape, part, got,
-        order, [], flops, name,
-    )
-
-
 def here():
     me = lax.axis_index("fsdp")
     return me // 8, (me // 4) % 2, (me // 2) % 2, me % 2
@@ -738,32 +641,128 @@
     return jnp.where(pick_second, b, a)
 
 
-def pair_kernel(blocks, core, own, got, chunk):
-    for c in range(2):
-
-        @pl.when(core[0] == c)
-        def _(c=c):
-            parts = (own, got) if c == 0 else (got, own)
-            at = 0
-            for size in blocks:
-                for k in range(2):
-                    chunk[0, 2 * at + k * size : 2 * at + (k + 1) * size, :] = parts[k][at : at + size, :]
-                at += size
-
-
-def pair_rows(own, got, blocks, core):
-    shape = jax.ShapeDtypeStruct((1, 2 * own.shape[0], own.shape[1]), BF)
+def neighbours():
+    me = lax.axis_index("fsdp")
+    core = lax.rem(me, 2)
+    x = lax.rem(me // 2, 2)
+    y = lax.rem(me // 4, 2)
+    along_y = 4 * (1 - 2 * y)
+    along_x = 2 * (1 - 2 * x)
+    first = (1 - core) * along_y + core * along_x
+    second = along_y + along_x - first
+    return me, core, me // 8, first, second
+
+
+def greet(others):
+    barrier = pltpu.get_barrier_semaphore()
+    for other in others:
+        pl.semaphore_signal(barrier, inc=1, device_id=(other,), device_id_type=pl.DeviceIdType.MESH)
+    pl.semaphore_wait(barrier, len(others))
+
+
+def gather_kernel(blocks, depth, *refs):
+    flows = len(blocks)
+    owns, oths, outs = refs[:flows], refs[flows : 2 * flows], refs[2 * flows : 3 * flows]
+    sems = refs[3 * flows :]
+    me, core, z, first, second = neighbours()
+    twin = me + 1 - 2 * core
+    chip = me // 2
+    deep = [chip * 2 + core] + [lax.rem(z + k, depth) * 8 + lax.rem(me, 8) for k in range(1, depth)]
+    greet([twin, me + first, me + second] + deep[1:])
+    mine = [lax.rem(z + depth - k, depth) * 4 + lax.rem(chip, 4) for k in range(depth)]
+    theirs = [at + first // 2 for at in mine]
+    last = [at + second // 2 for at in mine + theirs]
+
+    def send(f, at, send_sem, recv_sem, device):
+        pltpu.make_async_remote_copy(
+            src_ref=outs[f].at[core, at],
+            dst_ref=outs[f].at[core, at],
+            send_sem=send_sem,
+            recv_sem=recv_sem,
+            device_id=(device,),
+            device_id_type=pl.DeviceIdType.MESH,
+        ).start()
+
+    def arrived(ref, sem):
+        pltpu.make_async_copy(ref, ref, sem).wait()
+
+    def onward(f, k, at, steps):
+        far, near, cross, seen, local, out, twin_out, twin_in, pair_out, pair_in = sems[10 * f : 10 * f + 10]
+        if steps == 2:
+            send(f, at, out.at[0], near.at[k], me + first)
+        if steps >= 1:
+            send(f, at, out.at[0], cross.at[k if steps == 2 else depth + k], me + second)
+        send(f, at, twin_out.at[0], twin_in.at[0], twin)
+
+    for f in range(flows):
+        pair_out, pair_in, local = sems[10 * f + 8], sems[10 * f + 9], sems[10 * f + 4]
+        row = 0
+        for size in blocks[f]:
+            here_rows = pl.ds(pl.multiple_of(2 * row + core * size, 8), size)
+            pltpu.make_async_copy(
+                owns[f].at[pl.ds(row, size), :], outs[f].at[core, chip, here_rows, :], local.at[0]
+            ).start()
+            pltpu.make_async_remote_copy(
+                src_ref=oths[f].at[pl.ds(row, size), :],
+                dst_ref=outs[f].at[1 - core, chip, here_rows, :],
+                send_sem=pair_out.at[0],
+                recv_sem=pair_in.at[0],
+                device_id=(twin,),
+                device_id_type=pl.DeviceIdType.MESH,
+            ).start()
+            row += size
+    for f in range(flows):
+        far, out = sems[10 * f], sems[10 * f + 5]
+        arrived(owns[f], sems[10 * f + 4].at[0])
+        arrived(owns[f], sems[10 * f + 9].at[0])
+        for k in range(1, depth):
+            send(f, chip, out.at[0], far.at[k], deep[k])
+        onward(f, 0, chip, 2)
+
+    def from_far(f):
+        for k in range(1, depth):
+            arrived(outs[f].at[core, mine[k]], sems[10 * f].at[k])
+            onward(f, k, mine[k], 2)
+
+    def from_near(f):
+        for k in range(depth):
+            arrived(outs[f].at[core, theirs[k]], sems[10 * f + 1].at[k])
+            onward(f, k, theirs[k], 1)
+
+    def from_cross(f):
+        for k in range(2 * depth):
+            arrived(outs[f].at[core, last[k]], sems[10 * f + 2].at[k])
+            onward(f, k, last[k], 0)
+
+    for step in range(flows + 2):
+        for stage, run in enumerate((from_far, from_near, from_cross)):
+            if 0 <= step - stage < flows:
+                run(step - stage)
+    for f in range(flows):
+        chips = outs[f].shape[1]
+        arrived(outs[f].at[1 - core], sems[10 * f + 7].at[0])
+        arrived(outs[f].at[0], sems[10 * f + 6].at[0])
+        arrived(outs[f].at[0, pl.ds(0, chips - 1)], sems[10 * f + 5].at[0])
+        arrived(oths[f], sems[10 * f + 8].at[0])
+
+
+def gather_shards(owns, oths, blocks, depth):
+    chips = 4 * depth
+    outs = [jax.ShapeDtypeStruct((2, chips, 2 * o.shape[0], WIDE), BF) for o in owns]
+    dma = lambda n: pltpu.SemaphoreType.DMA((n,))
+    scratch = []
+    for _ in owns:
+        scratch += [dma(depth), dma(depth), dma(2 * depth)] + [dma(1)] * 7
     return pl.pallas_call(
-        functools.partial(pair_kernel, blocks),
-        grid_spec=pltpu.PrefetchScalarGridSpec(
-            num_scalar_prefetch=1,
-            grid=(1,),
-            in_specs=[whole(own.shape), whole(own.shape)],
-            out_specs=whole(shape.shape),
-        ),
-        out_shape=shape,
-        name="pair_rows",
-    )(core, own, got)
+        functools.partial(gather_kernel, blocks, depth),
+        in_specs=[ANYWHERE] * (2 * len(owns)),
+        out_specs=[ANYWHERE] * len(owns),
+        out_shape=outs,
+        scratch_shapes=scratch,
+        compiler_params=pltpu.CompilerParams(collective_id=0, has_side_effects=True),
+        cost_estimate=cost(0, 3e7),
+        name="gather_shards",
+    )(*owns, *oths)
 
 
 def pack_kernel(core, *refs):
@@ -805,16 +804,6 @@
 
 def gate(x, *after):
     return lax.optimization_barrier((x,) + after)[0]
-
-
-def chunk_places(moves):
-    z, y, x, c = here()
-    chip = jnp.arange(moves.chips, dtype=jnp.int32)
-    deep = (z - chip // 4) % moves.depth
-    far_y, far_x = (chip // 2) % 2 ^ y, chip % 2 ^ x
-    half0 = (far_x * 2 + far_y) * moves.depth + deep
-    half1 = (far_y * 2 + far_x) * moves.depth + deep
-    return jnp.stack([half0, half1]).astype(jnp.int32), c.astype(jnp.int32).reshape(1)
 
 
 def fold_kernel(send_at, keep_at, a_send, b_send, a_keep, b_keep, send, keep):
@@ -938,8 +927,7 @@
     n1 = norm(rows, g1, c1).astype(BF)
     bias = weight_halves(jnp.concatenate([bq, jnp.zeros_like(bq), bv])[None])
     qkv = (mm(n1, wqkv) + bias).astype(BF)
-    kept = attention_fwd(qkv, *tables, 0)
-    attn, attn_t, lse = attention_fwd(qkv, *tables, 1, tuple(kept))
+    attn, attn_t, lse = attention_fwd(qkv, *tables)
     middle = rows + mm(attn, wo) + bo
     n2 = norm(middle, g2, c2).astype(BF)
     act_value, gelu_pull = jax.vjp(functools.partial(jax.nn.gelu, approximate=True), mm(n2, w1) + b1)
@@ -980,30 +968,16 @@
     part = width // devices
     two = 2 * part
     hidden = w_up.shape[1]
-    places, core = chunk_places(moves)
+    core = here()[3].astype(jnp.int32).reshape(1)
 
     small = jnp.concatenate([ln1_gain, ln1_shift, bias_q, bias_v, bias_out, ln2_gain, ln2_shift, bias_down, bias_up])
     small = jnp.pad(small[None], ((0, 7), (0, WIDE - small.shape[0])))
     own1, own2, own3, oth1, oth2, oth3 = pack(w_qkv, small, w_out, w_up, w_down, core)
 
-    def deep(chunk):
-        return jnp.concatenate([chunk] + [swap(chunk, moves.deep[k]) for k in range(1, moves.depth)], axis=0)
-
-    def along(held, move):
-        return jnp.concatenate([held, swap(held, move)], axis=0)
-
-    got1, got2, got3 = swap(oth1, moves.core), swap(oth2, moves.core), swap(oth3, moves.core)
-    chunk1 = pair_rows(own1, got1, [part] * 3 + [8], core)
-    chunk2 = pair_rows(own2, got2, [part] * 5, core)
-    chunk3 = pair_rows(own3, got3, [4 * part], core)
-    held1 = deep(chunk1)
-    held1 = along(held1, moves.first)
-    deep2 = [swap(gate(chunk2, held1), moves.deep[k]) for k in range(1, moves.depth)]
-    held1 = along(held1, moves.second)
-    other1 = swap(held1, moves.core)
-
-    vecs = jnp.take(held1[:, 6 * part :: 8], of_two(core[0] == 1, places[0], places[1]), axis=0)
-    vecs = vecs.reshape(devices, WIDE).astype(F32)
+    chunks1, chunks2, chunks3 = gather_shards(
+        (own1, own2, own3), (oth1, oth2, oth3), ([part] * 3 + [8], [part] * 5, [4 * part]), moves.depth
+    )
+    vecs = chunks1[0, :, 6 * part :: 8].reshape(devices, WIDE).astype(F32)
     g1, c1, bq, bv, bo, g2, c2, b2 = [vecs[:, i * part : (i + 1) * part].reshape(-1) for i in range(8)]
     b1 = vecs[:, 8 * part : 12 * part].reshape(1, -1)
     bias = weight_halves(jnp.concatenate([bq, jnp.zeros_like(bq), bv])[None])
@@ -1022,43 +996,26 @@
     def spots_down(h, chip):
         return [(0, 4 * two, 0, (pl.ds(4 * two * chip, 4 * two), pl.ds(h * WIDE, WIDE)))]
 
-    n1, qkv, wqkv = project_qkv(tokens, jnp.stack([g1, c1]), bias, held1, other1, places, core, spots_qkv)
-    deep2 = lax.optimization_barrier(tuple(deep2) + (qkv,))[:-1]
-    held2 = along(jnp.concatenate([chunk2, *deep2], axis=0), moves.first)
-    deep3 = [swap(gate(chunk3, held2), moves.deep[k]) for k in range(1, moves.depth)]
-    kept = attention_fwd(gate(qkv, held2), *tables, 0)
-    more2 = swap(held2, moves.second)
-    *deep3, more2 = lax.optimization_barrier(tuple(deep3) + (more2, kept[0]))[:-1]
-    held2 = jnp.concatenate([held2, more2], axis=0)
-    held3 = jnp.concatenate([chunk3, *deep3], axis=0)
-    kept = lax.optimization_barrier(tuple(kept) + (held2, held3))[:3]
-    other2 = swap(held2, moves.core)
-    more3 = swap(held3, moves.first)
-    attn, attn_t, lse = attention_fwd(qkv, *tables, 1, tuple(kept))
-    held3 = jnp.concatenate([held3, gate(more3, attn)], axis=0)
-    more3 = swap(held3, moves.second)
-    mid, n2, pre, act, wo, w1 = up_part(
-        gate(attn, held3), tokens, jnp.stack([g2, c2, bo]), b1, held2, gate(other2, attn), places, core, spots_up
-    )
-    held3 = jnp.concatenate([held3, gate(more3, act)], axis=0)
-    other3 = swap(held3, moves.core)
+    n1, qkv, wqkv = project_qkv(tokens, jnp.stack([g1, c1]), bias, chunks1, spots_qkv)
+    attn, attn_t, lse = attention_fwd(qkv, *tables)
+    layer_out, n2, act, d_pre, d_mid, d_branch, d_attn, sums2, sum_up = middle_part(
+        attn, tokens, cotangent, jnp.stack([g2, c2, bo, b2]), b1, (chunks2, chunks3), (spots_up, spots_down)
+    )
 
     far, near = 1 - core, core
     orders = fold_places(moves)
-    sent_down = grad_down(gate(cotangent, held3), act, far, chips, "grad_down_far")
+    downs = lambda cot: [(cot, WIDE, True, act, hidden, False)]
+    ups = lambda n2: [(n2, width, False, d_pre, hidden // 2, True), (attn, width, False, d_branch, WIDE, True)]
+    qkvs = lambda n1, d: [(n1, width, False, d, 3 * WIDE, False)]
+    sent_down = grad_part(downs(cotangent), far, chips, "grad_down_far")
     got_down = swap(sent_down, moves.core)
-    layer_out, d_pre, d_mid, d_branch, d_attn, sums2, sum_up = down_part(
-        gate(act, sent_down), mid, pre, cotangent, jnp.stack([g2, g2, g2, b2]), w1, wo, held3, gate(other3, sent_down),
-        places, core, spots_down,
-    )
-    ups = lambda n2: [(n2, d_pre, 2, 2, True), (attn, d_branch, 1, 1, True)]
-    sent_up = grad_cols(ups(n2), far, chips, "grad_up_out_far")
+    sent_up = grad_part(ups(gate(n2, sent_down)), far, chips, "grad_up_out_far")
     got_up = swap(sent_up, moves.core)
-    send_down, keep_down = grad_down(
-        gate(cotangent, sent_up), act, near, chips, "grad_down_near", gate(got_down, d_pre), orders[0]
+    send_down, keep_down = grad_part(
+        downs(gate(cotangent, sent_up)), near, chips, "grad_down_near", gate(got_down, sent_up), orders[0]
     )
     got_down = swap(send_down, moves.second)
-    send_up, keep_up = grad_cols(
+    send_up, keep_up = grad_part(
         ups(gate(n2, send_down)), near, chips, "grad_up_out_near", gate(got_up, send_down), orders[0]
     )
     got_up = swap(send_up, moves.second)
@@ -1067,9 +1024,7 @@
     got_down = swap(send_down, moves.first)
     send_up, keep_up = fold(keep_up, gate(got_up, d_qkv_far), *orders[1])
     got_up = swap(send_up, moves.first)
-    sent_qkv = grad_cols(
-        [(gate(n1, send_up, send_down), d_qkv_far, 3, 1, False)], far, chips, "grad_qkv_far"
-    )
+    sent_qkv = grad_part(qkvs(gate(n1, send_up, send_down), d_qkv_far), far, chips, "grad_qkv_far")
     got_qkv = swap(sent_qkv, moves.core)
     d_qkv_near = attention_bwd(qkv, gate(d_attn, sent_qkv), attn_t, lse, *tables, near)
 
@@ -1082,15 +1037,16 @@
     first_down, *rest_down = level(keep_down, gate(got_down, d_qkv_near))
     first_up, *rest_up = level(keep_up, gate(got_up, d_qkv_near))
     gots_down, gots_up = spread(rest_down), spread(rest_up)
-    send_qkv, keep_qkv = grad_cols(
-        [(gate(n1, first_down, first_up), d_qkv_near, 3, 1, False)], near, chips, "grad_qkv_near",
-        gate(got_qkv, d_qkv_near), orders[0],
+    input_grad, sums1 = first_norm_back(
+        d_qkv_far, gate(d_qkv_near, first_down, first_up), wqkv, tokens, d_mid, g1[None], jnp.concatenate([far, near])
+    )
+    send_qkv, keep_qkv = grad_part(
+        qkvs(gate(n1, sums1), d_qkv_near), near, chips, "grad_qkv_near", gate(got_qkv, sums1), orders[0]
     )
     got_qkv = swap(send_qkv, moves.second)
-    input_grad, sums1 = first_norm_back(
-        d_qkv_far, gate(d_qkv_near, send_qkv), wqkv, tokens, d_mid, g1[None], jnp.concatenate([far, near])
-    )
-    send_qkv, keep_qkv = fold(keep_qkv, gate(got_qkv, sums1), *orders[1])
+    first_down, *gots_down = lax.optimization_barrier((first_down, *gots_down, send_qkv))[:-1]
+    first_up, *gots_up = lax.optimization_barrier((first_up, *gots_up, send_qkv))[:-1]
+    send_qkv, keep_qkv = fold(keep_qkv, got_qkv, *orders[1])
     got_qkv = swap(send_qkv, moves.first)
 
     odd = core[0] == 1

time: 507 us -> 474 us (0.935)
  Pallas kernels: 311 us -> 369 us
  waiting for transfers between devices: 75.5 us -> 34.3 us
  starting transfers between devices: 60.4 us -> 31.8 us
  local copies, waits for them, and re-layouts: 40.1 us -> 20.3 us
    pallas_call x14 -> x10, Pallas kernels: 212 us -> 269 us  [the longest x1 78.2 us: gather_shards(): pl.pallas_call(functools.partial(gather_kernel, blocks, depth), in_specs=...]
    ppermute x48 -> x27, waiting for transfers between devices: 75.5 us -> 34.3 us  [swap(): return lax.ppermute(x, 'fsdp', moves)]
    ppermute x48 -> x27, starting transfers between devices: 60.4 us -> 31.8 us  [swap(): return lax.ppermute(x, 'fsdp', moves)]
    unnamed x62 -> x44, local copies, waits for them, and re-layouts: 20.9 us -> 5.56 us
  transfers between devices with their start and end apart: 48 -> 27, of which waited for: 16 -> 12; matrix products, arithmetic and copies ran while one was open for 6% -> 2% of each run, Pallas kernels for 42% -> 28%
where the time goes in v2:
time: 474 us; the launch traced here: 466 us
  Pallas kernels  369 us (78%)
  waiting for transfers between devices  34.3 us (7%)
  starting transfers between devices  31.8 us (7%)
  local copies, waits for them, and re-layouts  20.3 us (4%)
  other arithmetic  8.45 us (2%)
    pallas_call x1, Pallas kernels, gather_shards(): pl.pallas_call(functools.partial(gather_kernel, blocks, depth), in_specs=...  78.2 us
    pallas_call x6, Pallas kernels, grad_part(): pl.pallas_call(functools.partial(grad_kernel, tuple(layout), near), grid_...  77.3 us
    pallas_call x1, Pallas kernels, middle_part(): pl.pallas_call(functools.partial(middle_kernel, spots), grid=(count // ro...  66.4 us
    pallas_call x2, Pallas kernels, attention_bwd(): pl.pallas_call(attn_bwd_kernel, grid_spec=pltpu.PrefetchScalarGridSpec(nu...  60.2 us
    ppermute x27, waiting for transfers between devices, swap(): return lax.ppermute(x, 'fsdp', moves)  34.3 us
    pallas_call x1, Pallas kernels, attention_fwd(): pl.pallas_call(attn_fwd_kernel, grid_spec=pltpu.PrefetchScalarGridSpec(nu...  32.6 us
    ppermute x27, starting transfers between devices, swap(): return lax.ppermute(x, 'fsdp', moves)  31.8 us
    pallas_call x1, Pallas kernels, first_norm_back(): pl.pallas_call(first_norm_kernel, grid_spec=pltpu.PrefetchScalarGridSpec(...  18.4 us
  transfers between devices with their start and end apart: 27, of which 12 were waited for; matrix products, arithmetic and copies ran while one was open for 2% of the time, Pallas kernels for 28%

profile of v2, /device:TPU:0, one launch (start us, length us, event | category | flops | bytes accessed | tf_op | source)
XLA Modules:
  0.0 466.0 jit_solution(7368870403047866310)
XLA Ops:
  3.7 2.0 pack_shards.1
  5.7 78.2 %gather_shards.1 = (bf16[2,16,160,384]{3,2,1,0:T(8,128)(2,1)}, bf16[2,16,240,384]{3,2,1,0:T(8,128)(2,1)}, bf16[2,16,192,384]{3,2,1,0:T(8,128)(2,1)}) custom-call(bf16[80,384]{1,0:T(8,128)(2,1)} %get-tuple-element.90.refs_0_, bf16[120,384]{1,0:T(8,128)(2,1)} %get-tuple-element.91.refs_1_, bf16[96,384]{1,0:T(8,128)(2,1)} %get-tuple-element.92.refs_2_, ...), custom_call_target="tpu_custom_call" | custom-call | bytes 30000000 | tf_op jit(solution)/shard_map/gather_shards/pallas_call | solution.py:756
  90.5 14.4 %norm_and_qkv.1 = (bf16[2048,768]{1,0:T(8,128)(2,1)}, bf16[2048,2304]{1,0:T(8,128)(2,1)}, bf16[768,2304]{1,0:T(8,128)(2,1)}) custom-call(bf16[2048,768]{1,0:T(8,128)(2,1)} %tok.5, f32[2,768]{1,0:T(2,128)} %pad_maximum_fusion.5.vec, f32[1,2304]{1,0:T(1,128)} %reshape.167.bias, bf16[2,16,160,384]{3,2,1,0:T(8,128)(2,1)} %get-tuple-element.96.chunks), custom_call_target="tpu_custom_call" | custom-call | flops 7247757312 | bytes 20000000 | tf_op jit(solution)/shard_map/norm_and_qkv/pallas_call | solution.py:391
  105.5 32.6 %attention_forward.1 = (bf16[2048,768]{1,0:T(8,128)(2,1)}, f32[2,768,1024]{2,1,0:T(8,128)}, f32[2,2,6,1024]{3,2,1,0:T(8,128)}) custom-call(s32[2,8]{1,0:T(2,128)} %get-tuple-element.216.lo, s32[2,8]{1,0:T(2,128)} %get-tuple-element.215.hi, bf16[2048,2304]{1,0:T(8,128)(2,1)} %get-tuple-element.97.q_ref.k_ref.v_ref, ...), custom_call_target="tpu_custom_call" | custom-call | flops 24000000000 | bytes 20000000 | tf_op jit(solution)/shard_map/attention_forward/pallas_call | solution.py:265
  138.1 66.4 %middle.1 = (bf16[2048,768]{1,0:T(8,128)(2,1)}, bf16[2048,768]{1,0:T(8,128)(2,1)}, bf16[2048,3072]{1,0:T(8,128)(2,1)}, bf16[2048,3072]{1,0:T(8,128)(2,1)}, f32[2...) custom-call(bf16[2048,768]{1,0:T(8,128)(2,1)} %get-tuple-element.98., ...), custom_call_target="tpu_custom_call" | custom-call | flops 43486543872 | bytes 60000000 | tf_op jit(solution)/shard_map/middle/pallas_call | solution.py:468
  204.6 10.9 %grad_down_far.1 = bf16[16,4,48,384]{3,2,1,0:T(8,128)(2,1)} custom-call(s32[1]{0:T(128)S(6)} %sub.45.part.send_at.keep_at, s32[1]{0:T(128)S(6)} %sub.45.part.send_at.keep_at, s32[1]{0:T(128)S(6)} %sub.45.part.send_at.keep_at, bf16[2048,768]{1,0:T(8,128)(2,1)} %refs_0_.4, bf16[2048,3072]{1,0:T(8,128)(2,1)} %get-tuple-element.104.refs_1_), custom_call_target="tpu_custom_call" | custom-call | flops 4831838208 | bytes 20000000 | tf_op jit(solution)/shard_map/grad_down_far/pallas_call | solution.py:596
  215.4 11.9 %grad_up_out_far.1 = bf16[16,5,48,384]{3,2,1,0:T(8,128)(2,1)} custom-call(s32[1]{0:T(128)S(6)} %sub.45.part.send_at.keep_at, s32[1]{0:T(128)S(6)} %sub.45.part.send_at.keep_at, s32[1]{0:T(128)S(6)} %sub.45.part.send_at.keep_at, bf16[2048,768]{1,0:T(8,128)(2,1)} %get-tuple-element.111.refs_0_, bf16[2048,3072]{1,0:T(8,128)(2,1)} %get-tuple-element.106.refs_1_, ...), custom_call_target="tpu_custom_call" | custom-call | flops 6039797760 | bytes 20000000 | tf_op jit(solution)/shard_map/grad_up_out_far/pallas_call | solution.py:596
  230.2 6.0 %collective-permute-done.refs_2_ = bf16[16,4,48,384]{3,2,1,0:T(8,128)(2,1)} collective-permute-done((bf16[16,4,48,384]{3,2,1,0:T(8,128)(2,1)S(1)}, bf16[16,4,48,384]{3,2,1,0:T(8,128)(2,1)}, u32[]{:S(2)}, u32[]{:S(2)}) %collective-permute-start) | collective-permute-done | bytes 2359328 | tf_op jit(solution)/shard_map/ppermute | solution.py:637
  236.2 23.6 %grad_down_near.1 = (bf16[8,4,48,384]{3,2,1,0:T(8,128)(2,1)}, bf16[8,4,48,384]{3,2,1,0:T(8,128)(2,1)}) custom-call(s32[1]{0:T(128)} %bitcast.core.part, s32[8]{0:T(128)} %copy-done.14, s32[8]{0:T(128)} %copy-done.15, bf16[2048,768]{1,0:T(8,128)(2,1)} %refs_0_.4, bf16[2048,3072]{1,0:T(8,128)(2,1)} %get-tuple-element.104.refs_1_, ...), custom_call_target="tpu_custom_call" | custom-call | flops 4831838208 | bytes 20000000 | tf_op jit(solution)/shard_map/grad_down_near/pallas_call | solution.py:596
  259.9 2.9 collective-permute-start.3
  262.7 13.1 %grad_up_out_near.1 = (bf16[8,5,48,384]{3,2,1,0:T(8,128)(2,1)}, bf16[8,5,48,384]{3,2,1,0:T(8,128)(2,1)}) custom-call(s32[1]{0:T(128)} %bitcast.core.part, s32[8]{0:T(128)} %copy-done.14, s32[8]{0:T(128)} %copy-done.15, bf16[2048,768]{1,0:T(8,128)(2,1)} %get-tuple-element.111.refs_0_, bf16[2048,3072]{1,0:T(8,128)(2,1)} %get-tuple-element.106.refs_1_, ...), custom_call_target="tpu_custom_call" | custom-call | flops 6039797760 | bytes 20000000 | tf_op jit(solution)/shard_map/grad_up_out_near/pallas_call | solution.py:596
  275.9 30.0 %attention_backward.2.refs_1_.far = bf16[2048,1152]{1,0:T(8,128)(2,1)} custom-call(s32[2,8]{1,0:T(2,128)} %get-tuple-element.216.lo, s32[2,8]{1,0:T(2,128)} %get-tuple-element.215.hi, s32[1]{0:T(128)S(6)} %sub.45.part.send_at.keep_at, bf16[2048,2304]{1,0:T(8,128)(2,1)} %get-tuple-element.97.q_ref.k_ref.v_ref, ...), custom_call_target="tpu_custom_call" | custom-call | flops 22000001024 | bytes 20000000 | tf_op jit(solution)/shard_map/attention_backward/pallas_call | solution.py:303
  307.0 4.5 fold_sums.4
  314.2 4.6 fold_sums.3
  319.2 8.4 %grad_qkv_far.1 = bf16[16,3,48,384]{3,2,1,0:T(8,128)(2,1)} custom-call(s32[1]{0:T(128)S(6)} %sub.45.part.send_at.keep_at, s32[1]{0:T(128)S(6)} %sub.45.part.send_at.keep_at, s32[1]{0:T(128)S(6)} %sub.45.part.send_at.keep_at, bf16[2048,768]{1,0:T(8,128)(2,1)} %get-tuple-element.139.refs_0_, bf16[2048,1152]{1,0:T(8,128)(2,1)} %attention_backward.2.refs_1_.far), custom_call_target="tpu_custom_call" | custom-call | flops 3623878656 | bytes 20000000 | tf_op jit(solution)/shard_map/grad_qkv_far/pallas_call | solution.py:596
  327.6 30.2 %attention_backward.3.near.refs_1_ = bf16[2048,1152]{1,0:T(8,128)(2,1)} custom-call(s32[2,8]{1,0:T(2,128)} %get-tuple-element.216.lo, s32[2,8]{1,0:T(2,128)} %get-tuple-element.215.hi, s32[1]{0:T(128)} %bitcast.core.part, bf16[2048,2304]{1,0:T(8,128)(2,1)} %get-tuple-element.97.q_ref.k_ref.v_ref, bf16[2048,2304]{1,0:T(8,128)(2,1)} %get-tuple-element.97.q_ref.k_ref.v_ref, ...), custom_call_target="tpu_custom_call" | custom-call | flops 22000001024 | bytes 20000000 | tf_op jit(solution)/shard_map/attention_backward/pallas_call | solution.py:303
  358.6 2.1 level_sums.3
  361.6 2.3 level_sums.4
  363.9 18.4 %first_norm_back.1 = (bf16[2048,768]{1,0:T(8,128)(2,1)}, f32[8,1152]{1,0:T(8,128)}) custom-call(s32[2]{0:T(128)} %pad_add_fusion.parts, bf16[2048,1152]{1,0:T(8,128)(2,1)} %attention_backward.2.refs_1_.far, bf16[2048,1152]{1,0:T(8,128)(2,1)} %attention_backward.3.near.refs_1_, bf16[768,2304]{1,0:T(8,128)(2,1)} %get-tuple-element.133.w_far.w_near, ...), custom_call_target="tpu_custom_call" | custom-call | flops 7247757312 | bytes 30000000 | tf_op jit(solution)/shard_map/first_norm_back/pallas_call | solution.py:507
  388.3 2.2 collective-permute-done.7
  395.0 5.9 %collective-permute-start.11 = (f32[384]{0:T(512)S(1)}, f32[384]{0:T(512)S(1)}, u32[]{:S(2)}, u32[]{:S(2)}) collective-permute-start(f32[384]{0:T(512)S(1)} %get-tuple-element.172), channel_id=1, source_target_pairs={{0,24},{1,25},{2,26},{3,27},{4,28},{5,29},{6,30},{7,31},{8,0},{9,1... | collective-permute-start | bytes 4616 | tf_op jit(solution)/shard_map/ppermute | solution.py:637
  401.5 2.0 collective-permute-start.23
  409.8 9.5 %grad_qkv_near.1 = (bf16[8,3,48,384]{3,2,1,0:T(8,128)(2,1)}, bf16[8,3,48,384]{3,2,1,0:T(8,128)(2,1)}) custom-call(s32[1]{0:T(128)} %bitcast.core.part, s32[8]{0:T(128)} %copy-done.14, s32[8]{0:T(128)} %copy-done.15, bf16[2048,768]{1,0:T(8,128)(2,1)} %get-tuple-element.139.refs_0_, bf16[2048,1152]{1,0:T(8,128)(2,1)} %attention_backward.3.near.refs_1_, ...), custom_call_target="tpu_custom_call" | custom-call | flops 3623878656 | bytes 20000000 | tf_op jit(solution)/shard_map/grad_qkv_near/pallas_call | solution.py:596
  419.3 2.7 collective-permute-start.21
  422.3 6.6 %collective-permute-done.20 = bf16[5,48,384]{2,1,0:T(8,128)(2,1)S(1)} collective-permute-done((bf16[5,48,384]{2,1,0:T(8,128)(2,1)S(1)}, bf16[5,48,384]{2,1,0:T(8,128)(2,1)S(1)}, u32[]{:S(2)}, u32[]{:S(2)}) %collective-permute-start.20) | collective-permute-done | bytes 184352 | tf_op jit(solution)/shard_map/ppermute | solution.py:637
  429.5 5.8 %collective-permute-done.13.b_send.b_keep = bf16[8,3,48,384]{3,2,1,0:T(8,128)(2,1)S(1)} collective-permute-done((bf16[8,3,48,384]{3,2,1,0:T(8,128)(2,1)}, bf16[8,3,48,384]{3,2,1,0:T(8,128)(2,1)S(1)}, u32[]{:S(2)}, u32[]{:S(2)}) %collective-permute-start.13) | collective-permute-done | bytes 884768 | tf_op jit(solution)/shard_map/ppermute | solution.py:637
  436.3 4.3 fold_sums.5
  440.5 2.1 collective-permute-start.14
  443.5 5.6 %collective-permute-done.14.got = bf16[4,3,48,384]{3,2,1,0:T(8,128)(2,1)S(1)} collective-permute-done((bf16[4,3,48,384]{3,2,1,0:T(8,128)(2,1)}, bf16[4,3,48,384]{3,2,1,0:T(8,128)(2,1)S(1)}, u32[]{:S(2)}, u32[]{:S(2)}) %collective-permute-start.14) | collective-permute-done | bytes 442400 | tf_op jit(solution)/shard_map/ppermute | solution.py:637
  449.9 2.0 level_sums.5
  452.7 3.5 collective-permute-start.16
  458.7 2.4 collective-permute-done.16
  (186 shorter events, 47.0 us)
Async XLA Ops:
  227.3 35.4 %collective-permute-start.1 = (bf16[16,5,48,384]{3,2,1,0:T(8,128)(2,1)}, bf16[16,5,48,384]{3,2,1,0:T(8,128)(2,1)}, u32[]{:S(2)}, u32[]{:S(2)}) collective-permute-start(bf16[16,5,48,384]{3,2,1,0:T(8,128)(2,1)} %grad_up_out_far.1), channel_id=1, source_target_pairs={{0,1},{1,0},{2,3},{3,2},{4,5},{5,4},{6,7},{7,6},{8,9},{9,8},{10,11... | collective-permute-start | bytes 8847368 | tf_op jit(solution)/shard_map/ppermute | solution.py:637
  227.7 8.5 %collective-permute-start = (bf16[16,4,48,384]{3,2,1,0:T(8,128)(2,1)S(1)}, bf16[16,4,48,384]{3,2,1,0:T(8,128)(2,1)}, u32[]{:S(2)}, u32[]{:S(2)}) collective-permute-start(bf16[16,4,48,384]{3,2,1,0:T(8,128)(2,1)S(1)} %copy-done.3), channel_id=1, source_target_pairs={{0,1},{1,0},{2,3},{3,2},{4,5},{5,4},{6,7},{7,6},{8,9},{9,8},{10,11... | collective-permute-start | bytes 7077896 | tf_op jit(solution)/shard_map/ppermute | solution.py:637
  259.9 46.1 %collective-permute-start.3 = (bf16[8,4,48,384]{3,2,1,0:T(8,128)(2,1)}, bf16[8,4,48,384]{3,2,1,0:T(8,128)(2,1)S(1)}, u32[]{:S(2)}, u32[]{:S(2)}) collective-permute-start(bf16[8,4,48,384]{3,2,1,0:T(8,128)(2,1)} %get-tuple-element.110), channel_id=1, source_target_pairs={{0,2},{1,5},{2,0},{3,7},{4,6},{5,1},{6,4},{7,3},{8,10},{9,13},{10,... | collective-permute-start | bytes 3538952 | tf_op jit(solution)/shard_map/ppermute | solution.py:637
  275.8 37.2 %collective-permute-start.2 = (bf16[8,5,48,384]{3,2,1,0:T(8,128)(2,1)}, bf16[8,5,48,384]{3,2,1,0:T(8,128)(2,1)S(1)}, u32[]{:S(2)}, u32[]{:S(2)}) collective-permute-start(bf16[8,5,48,384]{3,2,1,0:T(8,128)(2,1)} %get-tuple-element.113), channel_id=1, source_target_pairs={{0,2},{1,5},{2,0},{3,7},{4,6},{5,1},{6,4},{7,3},{8,10},{9,13},{10,... | collective-permute-start | bytes 4423688 | tf_op jit(solution)/shard_map/ppermute | solution.py:637
  311.4 46.4 %collective-permute-start.4 = (bf16[4,4,48,384]{3,2,1,0:T(8,128)(2,1)}, bf16[4,4,48,384]{3,2,1,0:T(8,128)(2,1)S(1)}, u32[]{:S(2)}, u32[]{:S(2)}) collective-permute-start(bf16[4,4,48,384]{3,2,1,0:T(8,128)(2,1)} %get-tuple-element.123), channel_id=1, source_target_pairs={{0,4},{1,3},{2,6},{3,1},{4,0},{5,7},{6,2},{7,5},{8,12},{9,11},{10,... | collective-permute-start | bytes 1769480 | tf_op jit(solution)/shard_map/ppermute | solution.py:637
  318.8 41.9 %collective-permute-start.5 = (bf16[4,5,48,384]{3,2,1,0:T(8,128)(2,1)}, bf16[4,5,48,384]{3,2,1,0:T(8,128)(2,1)S(1)}, u32[]{:S(2)}, u32[]{:S(2)}) collective-permute-start(bf16[4,5,48,384]{3,2,1,0:T(8,128)(2,1)} %get-tuple-element.120), channel_id=1, source_target_pairs={{0,4},{1,3},{2,6},{3,1},{4,0},{5,7},{6,2},{7,5},{8,12},{9,11},{10,... | collective-permute-start | bytes 2211848 | tf_op jit(solution)/shard_map/ppermute | solution.py:637
  363.9 37.6 %copy-start.21 = (bf16[4,48,384]{2,1,0:T(8,128)(2,1)S(1)}, bf16[4,48,384]{2,1,0:T(8,128)(2,1)}, u32[]{:S(2)}) copy-start(bf16[4,48,384]{2,1,0:T(8,128)(2,1)} %get-tuple-element.156) | copy-start | bytes 442372
  363.9 39.6 %copy-start.20 = (bf16[4,48,384]{2,1,0:T(8,128)(2,1)S(1)}, bf16[4,48,384]{2,1,0:T(8,128)(2,1)}, u32[]{:S(2)}) copy-start(bf16[4,48,384]{2,1,0:T(8,128)(2,1)} %get-tuple-element.157) | copy-start | bytes 442372
  363.9 41.5 %copy-start.19 = (bf16[4,48,384]{2,1,0:T(8,128)(2,1)S(1)}, bf16[4,48,384]{2,1,0:T(8,128)(2,1)}, u32[]{:S(2)}) copy-start(bf16[4,48,384]{2,1,0:T(8,128)(2,1)} %get-tuple-element.158) | copy-start | bytes 442372
  363.9 42.7 %copy-start.18 = (bf16[5,48,384]{2,1,0:T(8,128)(2,1)S(1)}, bf16[5,48,384]{2,1,0:T(8,128)(2,1)}, u32[]{:S(2)}) copy-start(bf16[5,48,384]{2,1,0:T(8,128)(2,1)} %get-tuple-element.149) | copy-start | bytes 552964
  363.9 44.7 %copy-start.17 = (bf16[5,48,384]{2,1,0:T(8,128)(2,1)S(1)}, bf16[5,48,384]{2,1,0:T(8,128)(2,1)}, u32[]{:S(2)}) copy-start(bf16[5,48,384]{2,1,0:T(8,128)(2,1)} %get-tuple-element.150) | copy-start | bytes 552964
  384.9 1.3 collective-permute-start.6
  385.0 23.6 %collective-permute-start.12 = (bf16[16,3,48,384]{3,2,1,0:T(8,128)(2,1)}, bf16[16,3,48,384]{3,2,1,0:T(8,128)(2,1)}, u32[]{:S(2)}, u32[]{:S(2)}) collective-permute-start(bf16[16,3,48,384]{3,2,1,0:T(8,128)(2,1)} %grad_qkv_far.1), channel_id=1, source_target_pairs={{0,1},{1,0},{2,3},{3,2},{4,5},{5,4},{6,7},{7,6},{8,9},{9,8},{10,11... | collective-permute-start | bytes 5308424 | tf_op jit(solution)/shard_map/ppermute | solution.py:637
  386.8 3.7 collective-permute-start.7
  391.2 3.6 collective-permute-start.8
  395.0 8.6 %collective-permute-start.10 = (f32[384]{0:T(512)S(1)}, f32[384]{0:T(512)S(1)}, u32[]{:S(2)}, u32[]{:S(2)}) collective-permute-start(f32[384]{0:T(512)S(1)} %get-tuple-element.173), channel_id=1, source_target_pairs={{0,16},{1,17},{2,18},{3,19},{4,20},{5,21},{6,22},{7,23},{8,24},{9,... | collective-permute-start | bytes 4616 | tf_op jit(solution)/shard_map/ppermute | solution.py:637
  395.0 10.3 %collective-permute-start.11 = (f32[384]{0:T(512)S(1)}, f32[384]{0:T(512)S(1)}, u32[]{:S(2)}, u32[]{:S(2)}) collective-permute-start(f32[384]{0:T(512)S(1)} %get-tuple-element.172), channel_id=1, source_target_pairs={{0,24},{1,25},{2,26},{3,27},{4,28},{5,29},{6,30},{7,31},{8,0},{9,1... | collective-permute-start | bytes 4616 | tf_op jit(solution)/shard_map/ppermute | solution.py:637
  401.0 5.6 %collective-permute-start.9 = (f32[384]{0:T(512)S(1)}, f32[384]{0:T(512)S(1)}, u32[]{:S(2)}, u32[]{:S(2)}) collective-permute-start(f32[384]{0:T(512)S(1)} %get-tuple-element.171), channel_id=1, source_target_pairs={{0,8},{1,9},{2,10},{3,11},{4,12},{5,13},{6,14},{7,15},{8,16},{9,17... | collective-permute-start | bytes 4616 | tf_op jit(solution)/shard_map/ppermute | solution.py:637
  401.5 17.8 %collective-permute-start.23 = (bf16[4,48,384]{2,1,0:T(8,128)(2,1)S(1)}, bf16[4,48,384]{2,1,0:T(8,128)(2,1)S(1)}, u32[]{:S(2)}, u32[]{:S(2)}) collective-permute-start(bf16[4,48,384]{2,1,0:T(8,128)(2,1)S(1)} %copy-done.21), channel_id=1, source_target_pairs={{0,8},{1,9},{2,10},{3,11},{4,12},{5,13},{6,14},{7,15},{8,16},{9,17... | collective-permute-start | bytes 442376 | tf_op jit(solution)/shard_map/ppermute | solution.py:637
  403.5 18.6 %collective-permute-start.24 = (bf16[4,48,384]{2,1,0:T(8,128)(2,1)S(1)}, bf16[4,48,384]{2,1,0:T(8,128)(2,1)S(1)}, u32[]{:S(2)}, u32[]{:S(2)}) collective-permute-start(bf16[4,48,384]{2,1,0:T(8,128)(2,1)S(1)} %copy-done.20), channel_id=1, source_target_pairs={{0,16},{1,17},{2,18},{3,19},{4,20},{5,21},{6,22},{7,23},{8,24},{9,... | collective-permute-start | bytes 442376 | tf_op jit(solution)/shard_map/ppermute | solution.py:637
  405.4 16.7 %collective-permute-start.25 = (bf16[4,48,384]{2,1,0:T(8,128)(2,1)S(1)}, bf16[4,48,384]{2,1,0:T(8,128)(2,1)S(1)}, u32[]{:S(2)}, u32[]{:S(2)}) collective-permute-start(bf16[4,48,384]{2,1,0:T(8,128)(2,1)S(1)} %copy-done.19), channel_id=1, source_target_pairs={{0,24},{1,25},{2,26},{3,27},{4,28},{5,29},{6,30},{7,31},{8,0},{9,1... | collective-permute-start | bytes 442376 | tf_op jit(solution)/shard_map/ppermute | solution.py:637
  406.6 15.7 %collective-permute-start.19 = (bf16[5,48,384]{2,1,0:T(8,128)(2,1)S(1)}, bf16[5,48,384]{2,1,0:T(8,128)(2,1)S(1)}, u32[]{:S(2)}, u32[]{:S(2)}) collective-permute-start(bf16[5,48,384]{2,1,0:T(8,128)(2,1)S(1)} %copy-done.18), channel_id=1, source_target_pairs={{0,8},{1,9},{2,10},{3,11},{4,12},{5,13},{6,14},{7,15},{8,16},{9,17... | collective-permute-start | bytes 552968 | tf_op jit(solution)/shard_map/ppermute | solution.py:637
  408.7 20.2 %collective-permute-start.20 = (bf16[5,48,384]{2,1,0:T(8,128)(2,1)S(1)}, bf16[5,48,384]{2,1,0:T(8,128)(2,1)S(1)}, u32[]{:S(2)}, u32[]{:S(2)}) collective-permute-start(bf16[5,48,384]{2,1,0:T(8,128)(2,1)S(1)} %copy-done.17), channel_id=1, source_target_pairs={{0,16},{1,17},{2,18},{3,19},{4,20},{5,21},{6,22},{7,23},{8,24},{9,... | collective-permute-start | bytes 552968 | tf_op jit(solution)/shard_map/ppermute | solution.py:637
  419.3 10.0 %collective-permute-start.21 = (bf16[5,48,384]{2,1,0:T(8,128)(2,1)S(1)}, bf16[5,48,384]{2,1,0:T(8,128)(2,1)S(1)}, u32[]{:S(2)}, u32[]{:S(2)}) collective-permute-start(bf16[5,48,384]{2,1,0:T(8,128)(2,1)S(1)} %copy-done.16), channel_id=1, source_target_pairs={{0,24},{1,25},{2,26},{3,27},{4,28},{5,29},{6,30},{7,31},{8,0},{9,1... | collective-permute-start | bytes 552968 | tf_op jit(solution)/shard_map/ppermute | solution.py:637
  422.1 13.3 %collective-permute-start.13 = (bf16[8,3,48,384]{3,2,1,0:T(8,128)(2,1)}, bf16[8,3,48,384]{3,2,1,0:T(8,128)(2,1)S(1)}, u32[]{:S(2)}, u32[]{:S(2)}) collective-permute-start(bf16[8,3,48,384]{3,2,1,0:T(8,128)(2,1)} %get-tuple-element.142), channel_id=1, source_target_pairs={{0,2},{1,5},{2,0},{3,7},{4,6},{5,1},{6,4},{7,3},{8,10},{9,13},{10,... | collective-permute-start | bytes 2654216 | tf_op jit(solution)/shard_map/ppermute | solution.py:637
  422.2 20.4 %collective-permute-start.26 = (f32[96,384]{1,0:T(8,128)S(1)}, f32[96,384]{1,0:T(8,128)S(1)}, u32[]{:S(2)}, u32[]{:S(2)}) collective-permute-start(f32[96,384]{1,0:T(8,128)S(1)} %bitcast.89), channel_id=1, source_target_pairs={{0,1},{1,0},{2,3},{3,2},{4,5},{5,4},{6,7},{7,6},{8,9},{9,8},{10,11... | collective-permute-start | bytes 442376 | tf_op jit(solution)/shard_map/ppermute | solution.py:637
  429.5 14.0 %collective-permute-start.22 = (f32[5,24,384]{2,1,0:T(8,128)S(1)}, f32[5,24,384]{2,1,0:T(8,128)S(1)}, u32[]{:S(2)}, u32[]{:S(2)}) collective-permute-start(f32[5,24,384]{2,1,0:T(8,128)S(1)} %fusion.3), channel_id=1, source_target_pairs={{0,1},{1,0},{2,3},{3,2},{4,5},{5,4},{6,7},{7,6},{8,9},{9,8},{10,11... | collective-permute-start | bytes 552968 | tf_op jit(solution)/shard_map/ppermute | solution.py:637
  440.5 8.6 %collective-permute-start.14 = (bf16[4,3,48,384]{3,2,1,0:T(8,128)(2,1)}, bf16[4,3,48,384]{3,2,1,0:T(8,128)(2,1)S(1)}, u32[]{:S(2)}, u32[]{:S(2)}) collective-permute-start(bf16[4,3,48,384]{3,2,1,0:T(8,128)(2,1)} %get-tuple-element.144), channel_id=1, source_target_pairs={{0,4},{1,3},{2,6},{3,1},{4,0},{5,7},{6,2},{7,5},{8,12},{9,11},{10,... | collective-permute-start | bytes 1327112 | tf_op jit(solution)/shard_map/ppermute | solution.py:637
  451.9 6.8 %collective-permute-start.15 = (bf16[3,48,384]{2,1,0:T(8,128)(2,1)}, bf16[3,48,384]{2,1,0:T(8,128)(2,1)S(1)}, u32[]{:S(2)}, u32[]{:S(2)}) collective-permute-start(bf16[3,48,384]{2,1,0:T(8,128)(2,1)} %get-tuple-element.146), channel_id=1, source_target_pairs={{0,8},{1,9},{2,10},{3,11},{4,12},{5,13},{6,14},{7,15},{8,16},{9,17... | collective-permute-start | bytes 331784 | tf_op jit(solution)/shard_map/ppermute | solution.py:637
  452.7 8.4 %collective-permute-start.16 = (bf16[3,48,384]{2,1,0:T(8,128)(2,1)}, bf16[3,48,384]{2,1,0:T(8,128)(2,1)S(1)}, u32[]{:S(2)}, u32[]{:S(2)}) collective-permute-start(bf16[3,48,384]{2,1,0:T(8,128)(2,1)} %get-tuple-element.147), channel_id=1, source_target_pairs={{0,16},{1,17},{2,18},{3,19},{4,20},{5,21},{6,22},{7,23},{8,24},{9,... | collective-permute-start | bytes 331784 | tf_op jit(solution)/shard_map/ppermute | solution.py:637
  456.2 5.9 %collective-permute-start.17 = (bf16[3,48,384]{2,1,0:T(8,128)(2,1)}, bf16[3,48,384]{2,1,0:T(8,128)(2,1)S(1)}, u32[]{:S(2)}, u32[]{:S(2)}) collective-permute-start(bf16[3,48,384]{2,1,0:T(8,128)(2,1)} %get-tuple-element.148), channel_id=1, source_target_pairs={{0,24},{1,25},{2,26},{3,27},{4,28},{5,29},{6,30},{7,31},{8,0},{9,1... | collective-permute-start | bytes 331784 | tf_op jit(solution)/shard_map/ppermute | solution.py:637
  463.2 1.4 collective-permute-start.18
  (17 other events, 178.5 us)

commit v3 on v2

--- a/solution.py
+++ b/solution.py
@@ -173,7 +173,7 @@
 
 
 def attn_bwd_kernel(
-    lo, hi, part, q_ref, k_ref, v_ref, do_ref, ot_ref, lse_ref, oh_ref, mr_ref, dqkv_ref,
+    lo, hi, q_ref, k_ref, v_ref, do_ref, ot_ref, lse_ref, oh_ref, mr_ref, dqkv_ref,
     qt, kt, dot, extra_q, extra_d, dqt, dkt, dvt,
 ):
     seq = pl.program_id(0)
@@ -295,25 +295,25 @@
     )(lo, hi, qkv, qkv, qkv, onehot, miss)
 
 
-def attention_bwd(qkv, d_attn, ot, lse, lo, hi, onehot, miss, part):
+def attention_bwd(qkv, d_attn, ot, lse, lo, hi, onehot, miss):
     seqs = lo.shape[0]
     rows = qkv.shape[0] // seqs
     wide = WIDE
-    col = lambda at: pl.BlockSpec((rows, wide), lambda s, lo, hi, p: (s, 3 * p[0] + at))
+    col = lambda at: pl.BlockSpec((rows, wide), lambda s, j, *_: (s, 3 * j + at))
     return pl.pallas_call(
         attn_bwd_kernel,
         grid_spec=pltpu.PrefetchScalarGridSpec(
-            num_scalar_prefetch=3,
-            grid=(seqs,),
+            num_scalar_prefetch=2,
+            grid=(seqs, d_attn.shape[1] // wide),
             in_specs=[
                 col(0), col(1), col(2),
-                pl.BlockSpec((rows, wide), lambda s, lo, hi, p: (s, p[0])),
-                pl.BlockSpec((1, wide, rows), lambda s, lo, hi, p: (s, p[0], 0)),
-                pl.BlockSpec((1, 1, wide // HD, rows), lambda s, lo, hi, p: (s, p[0], 0, 0)),
+                pl.BlockSpec((rows, wide), lambda s, j, *_: (s, j)),
+                pl.BlockSpec((1, wide, rows), lambda s, j, *_: (s, j, 0)),
+                pl.BlockSpec((1, 1, wide // HD, rows), lambda s, j, *_: (s, j, 0, 0)),
                 pl.BlockSpec((rows, 128), lambda s, *_: (s, 0)),
                 pl.BlockSpec((1, 8, rows), lambda s, *_: (s, 0, 0)),
             ],
-            out_specs=pl.BlockSpec((rows, 3 * wide), lambda s, *_: (s, 0)),
+            out_specs=pl.BlockSpec((rows, 3 * wide), lambda s, j, *_: (s, j)),
             scratch_shapes=[
                 pltpu.VMEM((wide, rows), BF),
                 pltpu.VMEM((wide, rows), BF),
@@ -325,11 +325,11 @@
                 pltpu.VMEM((wide, rows), F32),
             ],
         ),
-        out_shape=jax.ShapeDtypeStruct((qkv.shape[0], 3 * wide), BF),
-        compiler_params=params("arbitrary"),
-        cost_estimate=cost(22e9, 2e7),
+        out_shape=jax.ShapeDtypeStruct(qkv.shape, BF),
+        compiler_params=params("arbitrary", "arbitrary"),
+        cost_estimate=cost(44e9, 4e7),
         name="attention_backward",
-    )(lo, hi, part, qkv, qkv, qkv, d_attn, ot, lse, onehot, miss)
+    )(lo, hi, qkv, qkv, qkv, d_attn, ot, lse, onehot, miss)
 
 
 def normalized(x):
@@ -489,59 +489,43 @@
     )(attn, tokens, cotangent, vec, b1, *gathered)
 
 
-def first_norm_kernel(parts, far, near, w_far, w_near, tok, d_mid, vec, out, sums):
+def first_norm_kernel(d_qkv, w, tok, d_mid, vec, out, sums):
     clear_first(sums)
-    d = mm_nt(far[...], w_far[...]) + mm_nt(near[...], w_near[...])
+    d = mm_nt(d_qkv[...], w[...])
     xhat, scale = normalized(tok[...].astype(F32))
     add_row(sums, 0, d * xhat)
     add_row(sums, 1, d)
-    add_row(sums, 2, far[...].astype(F32))
-    add_row(sums, 3, near[...].astype(F32))
+    add_row(sums, 2, d_qkv[...].astype(F32))
     out[...] = (d_mid[...] + norm_back(d, xhat, scale, vec[0:1])).astype(BF)
 
 
-def first_norm_back(far, near, w, tokens, d_mid, vec, parts):
+def first_norm_back(d_qkv, w, tokens, d_mid, vec):
     count, width = tokens.shape
-    cols = far.shape[1]
-    tile = lambda w: pl.BlockSpec((TILE, w), lambda i, p: (i, 0))
+    cols = d_qkv.shape[1]
+    tile = lambda w: pl.BlockSpec((TILE, w), lambda i: (i, 0))
     return pl.pallas_call(
         first_norm_kernel,
-        grid_spec=pltpu.PrefetchScalarGridSpec(
-            num_scalar_prefetch=1,
-            grid=(count // TILE,),
-            in_specs=[
-                tile(cols), tile(cols),
-                pl.BlockSpec((width, cols), lambda i, p: (0, p[0])),
-                pl.BlockSpec((width, cols), lambda i, p: (0, p[1])),
-                tile(width), tile(width), whole(vec.shape),
-            ],
-            out_specs=[tile(width), whole((8, cols))],
-        ),
+        grid=(count // TILE,),
+        in_specs=[tile(cols), whole(w.shape), tile(width), tile(width), whole(vec.shape)],
+        out_specs=[tile(width), whole((8, cols))],
         out_shape=[jax.ShapeDtypeStruct((count, width), BF), jax.ShapeDtypeStruct((8, cols), F32)],
         compiler_params=params("arbitrary"),
-        cost_estimate=cost(4 * count * width * cols, 3e7),
+        cost_estimate=cost(2 * count * width * cols, 3e7),
         name="first_norm_back",
-    )(parts, far, near, w, w, tokens, d_mid, vec)
+    )(d_qkv, w, tokens, d_mid, vec)
 
 
 def tn(a, b):
     return lax.dot_general(a, b, (((0,), (0,)), ((), ())), preferred_element_type=F32)
 
 
-def grad_kernel(layout, near, part, send_at, keep_at, *refs):
+def grad_kernel(layout, *refs):
     count = len(layout)
-    ins, refs = refs[: 2 * count], refs[2 * count :]
-    if near:
-        got, (send, keep), (sums, total, held, sem) = refs[0], refs[1:3], (refs[3 : 3 + count], *refs[3 + count :])
-    else:
-        out, sums = refs[0], refs[1 : 1 + count]
+    ins, out, sums = refs[: 2 * count], refs[2 * count], refs[2 * count + 1 :]
     step = pl.program_id(0)
-    arrival = pltpu.make_async_copy(got, held, sem.at[0]) if near else None
 
     @pl.when(step == 0)
     def _():
-        if near:
-            arrival.start()
         for acc in sums:
             acc[...] = jnp.zeros_like(acc)
 
@@ -550,95 +534,41 @@
 
     @pl.when(step == pl.num_programs(0) - 1)
     def _():
-        target = total if near else out
-        chips, _, rows, _ = target.shape
-        kind = target.dtype
+        _, chips, _, rows, _ = out.shape
         base = 0
         for k, blocks in enumerate(layout):
-            if blocks == 0:
-                target[...] = sums[k][...].astype(kind).T.reshape(target.shape)
-            for b in range(blocks):
-                cols = slice(b * WIDE, (b + 1) * WIDE)
-                target[:, base + b] = sums[k][:, cols].astype(kind).reshape(chips, rows, WIDE)
-            base += blocks
-        if near:
-            arrival.wait()
-
-            def body(j, carry):
-                for at, ref in ((send_at, send), (keep_at, keep)):
-                    i = at[j]
-                    ref[j] = (total[i] + held[i].astype(F32)).astype(BF)
-                return carry
-
-            lax.fori_loop(0, chips // 2, body, 0)
-
-
-def grad_part(pairs, part, chips, name, got=None, order=None):
+            tall = sums[k].shape[0] // (chips * rows)
+            for h in range(2):
+                for b in range(blocks):
+                    at = (h * blocks + b) * WIDE
+                    low = sums[k][:, at : at + WIDE].astype(BF)
+                    out[h, :, base + b * tall : base + (b + 1) * tall] = low.reshape(chips, tall, rows, WIDE)
+            base += blocks * tall
+
+
+def grad_part(pairs, chips, rows, name):
     tokens = pairs[0][0].shape[0]
-    near = got is not None
-    specs, arrays, scratch, layout, flops = [], [], [], [], 0
-    for lhs, tall, lhs_part, rhs, wide, rhs_part in pairs:
-        for x, cols, by_part in ((lhs, tall, lhs_part), (rhs, wide, rhs_part)):
-            specs.append(pl.BlockSpec((TILE, cols), lambda i, p, *_, by_part=by_part: (i, p[0] if by_part else 0)))
+    specs, arrays, scratch, layout, flops, total = [], [], [], [], 0, 0
+    for lhs, rhs in pairs:
+        for x in (lhs, rhs):
+            specs.append(pl.BlockSpec((TILE, x.shape[1]), lambda i: (i, 0)))
             arrays.append(x)
-        scratch.append(pltpu.VMEM((tall, wide), F32))
-        layout.append(0 if tall == WIDE else wide // WIDE)
-        flops += 2 * tokens * tall * wide
-    if layout[0] == 0:
-        shape = (chips, 4, pairs[0][4] // chips // 4, WIDE)
-    else:
-        shape = (chips, sum(layout), pairs[0][1] // chips, WIDE)
-    out = jax.ShapeDtypeStruct((chips // 2 if near else chips,) + shape[1:], BF)
-    spec = whole(out.shape)
-    if near:
-        specs, arrays = specs + [ANYWHERE], arrays + [got]
-        scratch += [pltpu.VMEM(shape, F32), pltpu.VMEM(shape, BF), pltpu.SemaphoreType.DMA((1,))]
+        scratch.append(pltpu.VMEM((lhs.shape[1], rhs.shape[1]), F32))
+        layout.append(rhs.shape[1] // (2 * WIDE))
+        total += layout[-1] * (lhs.shape[1] // (chips * rows))
+        flops += 2 * tokens * lhs.shape[1] * rhs.shape[1]
+    shape = (2, chips, total, rows, WIDE)
     return pl.pallas_call(
-        functools.partial(grad_kernel, tuple(layout), near),
-        grid_spec=pltpu.PrefetchScalarGridSpec(
-            num_scalar_prefetch=3,
-            grid=(tokens // TILE,),
-            in_specs=specs,
-            out_specs=[spec, spec] if near else spec,
-            scratch_shapes=scratch,
-        ),
-        out_shape=[out, out] if near else out,
+        functools.partial(grad_kernel, tuple(layout)),
+        grid=(tokens // TILE,),
+        in_specs=specs,
+        out_specs=whole(shape),
+        out_shape=jax.ShapeDtypeStruct(shape, BF),
+        scratch_shapes=scratch,
         compiler_params=params("arbitrary"),
-        cost_estimate=cost(flops, 2e7),
+        cost_estimate=cost(flops, 3e7),
         name=name,
-    )(part, *(order or (part, part)), *arrays)
-
-
-def here():
-    me = lax.axis_index("fsdp")
-    return me // 8, (me // 4) % 2, (me // 2) % 2, me % 2
-
-
-def pairs_of(devices, move):
-    depth = devices // 8
-    found = []
-    for i in range(devices):
-        z, y, x, c = move(i // 8, (i // 4) % 2, (i // 2) % 2, i % 2)
-        found.append((i, (((z % depth) * 2 + y) * 2 + x) * 2 + c))
-    return found
-
-
-class Moves:
-    def __init__(self, devices):
-        self.depth = devices // 8
-        self.chips = devices // 2
-        self.core = pairs_of(devices, lambda z, y, x, c: (z, y, x, 1 - c))
-        self.first = pairs_of(devices, lambda z, y, x, c: (z, 1 - y, x, c) if c == 0 else (z, y, 1 - x, c))
-        self.second = pairs_of(devices, lambda z, y, x, c: (z, y, 1 - x, c) if c == 0 else (z, 1 - y, x, c))
-        self.deep = [pairs_of(devices, lambda z, y, x, c, k=k: (z + k, y, x, c)) for k in range(self.depth)]
-
-
-def swap(x, moves):
-    return lax.ppermute(x, "fsdp", moves)
-
-
-def of_two(pick_second, a, b):
-    return jnp.where(pick_second, b, a)
+    )(*arrays)
 
 
 def neighbours():
@@ -802,92 +732,184 @@
     )(core, *ins)
 
 
-def gate(x, *after):
-    return lax.optimization_barrier((x,) + after)[0]
-
-
-def fold_kernel(send_at, keep_at, a_send, b_send, a_keep, b_keep, send, keep):
-    send[...] = (a_send[...].astype(F32) + b_send[...].astype(F32)).astype(BF)
-    keep[...] = (a_keep[...].astype(F32) + b_keep[...].astype(F32)).astype(BF)
-
-
-def fold(a, b, send_at, keep_at):
-    count = send_at.shape[0]
-    block = (1,) + a.shape[1:]
-    none = (0,) * (a.ndim - 1)
-    sent = pl.BlockSpec(block, lambda j, s, k: (s[j],) + none)
-    kept = pl.BlockSpec(block, lambda j, s, k: (k[j],) + none)
-    out = pl.BlockSpec(block, lambda j, s, k: (j,) + none)
-    shape = jax.ShapeDtypeStruct((count,) + a.shape[1:], BF)
+def scatter_kernel(depth, splits, *refs):
+    flows = len(splits)
+    ins, outs, rest = refs[:flows], refs[flows : 2 * flows], refs[2 * flows :]
+    me, core, z, first, second = neighbours()
+    chip = me // 2
+    x, y = lax.rem(chip, 2), lax.rem(chip // 2, 2)
+    twin = me + 1 - 2 * core
+    deep = [lax.rem(z + k, depth) * 8 + lax.rem(me, 8) for k in range(1, depth)]
+    greet([twin, me + first, me + second] + deep)
+    plane = 2 * depth
+    chips = 2 * plane
+
+    def chip_of(j, core):
+        bit2, bit1 = x + core * (y - x), y + core * (x - y)
+        keep, side, k = j // plane, lax.rem(j, plane) // depth, lax.rem(j, depth)
+        bit2 = (1 - bit2) + keep * (2 * bit2 - 1)
+        bit1 = (1 - bit1) + side * (2 * bit1 - 1)
+        return lax.rem(z + 1 + k, depth) * 4 + bit1 * (2 - core) + bit2 * (1 + core)
+
+    def remote(src, dst, send_sem, recv_sem, device):
+        return pltpu.make_async_remote_copy(
+            src_ref=src,
+            dst_ref=dst,
+            send_sem=send_sem,
+            recv_sem=recv_sem,
+            device_id=(device,),
+            device_id_type=pl.DeviceIdType.MESH,
+        )
+
+    def arrived(ref, sem):
+        pltpu.make_async_copy(ref, ref, sem).wait()
+
+    def flow(f):
+        return rest[8 * f : 8 * f + 8]
+
+    def sems(f):
+        return rest[8 * flows + 11 * f : 8 * flows + 11 * f + 11]
+
+    def loop(count, body):
+        def step(j, carry):
+            body(j)
+            return carry
+
+        lax.fori_loop(0, count, step, 0)
+
+    def begin(f):
+        own, in0 = flow(f)[:2]
+        load, got0, sent0 = sems(f)[0], sems(f)[1], sems(f)[6]
+
+        def body(j):
+            pltpu.make_async_copy(ins[f].at[core, chip_of(j, core)], own.at[j], load.at[j]).start()
+            remote(ins[f].at[1 - core, chip_of(j, 1 - core)], in0.at[j], sent0.at[0], got0.at[j], twin).start()
+
+        loop(chips, body)
+
+    def sum_of(f, j):
+        own, in0 = flow(f)[:2]
+        arrived(own.at[j], sems(f)[0].at[j])
+        arrived(in0.at[j], sems(f)[1].at[j])
+        return own[j].astype(F32) + in0[j].astype(F32)
+
+    def lagging(count, compute, send):
+        def body(j):
+            compute(j)
+
+            @pl.when(j > 0)
+            def _():
+                send(j - 1)
+
+        loop(count, body)
+        send(count - 1)
+
+    def across(f):
+        own, _, in1 = flow(f)[:3]
+        got1, sent1 = sems(f)[2], sems(f)[7]
+
+        def compute(j):
+            own[j] = sum_of(f, j).astype(own.dtype)
+
+        lagging(plane, compute, lambda j: remote(own.at[j], in1.at[j], sent1.at[0], got1.at[j], me + second).start())
+
+    def kept(f, j):
+        in1 = flow(f)[2]
+        arrived(in1.at[j], sems(f)[2].at[j])
+        return sum_of(f, plane + j) + in1[j].astype(F32)
+
+    def along(f):
+        own, in2 = flow(f)[0], flow(f)[3]
+        got2, sent2 = sems(f)[3], sems(f)[8]
+
+        def compute(k):
+            own[plane + k] = kept(f, k).astype(own.dtype)
+
+        lagging(
+            depth, compute, lambda k: remote(own.at[plane + k], in2.at[k], sent2.at[0], got2.at[k], me + first).start()
+        )
+
+    def upward(f):
+        own, in2, in3, total = flow(f)[0], flow(f)[3], flow(f)[4], flow(f)[5]
+        got2, got3, sent3 = sems(f)[3], sems(f)[4], sems(f)[9]
+
+        def value(k):
+            arrived(in2.at[k], got2.at[k])
+            return kept(f, depth + k) + in2[k].astype(F32)
+
+        for k in range(depth - 1):
+            own[plane + depth + k] = value(k).astype(own.dtype)
+            if k > 0:
+                remote(own.at[plane + depth + k - 1], in3.at[k - 1], sent3.at[0], got3.at[k - 1], deep[k - 1]).start()
+        total[...] = value(depth - 1)
+        k = depth - 2
+        remote(own.at[plane + depth + k], in3.at[k], sent3.at[0], got3.at[k], deep[k]).start()
+
+    def mine(f, ref, which):
+        if splits[f] == "rows":
+            half = ref.shape[1] // 2
+            return ref.at[:, pl.ds(pl.multiple_of(which * half, 8), half), :]
+        half = ref.shape[0] // 2
+        return ref.at[pl.ds(which * half, half)]
+
+    def finish(f):
+        in3, total, theirs = flow(f)[4], flow(f)[5], flow(f)[6]
+        for k in range(depth - 1):
+            arrived(in3.at[k], sems(f)[4].at[k])
+            total[...] += in3[k].astype(F32)
+        if splits[f] is None:
+            outs[f][...] = total[...]
+        else:
+            outs[f][core] = mine(f, total, core)[...]
+            remote(mine(f, total, 1 - core), theirs, sems(f)[10].at[0], sems(f)[5].at[0], twin).start()
+
+    for f in range(flows):
+        begin(f)
+    for f in range(flows):
+        across(f)
+    for step in range(flows + 2):
+        for stage, run in enumerate((along, upward, finish)):
+            if 0 <= step - stage < flows:
+                run(step - stage)
+    for f in range(flows):
+        _, in0, in1, in2, in3, total, theirs, _ = flow(f)
+        if splits[f] is not None:
+            arrived(theirs, sems(f)[5].at[0])
+            outs[f][1 - core] = theirs[...]
+            arrived(theirs, sems(f)[10].at[0])
+        for ref, sem in zip((in0, in1, in2, in3), sems(f)[6:10]):
+            arrived(ref, sem.at[0])
+
+
+def scatter_sums(parts, splits, depth):
+    chips = 4 * depth
+    outs, buffers, signals = [], [], []
+    dma = lambda n: pltpu.SemaphoreType.DMA((n,))
+    for p, split in zip(parts, splits):
+        chunk = p.shape[2:]
+        if split == "rows":
+            part = (chunk[0], chunk[1] // 2) + chunk[2:]
+        elif split == "blocks":
+            part = (chunk[0] // 2,) + chunk[1:]
+        else:
+            part = chunk
+        outs.append(jax.ShapeDtypeStruct(part if split is None else (2,) + part, F32))
+        for count in (chips, chips, chips // 2, depth, depth - 1):
+            buffers.append(pltpu.VMEM((count,) + chunk, p.dtype))
+        buffers += [pltpu.VMEM(chunk, F32), pltpu.VMEM(part, F32), dma(1)]
+        signals += [dma(chips), dma(chips), dma(chips // 2), dma(depth), dma(depth - 1)] + [dma(1)] * 6
     return pl.pallas_call(
-        fold_kernel,
-        grid_spec=pltpu.PrefetchScalarGridSpec(
-            num_scalar_prefetch=2, grid=(count,), in_specs=[sent, sent, kept, kept], out_specs=[out, out]
+        functools.partial(scatter_kernel, depth, tuple(splits)),
+        in_specs=[ANYWHERE] * len(parts),
+        out_specs=[pl.BlockSpec(memory_space=pltpu.VMEM)] * len(parts),
+        out_shape=outs,
+        scratch_shapes=buffers + signals,
+        compiler_params=pltpu.CompilerParams(
+            collective_id=1, has_side_effects=True, vmem_limit_bytes=VMEM_LIMIT
         ),
-        out_shape=[shape, shape],
-        cost_estimate=pl.CostEstimate(flops=0, bytes_accessed=3 * 2 * a.size, transcendentals=0),
-        name="fold_sums",
-    )(send_at, keep_at, a, b, a, b)
-
-
-def fold_places(moves):
-    z, y, x, c = here()
-    plane = jnp.arange(2 * moves.depth, dtype=jnp.int32)
-    deep, side = plane // 2, plane % 2
-    bit = jnp.where(c == 0, x, y)
-
-    def spread(b):
-        return jnp.where(c == 0, deep * 4 + side * 2 + b, deep * 4 + b * 2 + side).astype(jnp.int32)
-
-    level = jnp.arange(moves.depth, dtype=jnp.int32)
-    turn = (z + level) % moves.depth
-    mine = jnp.where(c == 0, y, x)
-    return (
-        (spread(1 - bit), spread(bit)),
-        ((turn * 2 + 1 - mine).astype(jnp.int32), (turn * 2 + mine).astype(jnp.int32)),
-    )
-
-
-def level_kernel(keep, got, first, *rest):
-    first[...] = keep[0].astype(F32) + got[0].astype(F32)
-    for k, out in enumerate(rest):
-        out[...] = (keep[k + 1].astype(F32) + got[k + 1].astype(F32)).astype(BF)
-
-
-def level(keep, got):
-    shape = keep.shape[1:]
-    outs = [jax.ShapeDtypeStruct(shape, F32)] + [jax.ShapeDtypeStruct(shape, BF)] * (keep.shape[0] - 1)
-    return pl.pallas_call(
-        level_kernel,
-        in_specs=[whole(keep.shape)] * 2,
-        out_specs=[whole(shape)] * keep.shape[0],
-        grid=(1,),
-        out_shape=outs,
-        compiler_params=params("arbitrary"),
-        cost_estimate=cost(0, 4 * keep.size),
-        name="level_sums",
-    )(keep, got)
-
-
-def scattered_small(sums, moves, places):
-    c = here()[3]
-    odd = c == 1
-    part = of_two(odd, sums[:, 0], sums[:, 1]) + swap(of_two(odd, sums[:, 1], sums[:, 0]), moves.core)
-    for (send_at, keep_at), move in zip(places, (moves.second, moves.first)):
-        part = jnp.take(part, keep_at, axis=0) + swap(jnp.take(part, send_at, axis=0), move)
-    total = part[0]
-    for k in range(1, moves.depth):
-        total = total + swap(part[k], moves.deep[k])
-    return total
-
-
-def halves(total, cores_axis, moves):
-    odd = here()[3] == 1
-    zero = lax.index_in_dim(total, 0, cores_axis, keepdims=False)
-    one = lax.index_in_dim(total, 1, cores_axis, keepdims=False)
-    mine = of_two(odd, zero, one)
-    got = swap(of_two(odd, one, zero), moves.core)
-    return jnp.stack([of_two(odd, mine, got), of_two(odd, got, mine)])
+        cost_estimate=cost(0, 3e7),
+        name="scatter_sums",
+    )(*parts)
 
 
 def by_neighbours(devices, width, hidden, count):
@@ -940,10 +962,7 @@
     d_mid = d_out + d_mid
     d_branch = d_mid.astype(BF)
     d_attn = mm_nt(d_branch, wo).astype(BF)
-    parts = [
-        attention_bwd(qkv, d_attn, attn_t, lse, *tables, jnp.full((1,), h, jnp.int32)) for h in range(2)
-    ]
-    d_qkv = jnp.concatenate(parts, axis=1)
+    d_qkv = attention_bwd(qkv, d_attn, attn_t, lse, *tables)
     _, pull = jax.vjp(norm, rows, g1, c1)
     d_rows, d_g1, d_c1 = pull(mm_nt(d_qkv, wqkv))
     input_grad = (d_mid + d_rows).astype(BF)
@@ -961,21 +980,21 @@
 
 def by_chips(tokens, cotangent, tables, masters):
     devices = lax.axis_size("fsdp")
-    moves = Moves(devices)
-    chips = moves.chips
+    chips = devices // 2
+    depth = devices // 8
     count, width = tokens.shape
     ln1_gain, ln1_shift, w_qkv, bias_q, bias_v, w_out, bias_out, ln2_gain, ln2_shift, w_up, bias_up, w_down, bias_down = masters
     part = width // devices
     two = 2 * part
     hidden = w_up.shape[1]
-    core = here()[3].astype(jnp.int32).reshape(1)
+    core = lax.rem(lax.axis_index("fsdp"), 2).astype(jnp.int32).reshape(1)
 
     small = jnp.concatenate([ln1_gain, ln1_shift, bias_q, bias_v, bias_out, ln2_gain, ln2_shift, bias_down, bias_up])
     small = jnp.pad(small[None], ((0, 7), (0, WIDE - small.shape[0])))
     own1, own2, own3, oth1, oth2, oth3 = pack(w_qkv, small, w_out, w_up, w_down, core)
 
     chunks1, chunks2, chunks3 = gather_shards(
-        (own1, own2, own3), (oth1, oth2, oth3), ([part] * 3 + [8], [part] * 5, [4 * part]), moves.depth
+        (own1, own2, own3), (oth1, oth2, oth3), ([part] * 3 + [8], [part] * 5, [4 * part]), depth
     )
     vecs = chunks1[0, :, 6 * part :: 8].reshape(devices, WIDE).astype(F32)
     g1, c1, bq, bv, bo, g2, c2, b2 = [vecs[:, i * part : (i + 1) * part].reshape(-1) for i in range(8)]
@@ -1002,75 +1021,29 @@
         attn, tokens, cotangent, jnp.stack([g2, c2, bo, b2]), b1, (chunks2, chunks3), (spots_up, spots_down)
     )
 
-    far, near = 1 - core, core
-    orders = fold_places(moves)
-    downs = lambda cot: [(cot, WIDE, True, act, hidden, False)]
-    ups = lambda n2: [(n2, width, False, d_pre, hidden // 2, True), (attn, width, False, d_branch, WIDE, True)]
-    qkvs = lambda n1, d: [(n1, width, False, d, 3 * WIDE, False)]
-    sent_down = grad_part(downs(cotangent), far, chips, "grad_down_far")
-    got_down = swap(sent_down, moves.core)
-    sent_up = grad_part(ups(gate(n2, sent_down)), far, chips, "grad_up_out_far")
-    got_up = swap(sent_up, moves.core)
-    send_down, keep_down = grad_part(
-        downs(gate(cotangent, sent_up)), near, chips, "grad_down_near", gate(got_down, sent_up), orders[0]
-    )
-    got_down = swap(send_down, moves.second)
-    send_up, keep_up = grad_part(
-        ups(gate(n2, send_down)), near, chips, "grad_up_out_near", gate(got_up, send_down), orders[0]
-    )
-    got_up = swap(send_up, moves.second)
-    d_qkv_far = attention_bwd(qkv, gate(d_attn, send_up), attn_t, lse, *tables, far)
-    send_down, keep_down = fold(keep_down, gate(got_down, d_qkv_far), *orders[1])
-    got_down = swap(send_down, moves.first)
-    send_up, keep_up = fold(keep_up, gate(got_up, d_qkv_far), *orders[1])
-    got_up = swap(send_up, moves.first)
-    sent_qkv = grad_part(qkvs(gate(n1, send_up, send_down), d_qkv_far), far, chips, "grad_qkv_far")
-    got_qkv = swap(sent_qkv, moves.core)
-    d_qkv_near = attention_bwd(qkv, gate(d_attn, sent_qkv), attn_t, lse, *tables, near)
-
-    def spread(others):
-        return [swap(x, moves.deep[k + 1]) for k, x in enumerate(others)]
-
-    def total_of(first, gots):
-        return sum((g.astype(F32) for g in gots), first)
-
-    first_down, *rest_down = level(keep_down, gate(got_down, d_qkv_near))
-    first_up, *rest_up = level(keep_up, gate(got_up, d_qkv_near))
-    gots_down, gots_up = spread(rest_down), spread(rest_up)
-    input_grad, sums1 = first_norm_back(
-        d_qkv_far, gate(d_qkv_near, first_down, first_up), wqkv, tokens, d_mid, g1[None], jnp.concatenate([far, near])
-    )
-    send_qkv, keep_qkv = grad_part(
-        qkvs(gate(n1, sums1), d_qkv_near), near, chips, "grad_qkv_near", gate(got_qkv, sums1), orders[0]
-    )
-    got_qkv = swap(send_qkv, moves.second)
-    first_down, *gots_down = lax.optimization_barrier((first_down, *gots_down, send_qkv))[:-1]
-    first_up, *gots_up = lax.optimization_barrier((first_up, *gots_up, send_qkv))[:-1]
-    send_qkv, keep_qkv = fold(keep_qkv, got_qkv, *orders[1])
-    got_qkv = swap(send_qkv, moves.first)
-
-    odd = core[0] == 1
-    by_half = [of_two(odd, sums1[3], sums1[2]), of_two(odd, sums1[2], sums1[3])]
-    d_bq = jnp.concatenate([s[:WIDE] for s in by_half])
-    d_bv = jnp.concatenate([s[2 * WIDE :] for s in by_half])
-    vecs = [sums1[0, :width], sums1[1, :width], d_bq, d_bv, sums2[2], sums2[0], sums2[1], sums2[3]]
+    g_parts = [
+        grad_part([(n2, d_pre), (attn, d_branch)], chips, two, "grad_up_out"),
+        grad_part([(act, cotangent)], chips, two, "grad_down"),
+    ]
+    d_qkv = attention_bwd(qkv, d_attn, attn_t, lse, *tables)
+    input_grad, sums1 = first_norm_back(d_qkv, wqkv, tokens, d_mid, g1[None])
+    g_parts.append(grad_part([(n1, d_qkv)], chips, two, "grad_qkv"))
+    by_half = sums1[2].reshape(2, 3, WIDE)
+    vecs = [
+        sums1[0, :width], sums1[1, :width], by_half[:, 0].reshape(-1), by_half[:, 2].reshape(-1),
+        sums2[2], sums2[0], sums2[1], sums2[3],
+    ]
     small = jnp.concatenate([v.reshape(devices, part) for v in vecs] + [sum_up.reshape(devices, 4 * part)], axis=1)
-    small = jnp.pad(small, ((0, 0), (0, WIDE - small.shape[1]))).reshape(chips, 2, WIDE)
-    small = scattered_small(small, moves, orders)
+    small = small.reshape(chips, 2, 1, -1).swapaxes(0, 1)
+    small = jnp.pad(small, ((0, 0), (0, 0), (0, 7), (0, WIDE - small.shape[3])))
+    small, g_up_out, g_down, g_qkv = scatter_sums([small] + g_parts, (None, "rows", "blocks", "rows"), depth)
+    small = small[0]
     s = [small[i * part : (i + 1) * part] for i in range(8)]
     s_b1 = small[8 * part : 12 * part]
-
-    total_down = total_of(first_down, gots_down)
-    both_halves = halves(total_down.reshape(2, 4 * part, WIDE), 0, moves)
-    g_down = both_halves.transpose(1, 0, 2).reshape(4 * part, width)
-    total_up = total_of(first_up, gots_up)
-    both_halves = halves(total_up.reshape(5, 2, part, WIDE), 1, moves)
-    g_up = both_halves[:, :4].transpose(2, 0, 1, 3).reshape(part, hidden)
-    g_out = both_halves[:, 4].transpose(1, 0, 2).reshape(part, width)
-    first_qkv, *rest_qkv = level(keep_qkv, got_qkv)
-    total_qkv = total_of(first_qkv, spread(rest_qkv))
-    both_halves = halves(total_qkv.reshape(3, 2, part, WIDE), 1, moves)
-    g_qkv = both_halves.transpose(2, 1, 0, 3).reshape(part, 3 * width)
+    g_up = g_up_out[:, :4].transpose(2, 0, 1, 3).reshape(part, hidden)
+    g_out = g_up_out[:, 4].transpose(1, 0, 2).reshape(part, width)
+    g_down = g_down.reshape(2, 4 * part, WIDE).transpose(1, 0, 2).reshape(4 * part, width)
+    g_qkv = g_qkv.transpose(2, 1, 0, 3).reshape(part, 3 * width)
     return (
         layer_out, input_grad, s[0], s[1], g_qkv, s[2], s[3], g_out, s[4], s[5], s[6], g_up, s_b1, g_down, s[7],
     )

time: 474 us -> 433 us (0.914)
  waiting for transfers between devices: 34.3 us -> 0 us
  starting transfers between devices: 31.8 us -> 0 us
  Pallas kernels: 369 us -> 400 us
    pallas_call x13 -> x5, Pallas kernels: 115 us -> 152 us  [the longest x1 86.3 us: scatter_sums(): pl.pallas_call(functools.partial(scatter_kernel, depth, tuple(splits)), i...]
    ppermute x27 -> x0, waiting for transfers between devices: 34.3 us -> none  [swap(): return lax.ppermute(x, 'fsdp', moves)]
    ppermute x27 -> x0, starting transfers between devices: 31.8 us -> none  [swap(): return lax.ppermute(x, 'fsdp', moves)]
    pallas_call x2 -> x1, Pallas kernels: 60.2 us -> 53.8 us  [attention_bwd(): pl.pallas_call(attn_bwd_kernel, grid_spec=pltpu.PrefetchScalarGridSpec(nu...]
  transfers between devices with their start and end apart: 27 -> 0, of which waited for: 12 -> 0; matrix products, arithmetic and copies ran while one was open for 2% -> 0% of each run, Pallas kernels for 28% -> 0%
where the time goes in v3:
time: 433 us; the launch traced here: 425 us
  Pallas kernels  400 us (92%)
  local copies, waits for them, and re-layouts  19.2 us (4%)
  other arithmetic  4.54 us (1%)
    pallas_call x1, Pallas kernels, scatter_sums(): pl.pallas_call(functools.partial(scatter_kernel, depth, tuple(splits)), i...  86.3 us
    pallas_call x1, Pallas kernels, gather_shards(): pl.pallas_call(functools.partial(gather_kernel, blocks, depth), in_specs=...  78.2 us
    pallas_call x1, Pallas kernels, middle_part(): pl.pallas_call(functools.partial(middle_kernel, spots), grid=(count // ro...  66.4 us
    pallas_call x1, Pallas kernels, attention_bwd(): pl.pallas_call(attn_bwd_kernel, grid_spec=pltpu.PrefetchScalarGridSpec(nu...  53.8 us
    pallas_call x3, Pallas kernels, grad_part(): pl.pallas_call(functools.partial(grad_kernel, tuple(layout)), grid=(token...  48.9 us
    pallas_call x1, Pallas kernels, attention_fwd(): pl.pallas_call(attn_fwd_kernel, grid_spec=pltpu.PrefetchScalarGridSpec(nu...  33.1 us
    pallas_call x1, Pallas kernels, first_norm_back(): pl.pallas_call(first_norm_kernel, grid=(count // TILE,), in_specs=[tile(c...  16.8 us
    pallas_call x1, Pallas kernels, project_qkv(): pl.pallas_call(functools.partial(qkv_kernel, spots), grid=(count // TILE,...  14.4 us

profile of v3, /device:TPU:0, one launch (start us, length us, event | category | flops | bytes accessed | tf_op | source)
XLA Modules:
  0.0 425.0 jit_solution(18065210540932925221)
XLA Ops:
  0.7 0.9 concatenate.28
  2.1 2.0 pack_shards.1
  4.1 78.2 %gather_shards.1 = (bf16[2,16,160,384]{3,2,1,0:T(8,128)(2,1)}, bf16[2,16,240,384]{3,2,1,0:T(8,128)(2,1)}, bf16[2,16,192,384]{3,2,1,0:T(8,128)(2,1)}) custom-call(bf16[80,384]{1,0:T(8,128)(2,1)} %get-tuple-element.45.refs_0_, bf16[120,384]{1,0:T(8,128)(2,1)} %get-tuple-element.46.refs_1_, bf16[96,384]{1,0:T(8,128)(2,1)} %get-tuple-element.47.refs_2_, ...), custom_call_target="tpu_custom_call" | custom-call | bytes 30000000 | tf_op jit(solution)/shard_map/gather_shards/pallas_call | solution.py:686
  82.4 1.0 slice.135
  83.9 0.6 pad_maximum_fusion.1.vec
  84.7 0.6 reshape.122.bias
  85.6 0.6 pad_maximum_fusion.2.vec
  86.2 14.4 %norm_and_qkv.1 = (bf16[2048,768]{1,0:T(8,128)(2,1)}, bf16[2048,2304]{1,0:T(8,128)(2,1)}, bf16[768,2304]{1,0:T(8,128)(2,1)}) custom-call(bf16[2048,768]{1,0:T(8,128)(2,1)} %tok.5, f32[2,768]{1,0:T(2,128)} %pad_maximum_fusion.2.vec, f32[1,2304]{1,0:T(1,128)} %reshape.122.bias, bf16[2,16,160,384]{3,2,1,0:T(8,128)(2,1)} %get-tuple-element.51.chunks), custom_call_target="tpu_custom_call" | custom-call | flops 7247757312 | bytes 20000000 | tf_op jit(solution)/shard_map/norm_and_qkv/pallas_call | solution.py:391
  101.6 0.6 fusion.2.mr_ref
  102.2 1.2 fusion.1.oh_ref
  103.4 33.1 %attention_forward.1 = (bf16[2048,768]{1,0:T(8,128)(2,1)}, f32[2,768,1024]{2,1,0:T(8,128)}, f32[2,2,6,1024]{3,2,1,0:T(8,128)}) custom-call(s32[2,8]{1,0:T(2,128)} %get-tuple-element.102.lo, s32[2,8]{1,0:T(2,128)} %get-tuple-element.101.hi, bf16[2048,2304]{1,0:T(8,128)(2,1)} %get-tuple-element.52.q_ref.k_ref.v_ref, ...), custom_call_target="tpu_custom_call" | custom-call | flops 24000000000 | bytes 20000000 | tf_op jit(solution)/shard_map/attention_forward/pallas_call | solution.py:265
  136.5 0.7 reshape.123.b1
  137.2 66.4 %middle.1 = (bf16[2048,768]{1,0:T(8,128)(2,1)}, bf16[2048,768]{1,0:T(8,128)(2,1)}, bf16[2048,3072]{1,0:T(8,128)(2,1)}, bf16[2048,3072]{1,0:T(8,128)(2,1)}, f32[2...) custom-call(bf16[2048,768]{1,0:T(8,128)(2,1)} %get-tuple-element.53., ...), custom_call_target="tpu_custom_call" | custom-call | flops 43486543872 | bytes 60000000 | tf_op jit(solution)/shard_map/middle/pallas_call | solution.py:468
  203.6 53.8 %attention_backward.1.d_qkv.refs_1_ = bf16[2048,2304]{1,0:T(8,128)(2,1)} custom-call(s32[2,8]{1,0:T(2,128)} %get-tuple-element.102.lo, s32[2,8]{1,0:T(2,128)} %get-tuple-element.101.hi, bf16[2048,2304]{1,0:T(8,128)(2,1)} %get-tuple-element.52.q_ref.k_ref.v_ref, bf16[2048,2304]{1,0:T(8,128)(2,1)} %get-tuple-element.52.q_ref.k_ref.v_ref, ...), custom_call_target="tpu_custom_call" | custom-call | flops 44000002048 | bytes 40000000 | tf_op jit(solution)/shard_map/attention_backward/pallas_call | solution.py:303
  257.4 12.8 %grad_qkv.1.refs_3_ = bf16[2,16,3,48,384]{4,3,2,1,0:T(8,128)(2,1)} custom-call(bf16[2048,768]{1,0:T(8,128)(2,1)} %get-tuple-element.70.refs_0_, bf16[2048,2304]{1,0:T(8,128)(2,1)} %attention_backward.1.d_qkv.refs_1_), custom_call_target="tpu_custom_call" | custom-call | flops 7247757312 | bytes 30000000 | tf_op jit(solution)/shard_map/grad_qkv/pallas_call | solution.py:561
  270.2 19.9 %grad_up_out.1.refs_1_ = bf16[2,16,5,48,384]{4,3,2,1,0:T(8,128)(2,1)} custom-call(bf16[2048,768]{1,0:T(8,128)(2,1)} %get-tuple-element.66.refs_0_, bf16[2048,3072]{1,0:T(8,128)(2,1)} %get-tuple-element.67.refs_1_, bf16[2048,768]{1,0:T(8,128)(2,1)} %get-tuple-element.53.attn.refs_2_, bf16[2048,768]{1,0:T(8,128)(2,1)} %get-tuple-element.68.refs_3_), custom_call_target="tpu_custom_call" | custom-call | flops 12079595520 | bytes 30000000 | tf_op jit(solution)/shard_map/grad_up_out/pallas_call | solution.py:561
  290.1 16.8 %first_norm_back.1 = (bf16[2048,768]{1,0:T(8,128)(2,1)}, f32[8,2304]{1,0:T(8,128)}) custom-call(bf16[2048,2304]{1,0:T(8,128)(2,1)} %attention_backward.1.d_qkv.refs_1_, bf16[768,2304]{1,0:T(8,128)(2,1)} %get-tuple-element.60.w, bf16[2048,768]{1,0:T(8,128)(2,1)} %tok.5, f32[2048,768]{1,0:T(8,128)} %get-tuple-element.61.d_mid, f32[1,768]{1,0:T(1,128)} %copy-done.2), custom_call_target="tpu_custom_call" | custom-call | flops 7247757312 | bytes 30000000 | tf_op jit(solution)/shard_map/first_norm_back/pallas_call | solution.py:506
  306.9 0.9 slice_reduce_fusion
  308.1 0.8 slice_reduce_fusion.7
  310.2 0.7 reduce.21
  311.5 0.8 pad.9.refs_0_
  312.2 16.3 %grad_down.1.refs_2_ = bf16[2,16,4,48,384]{4,3,2,1,0:T(8,128)(2,1)} custom-call(bf16[2048,3072]{1,0:T(8,128)(2,1)} %get-tuple-element.69.refs_0_, bf16[2048,768]{1,0:T(8,128)(2,1)} %refs_1_.1), custom_call_target="tpu_custom_call" | custom-call | flops 9663676416 | bytes 30000000 | tf_op jit(solution)/shard_map/grad_down/pallas_call | solution.py:561
  328.6 86.3 %scatter_sums.1 = (f32[8,384]{1,0:T(8,128)}, f32[2,5,24,384]{3,2,1,0:T(8,128)}, f32[2,2,48,384]{3,2,1,0:T(8,128)}, f32[2,3,24,384]{3,2,1,0:T(8,128)}) custom-call(f32[2,16,8,384]{3,2,1,0:T(8,128)} %pad.9.refs_0_, bf16[2,16,5,48,384]{4,3,2,1,0:T(8,128)(2,1)} %grad_up_out.1.refs_1_, bf16[2,16,4,48,384]{4,3,2,1,0:T(8,128)(2,1)} %grad_down.1.refs_2_, ...), custom_call_target="tpu_custom_call" | custom-call | bytes 30000000 | tf_op jit(solution)/shard_map/scatter_sums/pallas_call | solution.py:901
  414.9 1.0 slice_bitcast_fusion
  416.0 0.8 reshape.126
  416.8 1.0 copy.56
  417.9 0.9 reshape.124
  418.7 1.7 copy.61
  420.4 0.9 slice_bitcast_fusion.1
  421.3 0.6 copy.60
  421.9 1.5 slice_bitcast_fusion.2
  423.5 1.3 slice_bitcast_fusion.3
  (56 shorter events, 4.6 us)
Async XLA Ops:
  85.5 15.1 %copy-start.2 = (f32[1,768]{1,0:T(1,128)}, f32[1,768]{1,0:T(1,128)S(1)}, u32[]{:S(2)}) copy-start(f32[1,768]{1,0:T(1,128)S(1)} %stack_reshape.18.vec) | copy-start | bytes 9220
  86.2 14.4 %copy-start = (s32[2048]{0:T(1024)S(1)}, s32[2048]{0:T(1024)}, u32[]{:S(2)}) copy-start(s32[2048]{0:T(1024)} %param.17) | copy-start | bytes 24580
  290.1 19.1 %copy-start.3 = (f32[8,768]{1,0:T(8,128)S(1)}, f32[8,768]{1,0:T(8,128)}, u32[]{:S(2)}) copy-start(f32[8,768]{1,0:T(8,128)} %get-tuple-element.64) | copy-start | bytes 73732
  290.1 20.2 %copy-start.1 = (f32[1,3072]{1,0:T(1,128)S(1)}, f32[1,3072]{1,0:T(1,128)}, u32[]{:S(2)}) copy-start(f32[1,3072]{1,0:T(1,128)} %get-tuple-element.65) | copy-start | bytes 36868

commit v4 on v3

--- a/solution.py
+++ b/solution.py
@@ -664,10 +664,12 @@
             arrived(outs[f].at[core, last[k]], sems[10 * f + 2].at[k])
             onward(f, k, last[k], 0)
 
-    for step in range(flows + 2):
-        for stage, run in enumerate((from_far, from_near, from_cross)):
-            if 0 <= step - stage < flows:
-                run(step - stage)
+    for f in range(flows):
+        from_far(f)
+        from_near(f)
+        if f > 0:
+            from_cross(f - 1)
+    from_cross(flows - 1)
     for f in range(flows):
         chips = outs[f].shape[1]
         arrived(outs[f].at[1 - core], sems[10 * f + 7].at[0])
@@ -734,7 +736,34 @@
 
 def scatter_kernel(depth, splits, *refs):
     flows = len(splits)
-    ins, outs, rest = refs[:flows], refs[flows : 2 * flows], refs[2 * flows :]
+    ready = flows - 2
+    ins, (act, cot, n1, d_qkv) = refs[:ready], refs[ready : ready + 4]
+    outs, rest = refs[ready + 4 : ready + 4 + flows], refs[ready + 4 + flows :]
+    (down, thirds, held, slots, held_sem, slot_sem), rest = rest[:6], rest[6:]
+    ins = list(ins) + [down, thirds]
+    width = cot.shape[1]
+    tall = act.shape[1] // width
+    tasks = tall + d_qkv.shape[1] // width
+
+    def held_copy(k):
+        return pltpu.make_async_copy((cot, n1)[k], held.at[k], held_sem.at[k])
+
+    def fetch_task(t):
+        slot = lax.rem(t, 2)
+
+        @pl.when(t < tall)
+        def _():
+            cols = pl.ds(pl.multiple_of(t * width, 128), width)
+            pltpu.make_async_copy(act.at[:, cols], slots.at[slot], slot_sem.at[slot]).start()
+
+        @pl.when(t >= tall)
+        def _():
+            cols = pl.ds(pl.multiple_of((t - tall) * width, 128), width)
+            pltpu.make_async_copy(d_qkv.at[:, cols], slots.at[slot], slot_sem.at[slot]).start()
+
+    for k in range(2):
+        held_copy(k).start()
+        fetch_task(jnp.int32(k))
     me, core, z, first, second = neighbours()
     chip = me // 2
     x, y = lax.rem(chip, 2), lax.rem(chip // 2, 2)
@@ -863,14 +892,72 @@
             outs[f][core] = mine(f, total, core)[...]
             remote(mine(f, total, 1 - core), theirs, sems(f)[10].at[0], sems(f)[5].at[0], twin).start()
 
-    for f in range(flows):
+    def multiply(t):
+        slot = lax.rem(t, 2)
+        pltpu.make_async_copy(slots.at[slot], slots.at[slot], slot_sem.at[slot]).wait()
+
+        @pl.when(t < tall)
+        def _():
+            low = tn(slots[slot], held[0]).astype(BF)
+            count = down.shape[1] // tall
+            for h in range(2):
+                part = low[:, h * WIDE : (h + 1) * WIDE].reshape((count,) + down.shape[2:])
+                down[h, pl.ds(t * count, count)] = part
+
+        @pl.when(t >= tall)
+        def _():
+            low = tn(held[1], slots[slot]).astype(BF)
+            for i in range(2):
+                block = 2 * (t - tall) + i
+                part = low[:, i * WIDE : (i + 1) * WIDE].reshape(thirds.shape[1], thirds.shape[3], WIDE)
+                thirds[block // 3, :, lax.rem(block, 3)] = part
+
+        @pl.when(t + 2 < tasks)
+        def _():
+            fetch_task(t + 2)
+
+    up, out, small, low, last = range(flows)
+    for f in range(ready):
         begin(f)
-    for f in range(flows):
-        across(f)
-    for step in range(flows + 2):
-        for stage, run in enumerate((along, upward, finish)):
-            if 0 <= step - stage < flows:
-                run(step - stage)
+    for k in range(2):
+        held_copy(k).wait()
+
+    def task(t):
+        multiply(t)
+
+        @pl.when(t == 0)
+        def _():
+            across(up)
+
+        @pl.when(t == 1)
+        def _():
+            across(out)
+            across(small)
+
+        @pl.when(t == tall)
+        def _():
+            begin(low)
+
+        @pl.when(t == tall + 1)
+        def _():
+            across(low)
+            along(up)
+
+    loop(tasks, task)
+    along(out)
+    along(small)
+    begin(last)
+    upward(up)
+    across(last)
+    upward(out)
+    upward(small)
+    along(low)
+    upward(low)
+    along(last)
+    for f in range(ready + 1):
+        finish(f)
+    upward(last)
+    finish(last)
     for f in range(flows):
         _, in0, in1, in2, in3, total, theirs, _ = flow(f)
         if splits[f] is not None:
@@ -881,12 +968,17 @@
             arrived(ref, sem.at[0])
 
 
-def scatter_sums(parts, splits, depth):
+def scatter_sums(parts, act, cot, n1, d_qkv, splits, depth):
     chips = 4 * depth
+    tokens, width = cot.shape
+    rows = width // chips
     outs, buffers, signals = [], [], []
     dma = lambda n: pltpu.SemaphoreType.DMA((n,))
-    for p, split in zip(parts, splits):
-        chunk = p.shape[2:]
+    shapes = [(2, chips, 4, rows, WIDE), (2, chips, 3, rows, WIDE)]
+    work = [pltpu.VMEM(x, BF) for x in shapes]
+    work += [pltpu.VMEM((2, tokens, width), BF), pltpu.VMEM((2, tokens, width), BF), dma(2), dma(2)]
+    kinds = [(p.shape[2:], p.dtype) for p in parts] + [(x[2:], BF) for x in shapes]
+    for (chunk, kind), split in zip(kinds, splits):
         if split == "rows":
             part = (chunk[0], chunk[1] // 2) + chunk[2:]
         elif split == "blocks":
@@ -895,21 +987,21 @@
             part = chunk
         outs.append(jax.ShapeDtypeStruct(part if split is None else (2,) + part, F32))
         for count in (chips, chips, chips // 2, depth, depth - 1):
-            buffers.append(pltpu.VMEM((count,) + chunk, p.dtype))
+            buffers.append(pltpu.VMEM((count,) + chunk, kind))
         buffers += [pltpu.VMEM(chunk, F32), pltpu.VMEM(part, F32), dma(1)]
         signals += [dma(chips), dma(chips), dma(chips // 2), dma(depth), dma(depth - 1)] + [dma(1)] * 6
     return pl.pallas_call(
         functools.partial(scatter_kernel, depth, tuple(splits)),
-        in_specs=[ANYWHERE] * len(parts),
-        out_specs=[pl.BlockSpec(memory_space=pltpu.VMEM)] * len(parts),
+        in_specs=[ANYWHERE] * (len(parts) + 4),
+        out_specs=[pl.BlockSpec(memory_space=pltpu.VMEM)] * len(outs),
         out_shape=outs,
-        scratch_shapes=buffers + signals,
+        scratch_shapes=work + buffers + signals,
         compiler_params=pltpu.CompilerParams(
             collective_id=1, has_side_effects=True, vmem_limit_bytes=VMEM_LIMIT
         ),
         cost_estimate=cost(0, 3e7),
         name="scatter_sums",
-    )(*parts)
+    )(*parts, act, cot, n1, d_qkv)
 
 
 def by_neighbours(devices, width, hidden, count):
@@ -1021,13 +1113,10 @@
         attn, tokens, cotangent, jnp.stack([g2, c2, bo, b2]), b1, (chunks2, chunks3), (spots_up, spots_down)
     )
 
-    g_parts = [
-        grad_part([(n2, d_pre), (attn, d_branch)], chips, two, "grad_up_out"),
-        grad_part([(act, cotangent)], chips, two, "grad_down"),
-    ]
+    g_up = grad_part([(n2, d_pre)], chips, two, "grad_up")
+    g_out = grad_part([(attn, d_branch)], chips, two, "grad_out")
     d_qkv = attention_bwd(qkv, d_attn, attn_t, lse, *tables)
     input_grad, sums1 = first_norm_back(d_qkv, wqkv, tokens, d_mid, g1[None])
-    g_parts.append(grad_part([(n1, d_qkv)], chips, two, "grad_qkv"))
     by_half = sums1[2].reshape(2, 3, WIDE)
     vecs = [
         sums1[0, :width], sums1[1, :width], by_half[:, 0].reshape(-1), by_half[:, 2].reshape(-1),
@@ -1036,12 +1125,14 @@
     small = jnp.concatenate([v.reshape(devices, part) for v in vecs] + [sum_up.reshape(devices, 4 * part)], axis=1)
     small = small.reshape(chips, 2, 1, -1).swapaxes(0, 1)
     small = jnp.pad(small, ((0, 0), (0, 0), (0, 7), (0, WIDE - small.shape[3])))
-    small, g_up_out, g_down, g_qkv = scatter_sums([small] + g_parts, (None, "rows", "blocks", "rows"), depth)
+    g_up, g_out, small, g_down, g_qkv = scatter_sums(
+        [g_up, g_out, small], act, cotangent, n1, d_qkv, ("rows", "rows", None, "blocks", "rows"), depth
+    )
     small = small[0]
     s = [small[i * part : (i + 1) * part] for i in range(8)]
     s_b1 = small[8 * part : 12 * part]
-    g_up = g_up_out[:, :4].transpose(2, 0, 1, 3).reshape(part, hidden)
-    g_out = g_up_out[:, 4].transpose(1, 0, 2).reshape(part, width)
+    g_up = g_up.transpose(2, 0, 1, 3).reshape(part, hidden)
+    g_out = g_out[:, 0].transpose(1, 0, 2).reshape(part, width)
     g_down = g_down.reshape(2, 4 * part, WIDE).transpose(1, 0, 2).reshape(4 * part, width)
     g_qkv = g_qkv.transpose(2, 1, 0, 3).reshape(part, 3 * width)
     return (

time: 433 us -> 404 us (0.933)
  Pallas kernels: 400 us -> 372 us
    pallas_call x3 -> x2, Pallas kernels: 48.9 us -> 22.7 us  [grad_part(): pl.pallas_call(functools.partial(grad_kernel, tuple(layout)), grid=(token...]
where the time goes in v4:
time: 404 us; the launch traced here: 397 us
  Pallas kernels  372 us (92%)
  local copies, waits for them, and re-layouts  19.2 us (5%)
  other arithmetic  4.56 us (1%)
    pallas_call x1, Pallas kernels, scatter_sums(): pl.pallas_call(functools.partial(scatter_kernel, depth, tuple(splits)), i...  89.9 us
    pallas_call x1, Pallas kernels, gather_shards(): pl.pallas_call(functools.partial(gather_kernel, blocks, depth), in_specs=...  74 us
    pallas_call x1, Pallas kernels, middle_part(): pl.pallas_call(functools.partial(middle_kernel, spots), grid=(count // ro...  66.3 us
    pallas_call x1, Pallas kernels, attention_bwd(): pl.pallas_call(attn_bwd_kernel, grid_spec=pltpu.PrefetchScalarGridSpec(nu...  53.7 us
    pallas_call x1, Pallas kernels, attention_fwd(): pl.pallas_call(attn_fwd_kernel, grid_spec=pltpu.PrefetchScalarGridSpec(nu...  31.7 us
    pallas_call x2, Pallas kernels, grad_part(): pl.pallas_call(functools.partial(grad_kernel, tuple(layout)), grid=(token...  22.7 us
    pallas_call x1, Pallas kernels, first_norm_back(): pl.pallas_call(first_norm_kernel, grid=(count // TILE,), in_specs=[tile(c...  17 us
    pallas_call x1, Pallas kernels, project_qkv(): pl.pallas_call(functools.partial(qkv_kernel, spots), grid=(count // TILE,...  14.4 us

profile of v4, /device:TPU:0, one launch (start us, length us, event | category | flops | bytes accessed | tf_op | source)
XLA Modules:
  0.0 397.0 jit_solution(7968463331658842325)
XLA Ops:
  0.7 0.9 concatenate.28
  1.5 0.6 pad.8.refs_1_
  2.1 2.0 pack_shards.1
  4.1 74.0 %gather_shards.1 = (bf16[2,16,160,384]{3,2,1,0:T(8,128)(2,1)}, bf16[2,16,240,384]{3,2,1,0:T(8,128)(2,1)}, bf16[2,16,192,384]{3,2,1,0:T(8,128)(2,1)}) custom-call(bf16[80,384]{1,0:T(8,128)(2,1)} %get-tuple-element.46.refs_0_, bf16[120,384]{1,0:T(8,128)(2,1)} %get-tuple-element.47.refs_1_, bf16[96,384]{1,0:T(8,128)(2,1)} %get-tuple-element.48.refs_2_, ...), custom_call_target="tpu_custom_call" | custom-call | bytes 30000000 | tf_op jit(solution)/shard_map/gather_shards/pallas_call | solution.py:688
  78.1 1.0 slice.129
  79.6 0.6 pad_maximum_fusion.1.vec
  80.5 0.6 reshape.122.bias
  81.3 0.6 pad_maximum_fusion.2.vec
  81.9 14.4 %norm_and_qkv.1 = (bf16[2048,768]{1,0:T(8,128)(2,1)}, bf16[2048,2304]{1,0:T(8,128)(2,1)}, bf16[768,2304]{1,0:T(8,128)(2,1)}) custom-call(bf16[2048,768]{1,0:T(8,128)(2,1)} %tok.5, f32[2,768]{1,0:T(2,128)} %pad_maximum_fusion.2.vec, f32[1,2304]{1,0:T(1,128)} %reshape.122.bias, bf16[2,16,160,384]{3,2,1,0:T(8,128)(2,1)} %get-tuple-element.52.chunks), custom_call_target="tpu_custom_call" | custom-call | flops 7247757312 | bytes 20000000 | tf_op jit(solution)/shard_map/norm_and_qkv/pallas_call | solution.py:391
  96.8 0.6 and_select_fusion
  97.4 0.6 fusion.2.mr_ref
  98.1 1.2 fusion.1.oh_ref
  99.2 31.7 %attention_forward.1 = (bf16[2048,768]{1,0:T(8,128)(2,1)}, f32[2,768,1024]{2,1,0:T(8,128)}, f32[2,2,6,1024]{3,2,1,0:T(8,128)}) custom-call(s32[2,8]{1,0:T(2,128)} %get-tuple-element.104.lo, s32[2,8]{1,0:T(2,128)} %get-tuple-element.103.hi, bf16[2048,2304]{1,0:T(8,128)(2,1)} %get-tuple-element.53.q_ref.k_ref.v_ref, ...), custom_call_target="tpu_custom_call" | custom-call | flops 24000000000 | bytes 20000000 | tf_op jit(solution)/shard_map/attention_forward/pallas_call | solution.py:265
  131.0 0.7 reshape.123.b1
  131.7 66.3 %middle.1 = (bf16[2048,768]{1,0:T(8,128)(2,1)}, bf16[2048,768]{1,0:T(8,128)(2,1)}, bf16[2048,3072]{1,0:T(8,128)(2,1)}, bf16[2048,3072]{1,0:T(8,128)(2,1)}, f32[2...) custom-call(bf16[2048,768]{1,0:T(8,128)(2,1)} %get-tuple-element.54., ...), custom_call_target="tpu_custom_call" | custom-call | flops 43486543872 | bytes 60000000 | tf_op jit(solution)/shard_map/middle/pallas_call | solution.py:468
  197.9 53.7 %attention_backward.1.d_qkv.refs_6_ = bf16[2048,2304]{1,0:T(8,128)(2,1)} custom-call(s32[2,8]{1,0:T(2,128)} %get-tuple-element.104.lo, s32[2,8]{1,0:T(2,128)} %get-tuple-element.103.hi, bf16[2048,2304]{1,0:T(8,128)(2,1)} %get-tuple-element.53.q_ref.k_ref.v_ref, bf16[2048,2304]{1,0:T(8,128)(2,1)} %get-tuple-element.53.q_ref.k_ref.v_ref, ...), custom_call_target="tpu_custom_call" | custom-call | flops 44000002048 | bytes 40000000 | tf_op jit(solution)/shard_map/attention_backward/pallas_call | solution.py:303
  251.7 17.0 %first_norm_back.1 = (bf16[2048,768]{1,0:T(8,128)(2,1)}, f32[8,2304]{1,0:T(8,128)}) custom-call(bf16[2048,2304]{1,0:T(8,128)(2,1)} %attention_backward.1.d_qkv.refs_6_, bf16[768,2304]{1,0:T(8,128)(2,1)} %get-tuple-element.61.w, bf16[2048,768]{1,0:T(8,128)(2,1)} %tok.5, f32[2048,768]{1,0:T(8,128)} %get-tuple-element.62.d_mid, f32[1,768]{1,0:T(1,128)} %copy-done.2), custom_call_target="tpu_custom_call" | custom-call | flops 7247757312 | bytes 30000000 | tf_op jit(solution)/shard_map/first_norm_back/pallas_call | solution.py:506
  268.7 0.9 slice_reduce_fusion
  269.9 0.8 slice_reduce_fusion.7
  272.1 0.7 reduce.21
  273.3 0.8 pad.9.refs_2_
  274.1 6.7 %grad_out.1.refs_1_ = bf16[2,16,1,48,384]{4,3,2,1,0:T(8,128)(2,1)} custom-call(bf16[2048,768]{1,0:T(8,128)(2,1)} %get-tuple-element.54.attn.refs_0_, bf16[2048,768]{1,0:T(8,128)(2,1)} %get-tuple-element.66.refs_1_), custom_call_target="tpu_custom_call" | custom-call | flops 2415919104 | bytes 30000000 | tf_op jit(solution)/shard_map/grad_out/pallas_call | solution.py:561
  280.8 16.1 %grad_up.1.refs_0_ = bf16[2,16,4,48,384]{4,3,2,1,0:T(8,128)(2,1)} custom-call(bf16[2048,768]{1,0:T(8,128)(2,1)} %get-tuple-element.64.refs_0_, bf16[2048,3072]{1,0:T(8,128)(2,1)} %get-tuple-element.65.refs_1_), custom_call_target="tpu_custom_call" | custom-call | flops 9663676416 | bytes 30000000 | tf_op jit(solution)/shard_map/grad_up/pallas_call | solution.py:561
  296.8 89.9 %scatter_sums.1 = (f32[2,4,24,384]{3,2,1,0:T(8,128)}, f32[2,1,24,384]{3,2,1,0:T(8,128)}, f32[8,384]{1,0:T(8,128)}, f32[2,2,48,384]{3,2,1,0:T(8,128)}, f32[2,3,24,384]{3,2,1,0:T(8,128)}) custom-call(bf16[2,16,4,48,384]{4,3,2,1,0:T(8,128)(2,1)} %grad_up.1.refs_0_, bf16[2,16,1,48,384]{4,3,2,1,0:T(8,128)(2,1)} %grad_out.1.refs_1_, ...), custom_call_target="tpu_custom_call" | custom-call | bytes 30000000 | tf_op jit(solution)/shard_map/scatter_sums/pallas_call | solution.py:993
  386.8 1.0 copy.58
  387.8 0.8 reshape.126
  388.6 1.0 copy.56
  389.7 0.9 reshape.124
  390.5 1.7 copy.61
  392.2 1.5 copy.60
  393.8 1.5 slice_bitcast_fusion
  395.3 1.3 slice_bitcast_fusion.1
  (53 shorter events, 3.4 us)
Async XLA Ops:
  81.2 15.1 %copy-start.2 = (f32[1,768]{1,0:T(1,128)}, f32[1,768]{1,0:T(1,128)S(1)}, u32[]{:S(2)}) copy-start(f32[1,768]{1,0:T(1,128)S(1)} %stack_reshape.18.vec) | copy-start | bytes 9220
  81.9 14.4 %copy-start = (s32[2048]{0:T(1024)S(1)}, s32[2048]{0:T(1024)}, u32[]{:S(2)}) copy-start(s32[2048]{0:T(1024)} %param.17) | copy-start | bytes 24580
  251.7 19.4 %copy-start.3 = (f32[8,768]{1,0:T(8,128)S(1)}, f32[8,768]{1,0:T(8,128)}, u32[]{:S(2)}) copy-start(f32[8,768]{1,0:T(8,128)} %get-tuple-element.68) | copy-start | bytes 73732
  251.7 20.4 %copy-start.1 = (f32[1,3072]{1,0:T(1,128)S(1)}, f32[1,3072]{1,0:T(1,128)}, u32[]{:S(2)}) copy-start(f32[1,3072]{1,0:T(1,128)} %get-tuple-element.69) | copy-start | bytes 36868

commit v5 on v4

--- a/solution.py
+++ b/solution.py
@@ -368,43 +368,7 @@
     pltpu.make_async_copy(out, out, sem).wait()
 
 
-def qkv_kernel(spots, tok, vec, bias, chunks, n1, qkv, w, sem):
-    @pl.when(pl.program_id(0) == 0)
-    def _():
-        fetch(chunks, spots, [w], sem)
-
-    xhat, _ = normalized(tok[...].astype(F32))
-    n = (xhat * vec[0:1] + vec[1:2]).astype(BF)
-    n1[...] = n
-
-    @pl.when(pl.program_id(0) == 0)
-    def _():
-        fetched(w, sem.at[0])
-
-    qkv[...] = (mm(n, w[...]) + bias[...]).astype(BF)
-
-
-def project_qkv(tokens, vec, bias, chunks, spots):
-    count, width = tokens.shape
-    cols = 3 * width
-    tile = lambda w: pl.BlockSpec((TILE, w), lambda i: (i, 0))
-    return pl.pallas_call(
-        functools.partial(qkv_kernel, spots),
-        grid=(count // TILE,),
-        in_specs=[tile(width), whole(vec.shape), whole(bias.shape), ANYWHERE],
-        out_specs=[tile(width), tile(cols), whole((width, cols))],
-        scratch_shapes=[pltpu.SemaphoreType.DMA((1,))],
-        out_shape=[
-            jax.ShapeDtypeStruct((count, width), BF),
-            jax.ShapeDtypeStruct((count, cols), BF),
-            jax.ShapeDtypeStruct((width, cols), BF),
-        ],
-        compiler_params=params("arbitrary"),
-        cost_estimate=cost(2 * count * width * cols, 2e7),
-        name="norm_and_qkv",
-    )(tokens, vec, bias, chunks)
-
-
+GAIN1, SHIFT1, BIAS_Q, BIAS_V, BIAS_OUT, GAIN2, SHIFT2, BIAS_DOWN = range(8)
 STRIP = 768
 CURVE = 0.7978845608028654
 CUBIC = 0.044715
@@ -423,12 +387,12 @@
         for k, ref in enumerate((wo, w1, w2)):
             fetched(ref, sem.at[k])
 
-    x = tok[...].astype(F32) + mm(attn[...], wo[...]) + vec[2:3]
+    x = tok[...].astype(F32) + mm(attn[...], wo[...]) + vec[BIAS_OUT : BIAS_OUT + 1]
     xhat, scale = normalized(x)
-    n = (xhat * vec[0:1] + vec[1:2]).astype(BF)
+    n = (xhat * vec[GAIN2 : GAIN2 + 1] + vec[SHIFT2 : SHIFT2 + 1]).astype(BF)
     n2[...] = n
     d_out = cot[...]
-    y = x + vec[3:4]
+    y = x + vec[BIAS_DOWN : BIAS_DOWN + 1]
     d_n2 = None
     for j in range(w1.shape[1] // STRIP):
         cols = slice(j * STRIP, (j + 1) * STRIP)
@@ -451,7 +415,7 @@
     add_row(sums, 1, d_n2)
     g = d_out.astype(F32)
     add_row(sums, 3, g)
-    d = g + norm_back(d_n2, xhat, scale, vec[0:1])
+    d = g + norm_back(d_n2, xhat, scale, vec[GAIN2 : GAIN2 + 1])
     d_mid[...] = d
     low = d.astype(BF)
     d_branch[...] = low
@@ -519,58 +483,6 @@
     return lax.dot_general(a, b, (((0,), (0,)), ((), ())), preferred_element_type=F32)
 
 
-def grad_kernel(layout, *refs):
-    count = len(layout)
-    ins, out, sums = refs[: 2 * count], refs[2 * count], refs[2 * count + 1 :]
-    step = pl.program_id(0)
-
-    @pl.when(step == 0)
-    def _():
-        for acc in sums:
-            acc[...] = jnp.zeros_like(acc)
-
-    for k in range(count):
-        sums[k][...] += tn(ins[2 * k][...], ins[2 * k + 1][...])
-
-    @pl.when(step == pl.num_programs(0) - 1)
-    def _():
-        _, chips, _, rows, _ = out.shape
-        base = 0
-        for k, blocks in enumerate(layout):
-            tall = sums[k].shape[0] // (chips * rows)
-            for h in range(2):
-                for b in range(blocks):
-                    at = (h * blocks + b) * WIDE
-                    low = sums[k][:, at : at + WIDE].astype(BF)
-                    out[h, :, base + b * tall : base + (b + 1) * tall] = low.reshape(chips, tall, rows, WIDE)
-            base += blocks * tall
-
-
-def grad_part(pairs, chips, rows, name):
-    tokens = pairs[0][0].shape[0]
-    specs, arrays, scratch, layout, flops, total = [], [], [], [], 0, 0
-    for lhs, rhs in pairs:
-        for x in (lhs, rhs):
-            specs.append(pl.BlockSpec((TILE, x.shape[1]), lambda i: (i, 0)))
-            arrays.append(x)
-        scratch.append(pltpu.VMEM((lhs.shape[1], rhs.shape[1]), F32))
-        layout.append(rhs.shape[1] // (2 * WIDE))
-        total += layout[-1] * (lhs.shape[1] // (chips * rows))
-        flops += 2 * tokens * lhs.shape[1] * rhs.shape[1]
-    shape = (2, chips, total, rows, WIDE)
-    return pl.pallas_call(
-        functools.partial(grad_kernel, tuple(layout)),
-        grid=(tokens // TILE,),
-        in_specs=specs,
-        out_specs=whole(shape),
-        out_shape=jax.ShapeDtypeStruct(shape, BF),
-        scratch_shapes=scratch,
-        compiler_params=params("arbitrary"),
-        cost_estimate=cost(flops, 3e7),
-        name=name,
-    )(*arrays)
-
-
 def neighbours():
     me = lax.axis_index("fsdp")
     core = lax.rem(me, 2)
@@ -590,10 +502,32 @@
     pl.semaphore_wait(barrier, len(others))
 
 
-def gather_kernel(blocks, depth, *refs):
+def gathered_vectors(rows, vecs, wide):
+    width = vecs.shape[1]
+    devices = rows.shape[0] // 8
+    part = width // devices
+    source = lax.broadcasted_iota(jnp.int32, (WIDE, width), 0)
+    owner = lax.broadcasted_iota(jnp.int32, (rows.shape[0], width), 0)
+
+    def spread(first, size, lane):
+        lanes = lane * width + lax.broadcasted_iota(jnp.int32, (1, width), 1)
+        device = lanes // size
+        pick = (source == first + lanes - device * size).astype(F32).astype(BF)
+        return jnp.sum(jnp.where(owner == 8 * device, mm(rows, pick), 0.0), axis=0, keepdims=True)
+
+    for v in range(8):
+        vecs[v : v + 1, :] = spread(v * part, part, 0)
+    for b in range(4):
+        wide[:, b * width : (b + 1) * width] = spread(8 * part, 4 * part, b)
+
+
+def gather_kernel(blocks, depth, spots, *refs):
     flows = len(blocks)
-    owns, oths, outs = refs[:flows], refs[flows : 2 * flows], refs[2 * flows : 3 * flows]
-    sems = refs[3 * flows :]
+    owns, oths, tok_in, refs = refs[:flows], refs[flows : 2 * flows], refs[2 * flows], refs[2 * flows + 1 :]
+    outs, (n1_out, qkv_out, w_out, vecs, wide), refs = refs[:flows], refs[flows : flows + 5], refs[flows + 5 :]
+    (tok, w, rows, n1, qkv, load_sem, rows_sem, w_sem, put_sem), sems = refs[:9], refs[9:]
+    tok_load = pltpu.make_async_copy(tok_in, tok, load_sem.at[0])
+    tok_load.start()
     me, core, z, first, second = neighbours()
     twin = me + 1 - 2 * core
     chip = me // 2
@@ -664,37 +598,116 @@
             arrived(outs[f].at[core, last[k]], sems[10 * f + 2].at[k])
             onward(f, k, last[k], 0)
 
-    for f in range(flows):
-        from_far(f)
-        from_near(f)
-        if f > 0:
-            from_cross(f - 1)
-    from_cross(flows - 1)
+    def from_twin(f):
+        arrived(outs[f].at[1 - core], sems[10 * f + 7].at[0])
+
+    tile = n1.shape[1]
+    tiles = tok.shape[0] // tile
+
+    def put(i):
+        slot, span = lax.rem(i, 2), pl.ds(pl.multiple_of(i * tile, tile), tile)
+        return (
+            pltpu.make_async_copy(n1.at[slot], n1_out.at[span, :], put_sem.at[slot]),
+            pltpu.make_async_copy(qkv.at[slot], qkv_out.at[span, :], put_sem.at[2 + slot]),
+        )
+
+    def project(i):
+        @pl.when(i >= 2)
+        def _():
+            for copy in put(i - 2):
+                copy.wait()
+
+        slot = lax.rem(i, 2)
+        x = tok[pl.ds(pl.multiple_of(i * tile, tile), tile), :].astype(F32)
+        n = (normalized(x)[0] * vecs[GAIN1 : GAIN1 + 1, :] + vecs[SHIFT1 : SHIFT1 + 1, :]).astype(BF)
+        n1[slot] = n
+        bias = []
+        for h in range(2):
+            cols = slice(h * WIDE, (h + 1) * WIDE)
+            q, v = vecs[BIAS_Q : BIAS_Q + 1, cols], vecs[BIAS_V : BIAS_V + 1, cols]
+            bias += [q, jnp.zeros_like(q), v]
+        qkv[slot] = (mm(n, w[...]) + jnp.concatenate(bias, axis=1)).astype(BF)
+        for copy in put(i):
+            copy.start()
+
+    def several(first, last):
+        def step(i, carry):
+            project(i)
+            return carry
+
+        lax.fori_loop(first, last, step, 0)
+
+    from_far(0)
+    from_near(0)
+    from_far(1)
+    from_near(1)
+    from_cross(0)
+    from_twin(0)
+    fetch(outs[0], spots, [w], w_sem)
+    chips = outs[0].shape[1]
+    first_row = outs[0].shape[2] - 16
+    for at in range(chips):
+        pltpu.make_async_copy(outs[0].at[0, at, pl.ds(first_row, 16), :], rows.at[pl.ds(16 * at, 16), :], rows_sem.at[0]).start()
+    from_far(2)
+    from_near(2)
+    arrived(rows, rows_sem.at[0])
+    gathered_vectors(rows[...], vecs, wide)
+    tok_load.wait()
+    fetched(w, w_sem.at[0])
+    w_put = pltpu.make_async_copy(w, w_out, load_sem.at[1])
+    w_put.start()
+    several(0, tiles // 2)
+    from_cross(1)
+    several(tiles // 2, tiles)
+    from_cross(2)
+    for i in (tiles - 2, tiles - 1):
+        for copy in put(jnp.int32(i)):
+            copy.wait()
+    w_put.wait()
     for f in range(flows):
         chips = outs[f].shape[1]
-        arrived(outs[f].at[1 - core], sems[10 * f + 7].at[0])
+        if f > 0:
+            from_twin(f)
         arrived(outs[f].at[0], sems[10 * f + 6].at[0])
         arrived(outs[f].at[0, pl.ds(0, chips - 1)], sems[10 * f + 5].at[0])
         arrived(oths[f], sems[10 * f + 8].at[0])
 
 
-def gather_shards(owns, oths, blocks, depth):
+def gather_shards(owns, oths, blocks, tokens, spots, depth):
     chips = 4 * depth
+    count, width = tokens.shape
+    tile = TILE // 2
     outs = [jax.ShapeDtypeStruct((2, chips, 2 * o.shape[0], WIDE), BF) for o in owns]
+    outs += [
+        jax.ShapeDtypeStruct((count, width), BF),
+        jax.ShapeDtypeStruct((count, 3 * width), BF),
+        jax.ShapeDtypeStruct((width, 3 * width), BF),
+        jax.ShapeDtypeStruct((8, width), F32),
+        jax.ShapeDtypeStruct((1, 4 * width), F32),
+    ]
     dma = lambda n: pltpu.SemaphoreType.DMA((n,))
-    scratch = []
+    scratch = [
+        pltpu.VMEM((count, width), BF),
+        pltpu.VMEM((width, 3 * width), BF),
+        pltpu.VMEM((16 * chips, WIDE), BF),
+        pltpu.VMEM((2, tile, width), BF),
+        pltpu.VMEM((2, tile, 3 * width), BF),
+        dma(2), dma(1), dma(1), dma(4),
+    ]
     for _ in owns:
         scratch += [dma(depth), dma(depth), dma(2 * depth)] + [dma(1)] * 7
     return pl.pallas_call(
-        functools.partial(gather_kernel, blocks, depth),
-        in_specs=[ANYWHERE] * (2 * len(owns)),
-        out_specs=[ANYWHERE] * len(owns),
+        functools.partial(gather_kernel, blocks, depth, spots),
+        in_specs=[ANYWHERE] * (2 * len(owns) + 1),
+        out_specs=[ANYWHERE] * (len(owns) + 3) + [pl.BlockSpec(memory_space=pltpu.VMEM)] * 2,
         out_shape=outs,
         scratch_shapes=scratch,
-        compiler_params=pltpu.CompilerParams(collective_id=0, has_side_effects=True),
-        cost_estimate=cost(0, 3e7),
-        name="gather_shards",
-    )(*owns, *oths)
+        compiler_params=pltpu.CompilerParams(
+            collective_id=0, has_side_effects=True, vmem_limit_bytes=VMEM_LIMIT
+        ),
+        cost_estimate=cost(6 * count * width * width, 3e7),
+        name="gather_and_qkv",
+    )(*owns, *oths, tokens)
 
 
 def pack_kernel(core, *refs):
@@ -736,35 +749,37 @@
 
 def scatter_kernel(depth, splits, *refs):
     flows = len(splits)
-    ready = flows - 2
-    ins, (act, cot, n1, d_qkv) = refs[:ready], refs[ready : ready + 4]
-    outs, rest = refs[ready + 4 : ready + 4 + flows], refs[ready + 4 + flows :]
-    (down, thirds, held, slots, held_sem, slot_sem), rest = rest[:6], rest[6:]
-    ins = list(ins) + [down, thirds]
+    small_in, act, cot, n2, d_pre, attn, d_branch, n1, d_qkv = refs[:9]
+    outs, rest = refs[9 : 9 + flows], refs[9 + flows :]
+    (down, up, out, thirds, held, slots, held_sem, slot_sem), rest = rest[:8], rest[8:]
+    ins = [small_in, down, up, out, thirds]
     width = cot.shape[1]
     tall = act.shape[1] // width
-    tasks = tall + d_qkv.shape[1] // width
+    ends = (tall, 2 * tall, 2 * tall + 1, 2 * tall + 1 + d_qkv.shape[1] // width)
+    me, core, z, first, second = neighbours()
 
     def held_copy(k):
-        return pltpu.make_async_copy((cot, n1)[k], held.at[k], held_sem.at[k])
+        return pltpu.make_async_copy((cot, n2, attn, n1)[k], held.at[k % 2], held_sem.at[k % 2])
+
+    def level(t):
+        return lax.rem(z + 1 + t, depth)
 
     def fetch_task(t):
         slot = lax.rem(t, 2)
-
-        @pl.when(t < tall)
-        def _():
-            cols = pl.ds(pl.multiple_of(t * width, 128), width)
-            pltpu.make_async_copy(act.at[:, cols], slots.at[slot], slot_sem.at[slot]).start()
-
-        @pl.when(t >= tall)
-        def _():
-            cols = pl.ds(pl.multiple_of((t - tall) * width, 128), width)
-            pltpu.make_async_copy(d_qkv.at[:, cols], slots.at[slot], slot_sem.at[slot]).start()
+        start = 0
+        for source, end in zip((act, d_pre, d_branch, d_qkv), ends):
+            block = level(t) if source is act else t - start
+
+            @pl.when((t >= start) & (t < end))
+            def _(source=source, block=block):
+                cols = pl.ds(pl.multiple_of(block * width, 128), width)
+                pltpu.make_async_copy(source.at[:, cols], slots.at[slot], slot_sem.at[slot]).start()
+
+            start = end
 
     for k in range(2):
         held_copy(k).start()
         fetch_task(jnp.int32(k))
-    me, core, z, first, second = neighbours()
     chip = me // 2
     x, y = lax.rem(chip, 2), lax.rem(chip // 2, 2)
     twin = me + 1 - 2 * core
@@ -806,7 +821,7 @@
 
         lax.fori_loop(0, count, step, 0)
 
-    def begin(f):
+    def begin(f, some=None):
         own, in0 = flow(f)[:2]
         load, got0, sent0 = sems(f)[0], sems(f)[1], sems(f)[6]
 
@@ -814,7 +829,7 @@
             pltpu.make_async_copy(ins[f].at[core, chip_of(j, core)], own.at[j], load.at[j]).start()
             remote(ins[f].at[1 - core, chip_of(j, 1 - core)], in0.at[j], sent0.at[0], got0.at[j], twin).start()
 
-        loop(chips, body)
+        loop(chips, body) if some is None else [body(j) for j in some]
 
     def sum_of(f, j):
         own, in0 = flow(f)[:2]
@@ -892,6 +907,14 @@
             outs[f][core] = mine(f, total, core)[...]
             remote(mine(f, total, 1 - core), theirs, sems(f)[10].at[0], sems(f)[5].at[0], twin).start()
 
+    def across_level(f, k):
+        own, _, in1 = flow(f)[:3]
+        got1, sent1 = sems(f)[2], sems(f)[7]
+        for j in (k, depth + k):
+            own[j] = sum_of(f, j).astype(own.dtype)
+        for j in (k, depth + k):
+            remote(own.at[j], in1.at[j], sent1.at[0], got1.at[j], me + second).start()
+
     def multiply(t):
         slot = lax.rem(t, 2)
         pltpu.make_async_copy(slots.at[slot], slots.at[slot], slot_sem.at[slot]).wait()
@@ -899,62 +922,99 @@
         @pl.when(t < tall)
         def _():
             low = tn(slots[slot], held[0]).astype(BF)
-            count = down.shape[1] // tall
+            count = chips // tall
             for h in range(2):
                 part = low[:, h * WIDE : (h + 1) * WIDE].reshape((count,) + down.shape[2:])
-                down[h, pl.ds(t * count, count)] = part
+                down[h, pl.ds(level(t) * count, count)] = part
 
         @pl.when(t >= tall)
         def _():
-            low = tn(held[1], slots[slot]).astype(BF)
-            for i in range(2):
-                block = 2 * (t - tall) + i
-                part = low[:, i * WIDE : (i + 1) * WIDE].reshape(thirds.shape[1], thirds.shape[3], WIDE)
-                thirds[block // 3, :, lax.rem(block, 3)] = part
-
-        @pl.when(t + 2 < tasks)
+            k = jnp.where(t == ends[1], 0, 1)
+            low = tn(held[k], slots[slot]).astype(BF)
+            parts = [low[:, i * WIDE : (i + 1) * WIDE].reshape(chips, width // chips, WIDE) for i in range(2)]
+
+            @pl.when(t < ends[1])
+            def _():
+                for i in range(2):
+                    block = 2 * (t - tall) + i
+                    up[block // tall, :, lax.rem(block, tall)] = parts[i]
+
+            @pl.when(t == ends[1])
+            def _():
+                for i in range(2):
+                    out[i, :, 0] = parts[i]
+
+            @pl.when(t > ends[1])
+            def _():
+                for i in range(2):
+                    block = 2 * (t - ends[2]) + i
+                    thirds[block // 3, :, lax.rem(block, 3)] = parts[i]
+
+        @pl.when(t + 2 < ends[3])
         def _():
             fetch_task(t + 2)
 
-    up, out, small, low, last = range(flows)
-    for f in range(ready):
-        begin(f)
+        for k, at in ((2, ends[0] - 1), (3, ends[1] - 1)):
+
+            @pl.when(t == at)
+            def _(k=k):
+                held_copy(k).start()
+
+    tiny, low, wide, side, last = range(flows)
+    begin(tiny)
     for k in range(2):
         held_copy(k).wait()
 
     def task(t):
+        for k, at in ((2, ends[1]), (3, ends[2])):
+
+            @pl.when(t == at)
+            def _(k=k):
+                held_copy(k).wait()
+
         multiply(t)
 
-        @pl.when(t == 0)
+        @pl.when((t >= 1) & (t <= depth))
         def _():
-            across(up)
-
-        @pl.when(t == 1)
+            begin(low, [t - 1 + q * depth for q in range(4)])
+
+        @pl.when((t >= 2) & (t <= depth + 1))
         def _():
-            across(out)
-            across(small)
-
-        @pl.when(t == tall)
+            across_level(low, t - 2)
+
+        @pl.when(t == depth + 2)
         def _():
-            begin(low)
-
-        @pl.when(t == tall + 1)
+            across(tiny)
+
+        @pl.when(t == ends[1])
         def _():
-            across(low)
-            along(up)
-
-    loop(tasks, task)
-    along(out)
-    along(small)
+            begin(wide)
+            along(low)
+
+        @pl.when(t == ends[2])
+        def _():
+            begin(side)
+
+        @pl.when(t == ends[2] + 1)
+        def _():
+            across(wide)
+
+        @pl.when(t == ends[2] + 2)
+        def _():
+            across(side)
+
+    loop(ends[3], task)
+    upward(low)
     begin(last)
-    upward(up)
+    along(wide)
     across(last)
-    upward(out)
-    upward(small)
-    along(low)
-    upward(low)
+    along(side)
+    along(tiny)
+    upward(wide)
+    upward(side)
+    upward(tiny)
     along(last)
-    for f in range(ready + 1):
+    for f in range(flows - 1):
         finish(f)
     upward(last)
     finish(last)
@@ -968,16 +1028,17 @@
             arrived(ref, sem.at[0])
 
 
-def scatter_sums(parts, act, cot, n1, d_qkv, splits, depth):
+def scatter_sums(small, down, up, out, qkv, depth):
     chips = 4 * depth
-    tokens, width = cot.shape
+    tokens, width = down[1].shape
     rows = width // chips
     outs, buffers, signals = [], [], []
     dma = lambda n: pltpu.SemaphoreType.DMA((n,))
-    shapes = [(2, chips, 4, rows, WIDE), (2, chips, 3, rows, WIDE)]
+    shapes = [(2, chips, blocks, rows, WIDE) for blocks in (4, 4, 1, 3)]
     work = [pltpu.VMEM(x, BF) for x in shapes]
     work += [pltpu.VMEM((2, tokens, width), BF), pltpu.VMEM((2, tokens, width), BF), dma(2), dma(2)]
-    kinds = [(p.shape[2:], p.dtype) for p in parts] + [(x[2:], BF) for x in shapes]
+    kinds = [(small.shape[2:], small.dtype)] + [(x[2:], BF) for x in shapes]
+    splits = (None, "blocks", "rows", "rows", "rows")
     for (chunk, kind), split in zip(kinds, splits):
         if split == "rows":
             part = (chunk[0], chunk[1] // 2) + chunk[2:]
@@ -991,17 +1052,17 @@
         buffers += [pltpu.VMEM(chunk, F32), pltpu.VMEM(part, F32), dma(1)]
         signals += [dma(chips), dma(chips), dma(chips // 2), dma(depth), dma(depth - 1)] + [dma(1)] * 6
     return pl.pallas_call(
-        functools.partial(scatter_kernel, depth, tuple(splits)),
-        in_specs=[ANYWHERE] * (len(parts) + 4),
+        functools.partial(scatter_kernel, depth, splits),
+        in_specs=[ANYWHERE] * 9,
         out_specs=[pl.BlockSpec(memory_space=pltpu.VMEM)] * len(outs),
         out_shape=outs,
         scratch_shapes=work + buffers + signals,
         compiler_params=pltpu.CompilerParams(
-            collective_id=1, has_side_effects=True, vmem_limit_bytes=VMEM_LIMIT
+            collective_id=1, has_side_effects=True, vmem_limit_bytes=63 * 1024 * 1024
         ),
         cost_estimate=cost(0, 3e7),
         name="scatter_sums",
-    )(*parts, act, cot, n1, d_qkv)
+    )(small, *down, *up, *out, *qkv)
 
 
 def by_neighbours(devices, width, hidden, count):
@@ -1085,14 +1146,6 @@
     small = jnp.pad(small[None], ((0, 7), (0, WIDE - small.shape[0])))
     own1, own2, own3, oth1, oth2, oth3 = pack(w_qkv, small, w_out, w_up, w_down, core)
 
-    chunks1, chunks2, chunks3 = gather_shards(
-        (own1, own2, own3), (oth1, oth2, oth3), ([part] * 3 + [8], [part] * 5, [4 * part]), depth
-    )
-    vecs = chunks1[0, :, 6 * part :: 8].reshape(devices, WIDE).astype(F32)
-    g1, c1, bq, bv, bo, g2, c2, b2 = [vecs[:, i * part : (i + 1) * part].reshape(-1) for i in range(8)]
-    b1 = vecs[:, 8 * part : 12 * part].reshape(1, -1)
-    bias = weight_halves(jnp.concatenate([bq, jnp.zeros_like(bq), bv])[None])
-
     def spots_qkv(h, chip):
         return [
             (two * t, two, 0, (pl.ds(two * chip, two), pl.ds((3 * h + t) * WIDE, WIDE))) for t in range(3)
@@ -1107,16 +1160,17 @@
     def spots_down(h, chip):
         return [(0, 4 * two, 0, (pl.ds(4 * two * chip, 4 * two), pl.ds(h * WIDE, WIDE)))]
 
-    n1, qkv, wqkv = project_qkv(tokens, jnp.stack([g1, c1]), bias, chunks1, spots_qkv)
+    blocks = ([part] * 3 + [8], [part] * 5, [4 * part])
+    _, chunks2, chunks3, n1, qkv, wqkv, vecs, b1 = gather_shards(
+        (own1, own2, own3), (oth1, oth2, oth3), blocks, tokens, spots_qkv, depth
+    )
     attn, attn_t, lse = attention_fwd(qkv, *tables)
     layer_out, n2, act, d_pre, d_mid, d_branch, d_attn, sums2, sum_up = middle_part(
-        attn, tokens, cotangent, jnp.stack([g2, c2, bo, b2]), b1, (chunks2, chunks3), (spots_up, spots_down)
+        attn, tokens, cotangent, vecs, b1, (chunks2, chunks3), (spots_up, spots_down)
     )
 
-    g_up = grad_part([(n2, d_pre)], chips, two, "grad_up")
-    g_out = grad_part([(attn, d_branch)], chips, two, "grad_out")
     d_qkv = attention_bwd(qkv, d_attn, attn_t, lse, *tables)
-    input_grad, sums1 = first_norm_back(d_qkv, wqkv, tokens, d_mid, g1[None])
+    input_grad, sums1 = first_norm_back(d_qkv, wqkv, tokens, d_mid, vecs)
     by_half = sums1[2].reshape(2, 3, WIDE)
     vecs = [
         sums1[0, :width], sums1[1, :width], by_half[:, 0].reshape(-1), by_half[:, 2].reshape(-1),
@@ -1125,8 +1179,8 @@
     small = jnp.concatenate([v.reshape(devices, part) for v in vecs] + [sum_up.reshape(devices, 4 * part)], axis=1)
     small = small.reshape(chips, 2, 1, -1).swapaxes(0, 1)
     small = jnp.pad(small, ((0, 0), (0, 0), (0, 7), (0, WIDE - small.shape[3])))
-    g_up, g_out, small, g_down, g_qkv = scatter_sums(
-        [g_up, g_out, small], act, cotangent, n1, d_qkv, ("rows", "rows", None, "blocks", "rows"), depth
+    small, g_down, g_up, g_out, g_qkv = scatter_sums(
+        small, (act, cotangent), (n2, d_pre), (attn, d_branch), (n1, d_qkv), depth
     )
     small = small[0]
     s = [small[i * part : (i + 1) * part] for i in range(8)]

time: 404 us -> 385 us (0.953)
  Pallas kernels: 372 us -> 359 us
    pallas_call x5 -> x2, Pallas kernels: 201 us -> 184 us  [the longest x1 99.7 us: scatter_sums(): pl.pallas_call(functools.partial(scatter_kernel, depth, splits), in_specs...]
where the time goes in v5:
time: 385 us; the launch traced here: 380 us
  Pallas kernels  359 us (93%)
  local copies, waits for them, and re-layouts  16 us (4%)
    pallas_call x1, Pallas kernels, scatter_sums(): pl.pallas_call(functools.partial(scatter_kernel, depth, splits), in_specs...  99.7 us
    pallas_call x1, Pallas kernels, gather_shards(): pl.pallas_call(functools.partial(gather_kernel, blocks, depth, spots), in...  84.3 us
    pallas_call x1, Pallas kernels, middle_part(): pl.pallas_call(functools.partial(middle_kernel, spots), grid=(count // ro...  66.3 us
    pallas_call x1, Pallas kernels, attention_bwd(): pl.pallas_call(attn_bwd_kernel, grid_spec=pltpu.PrefetchScalarGridSpec(nu...  57.6 us
    pallas_call x1, Pallas kernels, attention_fwd(): pl.pallas_call(attn_fwd_kernel, grid_spec=pltpu.PrefetchScalarGridSpec(nu...  32.6 us
    pallas_call x1, Pallas kernels, first_norm_back(): pl.pallas_call(first_norm_kernel, grid=(count // TILE,), in_specs=[tile(c...  17 us

profile of v5, /device:TPU:0, one launch (start us, length us, event | category | flops | bytes accessed | tf_op | source)
XLA Modules:
  0.0 380.0 jit_solution(17817392325584973079)
XLA Ops:
  0.7 0.9 concatenate.25
  1.5 0.6 pad.8.refs_1_
  2.1 2.0 pack_shards.1
  4.1 84.3 %gather_and_qkv.1 = (bf16[2,16,160,384]{3,2,1,0:T(8,128)(2,1)}, bf16[2,16,240,384]{3,2,1,0:T(8,128)(2,1)}, bf16[2,16,192,384]{3,2,1,0:T(8,128)(2,1)}, bf16[2048,...) custom-call(bf16[80,384]{1,0:T(8,128)(2,1)} %get-tuple-element.47.re, ...), custom_call_target="tpu_custom_call" | custom-call | flops 7247757312 | bytes 30000000 | tf_op jit(solution)/shard_map/gather_and_qkv/pallas_call | solution.py:699
  88.5 0.1 slice.97
  88.6 0.1 slice.98
  88.7 0.2 convert_reduce_fusion
  89.0 0.6 and_select_fusion
  89.6 0.6 fusion.2.mr_ref
  90.2 1.2 fusion.1.oh_ref
  91.4 32.6 %attention_forward.1 = (bf16[2048,768]{1,0:T(8,128)(2,1)}, f32[2,768,1024]{2,1,0:T(8,128)}, f32[2,2,6,1024]{3,2,1,0:T(8,128)}) custom-call(s32[2,8]{1,0:T(2,128)} %get-tuple-element.98.lo, s32[2,8]{1,0:T(2,128)} %get-tuple-element.97.hi, bf16[2048,2304]{1,0:T(8,128)(2,1)} %get-tuple-element.53.q_ref.k_ref.v_ref, ...), custom_call_target="tpu_custom_call" | custom-call | flops 24000000000 | bytes 20000000 | tf_op jit(solution)/shard_map/attention_forward/pallas_call | solution.py:265
  123.9 66.3 %middle.1 = (bf16[2048,768]{1,0:T(8,128)(2,1)}, bf16[2048,768]{1,0:T(8,128)(2,1)}, bf16[2048,3072]{1,0:T(8,128)(2,1)}, bf16[2048,3072]{1,0:T(8,128)(2,1)}, f32[2...) custom-call(bf16[2048,768]{1,0:T(8,128)(2,1)} %get-tuple-element.54., ...), custom_call_target="tpu_custom_call" | custom-call | flops 43486543872 | bytes 60000000 | tf_op jit(solution)/shard_map/middle/pallas_call | solution.py:432
  190.2 57.6 %attention_backward.1.d_qkv.refs_8_ = bf16[2048,2304]{1,0:T(8,128)(2,1)} custom-call(s32[2,8]{1,0:T(2,128)} %get-tuple-element.98.lo, s32[2,8]{1,0:T(2,128)} %get-tuple-element.97.hi, bf16[2048,2304]{1,0:T(8,128)(2,1)} %get-tuple-element.53.q_ref.k_ref.v_ref, bf16[2048,2304]{1,0:T(8,128)(2,1)} %get-tuple-element.53.q_ref.k_ref.v_ref, ...), custom_call_target="tpu_custom_call" | custom-call | flops 44000002048 | bytes 40000000 | tf_op jit(solution)/shard_map/attention_backward/pallas_call | solution.py:303
  247.8 17.0 %first_norm_back.1 = (bf16[2048,768]{1,0:T(8,128)(2,1)}, f32[8,2304]{1,0:T(8,128)}) custom-call(bf16[2048,2304]{1,0:T(8,128)(2,1)} %attention_backward.1.d_qkv.refs_8_, bf16[768,2304]{1,0:T(8,128)(2,1)} %get-tuple-element.63.w, bf16[2048,768]{1,0:T(8,128)(2,1)} %tok.3, f32[2048,768]{1,0:T(8,128)} %get-tuple-element.64.d_mid, f32[8,768]{1,0:T(8,128)} %get-tuple-element.55.vec), custom_call_target="tpu_custom_call" | custom-call | flops 7247757312 | bytes 30000000 | tf_op jit(solution)/shard_map/first_norm_back/pallas_call | solution.py:470
  264.8 0.9 slice_reduce_fusion
  265.7 0.1 concatenate.28
  265.9 0.1 concatenate.29
  266.0 0.8 slice_reduce_fusion.7
  266.8 0.1 concatenate.26
  267.6 0.5 broadcast.68
  268.1 0.7 reduce.21
  268.9 0.4 concatenate.35
  269.4 0.8 pad.9.refs_0_
  270.2 99.7 %scatter_sums.1 = (f32[8,384]{1,0:T(8,128)}, f32[2,2,48,384]{3,2,1,0:T(8,128)}, f32[2,4,24,384]{3,2,1,0:T(8,128)}, f32[2,1,24,384]{3,2,1,0:T(8,128)}, f32[2,3,24,384]{3,2,1,0:T(8,128)}) custom-call(f32[2,16,8,384]{3,2,1,0:T(8,128)} %pad.9.refs_0_, bf16[2048,3072]{1,0:T(8,128)(2,1)} %get-tuple-element.69.refs_1_, bf16[2048,768]{1,0:T(8,128)(2,1)} %refs_2_.3, ...), custom_call_target="tpu_custom_call" | custom-call | bytes 30000000 | tf_op jit(solution)/shard_map/scatter_sums/pallas_call | solution.py:1054
  369.9 1.0 copy.56
  371.0 0.8 reshape.108
  371.8 1.0 copy.54
  372.9 0.9 reshape.106
  373.7 1.7 copy.59
  375.4 1.5 copy.58
  376.9 1.5 slice_bitcast_fusion
  378.4 1.3 slice_bitcast_fusion.1
  (28 shorter events, 0.8 us)
Async XLA Ops:
  4.1 84.4 %copy-start = (s32[2048]{0:T(1024)S(1)}, s32[2048]{0:T(1024)}, u32[]{:S(2)}) copy-start(s32[2048]{0:T(1024)} %param.17) | copy-start | bytes 24580
  247.8 19.3 %copy-start.2 = (f32[8,768]{1,0:T(8,128)S(1)}, f32[8,768]{1,0:T(8,128)}, u32[]{:S(2)}) copy-start(f32[8,768]{1,0:T(8,128)} %get-tuple-element.67) | copy-start | bytes 73732
  247.8 20.4 %copy-start.1 = (f32[1,3072]{1,0:T(1,128)S(1)}, f32[1,3072]{1,0:T(1,128)}, u32[]{:S(2)}) copy-start(f32[1,3072]{1,0:T(1,128)} %get-tuple-element.68) | copy-start | bytes 36868

commit v6 on v5

--- a/solution.py
+++ b/solution.py
@@ -483,6 +483,24 @@
     return lax.dot_general(a, b, (((0,), (0,)), ((), ())), preferred_element_type=F32)
 
 
+def hand_over_kernel(*refs):
+    count = len(refs) // 2
+    for x, out in zip(refs[:count], refs[count:]):
+        out[...] = x[...]
+
+
+def hand_over(*arrays):
+    return pl.pallas_call(
+        hand_over_kernel,
+        grid=(1,),
+        in_specs=[whole(x.shape) for x in arrays],
+        out_specs=[whole(x.shape) for x in arrays],
+        out_shape=[jax.ShapeDtypeStruct(x.shape, x.dtype) for x in arrays],
+        compiler_params=params("arbitrary"),
+        name="hand_over",
+    )(*arrays)
+
+
 def neighbours():
     me = lax.axis_index("fsdp")
     core = lax.rem(me, 2)
@@ -639,8 +657,6 @@
 
     from_far(0)
     from_near(0)
-    from_far(1)
-    from_near(1)
     from_cross(0)
     from_twin(0)
     fetch(outs[0], spots, [w], w_sem)
@@ -648,15 +664,18 @@
     first_row = outs[0].shape[2] - 16
     for at in range(chips):
         pltpu.make_async_copy(outs[0].at[0, at, pl.ds(first_row, 16), :], rows.at[pl.ds(16 * at, 16), :], rows_sem.at[0]).start()
-    from_far(2)
-    from_near(2)
+    from_far(1)
+    from_near(1)
     arrived(rows, rows_sem.at[0])
     gathered_vectors(rows[...], vecs, wide)
     tok_load.wait()
     fetched(w, w_sem.at[0])
     w_put = pltpu.make_async_copy(w, w_out, load_sem.at[1])
     w_put.start()
-    several(0, tiles // 2)
+    several(0, tiles // 4)
+    from_far(2)
+    several(tiles // 4, tiles // 2)
+    from_near(2)
     from_cross(1)
     several(tiles // 2, tiles)
     from_cross(2)
@@ -896,6 +915,14 @@
         half = ref.shape[0] // 2
         return ref.at[pl.ds(which * half, half)]
 
+    def place(f, half, part):
+        if splits[f] == "blocks":
+            part = part.reshape((1,) + outs[f].shape[:1] + part.shape[2:])
+        half_step, block_step = {4: (4, 1), 1: (1, 1), 3: (1, 2)}[part.shape[0]]
+        for b in range(part.shape[0]):
+            at = (half * half_step + b * block_step) * WIDE
+            outs[f][:, pl.ds(pl.multiple_of(at, 128), WIDE)] = part[b]
+
     def finish(f):
         in3, total, theirs = flow(f)[4], flow(f)[5], flow(f)[6]
         for k in range(depth - 1):
@@ -904,7 +931,7 @@
         if splits[f] is None:
             outs[f][...] = total[...]
         else:
-            outs[f][core] = mine(f, total, core)[...]
+            place(f, core, mine(f, total, core)[...])
             remote(mine(f, total, 1 - core), theirs, sems(f)[10].at[0], sems(f)[5].at[0], twin).start()
 
     def across_level(f, k):
@@ -1022,7 +1049,7 @@
         _, in0, in1, in2, in3, total, theirs, _ = flow(f)
         if splits[f] is not None:
             arrived(theirs, sems(f)[5].at[0])
-            outs[f][1 - core] = theirs[...]
+            place(f, 1 - core, theirs[...])
             arrived(theirs, sems(f)[10].at[0])
         for ref, sem in zip((in0, in1, in2, in3), sems(f)[6:10]):
             arrived(ref, sem.at[0])
@@ -1046,7 +1073,9 @@
             part = (chunk[0] // 2,) + chunk[1:]
         else:
             part = chunk
-        outs.append(jax.ShapeDtypeStruct(part if split is None else (2,) + part, F32))
+        tall = part[-2] if split == "rows" else part[0] * part[1]
+        cols = 2 * WIDE * (chunk[0] if split == "rows" else 1)
+        outs.append(jax.ShapeDtypeStruct(part if split is None else (tall, cols), F32))
         for count in (chips, chips, chips // 2, depth, depth - 1):
             buffers.append(pltpu.VMEM((count,) + chunk, kind))
         buffers += [pltpu.VMEM(chunk, F32), pltpu.VMEM(part, F32), dma(1)]
@@ -1171,24 +1200,19 @@
 
     d_qkv = attention_bwd(qkv, d_attn, attn_t, lse, *tables)
     input_grad, sums1 = first_norm_back(d_qkv, wqkv, tokens, d_mid, vecs)
-    by_half = sums1[2].reshape(2, 3, WIDE)
-    vecs = [
-        sums1[0, :width], sums1[1, :width], by_half[:, 0].reshape(-1), by_half[:, 2].reshape(-1),
-        sums2[2], sums2[0], sums2[1], sums2[3],
-    ]
-    small = jnp.concatenate([v.reshape(devices, part) for v in vecs] + [sum_up.reshape(devices, 4 * part)], axis=1)
+    by_half = sums1[2].reshape(2, 3, WIDE).swapaxes(0, 1).reshape(3, width)
+    vecs = jnp.concatenate([sums1[:2, :width], by_half[0:1], by_half[2:3], sums2[2:3], sums2[0:2], sums2[3:4]])
+    vecs = vecs.reshape(8, devices, part).swapaxes(0, 1).reshape(devices, width // devices * 8)
+    small = jnp.concatenate([vecs, sum_up.reshape(devices, 4 * part)], axis=1)
     small = small.reshape(chips, 2, 1, -1).swapaxes(0, 1)
     small = jnp.pad(small, ((0, 0), (0, 0), (0, 7), (0, WIDE - small.shape[3])))
     small, g_down, g_up, g_out, g_qkv = scatter_sums(
         small, (act, cotangent), (n2, d_pre), (attn, d_branch), (n1, d_qkv), depth
     )
+    small, g_down, g_up, g_out, g_qkv = hand_over(small[:1], g_down, g_up, g_out, g_qkv)
     small = small[0]
     s = [small[i * part : (i + 1) * part] for i in range(8)]
     s_b1 = small[8 * part : 12 * part]
-    g_up = g_up.transpose(2, 0, 1, 3).reshape(part, hidden)
-    g_out = g_out[:, 0].transpose(1, 0, 2).reshape(part, width)
-    g_down = g_down.reshape(2, 4 * part, WIDE).transpose(1, 0, 2).reshape(4 * part, width)
-    g_qkv = g_qkv.transpose(2, 1, 0, 3).reshape(part, 3 * width)
     return (
         layer_out, input_grad, s[0], s[1], g_qkv, s[2], s[3], g_out, s[4], s[5], s[6], g_up, s_b1, g_down, s[7],
     )

time: 385 us -> 377 us (0.979)
  local copies, waits for them, and re-layouts: 16 us -> 9.56 us
    reshape x4 -> x0, local copies, waits for them, and re-layouts: 4.91 us -> none  [the longest x1 1.69 us: by_chips(): g_down.reshape(2, 4 * part, WIDE).transpose(1, 0, 2)]
where the time goes in v6:
time: 377 us; the launch traced here: 372 us
  Pallas kernels  358 us (95%)
  local copies, waits for them, and re-layouts  9.56 us (3%)
    pallas_call x1, Pallas kernels, scatter_sums(): pl.pallas_call(functools.partial(scatter_kernel, depth, splits), in_specs...  101 us
    pallas_call x1, Pallas kernels, gather_shards(): pl.pallas_call(functools.partial(gather_kernel, blocks, depth, spots), in...  82.1 us
    pallas_call x1, Pallas kernels, middle_part(): pl.pallas_call(functools.partial(middle_kernel, spots), grid=(count // ro...  66.2 us
    pallas_call x1, Pallas kernels, attention_bwd(): pl.pallas_call(attn_bwd_kernel, grid_spec=pltpu.PrefetchScalarGridSpec(nu...  55 us
    pallas_call x1, Pallas kernels, attention_fwd(): pl.pallas_call(attn_fwd_kernel, grid_spec=pltpu.PrefetchScalarGridSpec(nu...  33.1 us
    pallas_call x1, Pallas kernels, first_norm_back(): pl.pallas_call(first_norm_kernel, grid=(count // TILE,), in_specs=[tile(c...  17 us

profile of v6, /device:TPU:0, one launch (start us, length us, event | category | flops | bytes accessed | tf_op | source)
XLA Modules:
  0.0 372.3 jit_solution(13069618592518889365)
XLA Ops:
  0.7 0.9 concatenate.27
  1.5 0.6 pad.8.refs_1_
  2.1 2.0 pack_shards.1
  4.1 82.1 %gather_and_qkv.1 = (bf16[2,16,160,384]{3,2,1,0:T(8,128)(2,1)}, bf16[2,16,240,384]{3,2,1,0:T(8,128)(2,1)}, bf16[2,16,192,384]{3,2,1,0:T(8,128)(2,1)}, bf16[2048,...) custom-call(bf16[80,384]{1,0:T(8,128)(2,1)} %get-tuple-element.52.re, ...), custom_call_target="tpu_custom_call" | custom-call | flops 7247757312 | bytes 30000000 | tf_op jit(solution)/shard_map/gather_and_qkv/pallas_call | solution.py:718
  86.2 0.1 slice.86
  86.3 0.1 slice.87
  86.4 0.2 convert_reduce_fusion
  86.7 0.6 and_select_fusion
  87.3 0.6 fusion.2.mr_ref
  87.9 1.2 fusion.1.oh_ref
  89.1 33.1 %attention_forward.1 = (bf16[2048,768]{1,0:T(8,128)(2,1)}, f32[2,768,1024]{2,1,0:T(8,128)}, f32[2,2,6,1024]{3,2,1,0:T(8,128)}) custom-call(s32[2,8]{1,0:T(2,128)} %get-tuple-element.104.lo, s32[2,8]{1,0:T(2,128)} %get-tuple-element.103.hi, bf16[2048,2304]{1,0:T(8,128)(2,1)} %get-tuple-element.58.q_ref.k_ref.v_ref, ...), custom_call_target="tpu_custom_call" | custom-call | flops 24000000000 | bytes 20000000 | tf_op jit(solution)/shard_map/attention_forward/pallas_call | solution.py:265
  122.2 66.2 %middle.1 = (bf16[2048,768]{1,0:T(8,128)(2,1)}, bf16[2048,768]{1,0:T(8,128)(2,1)}, bf16[2048,3072]{1,0:T(8,128)(2,1)}, bf16[2048,3072]{1,0:T(8,128)(2,1)}, f32[2...) custom-call(bf16[2048,768]{1,0:T(8,128)(2,1)} %get-tuple-element.59., ...), custom_call_target="tpu_custom_call" | custom-call | flops 43486543872 | bytes 60000000 | tf_op jit(solution)/shard_map/middle/pallas_call | solution.py:432
  188.4 55.0 %attention_backward.1.d_qkv.refs_8_ = bf16[2048,2304]{1,0:T(8,128)(2,1)} custom-call(s32[2,8]{1,0:T(2,128)} %get-tuple-element.104.lo, s32[2,8]{1,0:T(2,128)} %get-tuple-element.103.hi, bf16[2048,2304]{1,0:T(8,128)(2,1)} %get-tuple-element.58.q_ref.k_ref.v_ref, bf16[2048,2304]{1,0:T(8,128)(2,1)} %get-tuple-element.58.q_ref.k_ref.v_ref, ...), custom_call_target="tpu_custom_call" | custom-call | flops 44000002048 | bytes 40000000 | tf_op jit(solution)/shard_map/attention_backward/pallas_call | solution.py:303
  243.4 17.0 %first_norm_back.1 = (bf16[2048,768]{1,0:T(8,128)(2,1)}, f32[8,2304]{1,0:T(8,128)}) custom-call(bf16[2048,2304]{1,0:T(8,128)(2,1)} %attention_backward.1.d_qkv.refs_8_, bf16[768,2304]{1,0:T(8,128)(2,1)} %get-tuple-element.68.w, bf16[2048,768]{1,0:T(8,128)(2,1)} %tok.3, f32[2048,768]{1,0:T(8,128)} %get-tuple-element.69.d_mid, f32[8,768]{1,0:T(8,128)} %get-tuple-element.60.vec), custom_call_target="tpu_custom_call" | custom-call | flops 7247757312 | bytes 30000000 | tf_op jit(solution)/shard_map/first_norm_back/pallas_call | solution.py:470
  260.4 0.7 slice.88
  261.2 0.1 concatenate.28
  261.3 0.9 slice_reduce_fusion
  262.3 0.1 concatenate.29
  262.4 0.1 concatenate.30
  262.6 0.1 concatenate.32
  262.8 0.1 copy.34
  262.9 0.1 concatenate.35
  263.1 0.5 broadcast.64
  263.6 0.7 reduce.13
  264.3 0.1 concatenate.36
  264.4 0.1 maximum_bitcast_fusion
  264.5 0.8 pad.9.refs_0_
  265.3 100.6 %scatter_sums.1 = (f32[8,384]{1,0:T(8,128)}, f32[96,768]{1,0:T(8,128)}, f32[24,3072]{1,0:T(8,128)}, f32[24,768]{1,0:T(8,128)}, f32[24,2304]{1,0:T(8,128)}) custom-call(f32[2,16,8,384]{3,2,1,0:T(8,128)} %pad.9.refs_0_, bf16[2048,3072]{1,0:T(8,128)(2,1)} %get-tuple-element.74.refs_1_, bf16[2048,768]{1,0:T(8,128)(2,1)} %refs_2_.3, ...), custom_call_target="tpu_custom_call" | custom-call | bytes 30000000 | tf_op jit(solution)/shard_map/scatter_sums/pallas_call | solution.py:1083
  365.9 1.3 slice.95.refs_0_
  367.2 2.1 hand_over.1
  369.3 1.4 slice_bitcast_fusion
  370.7 1.3 slice_bitcast_fusion.1
  (24 shorter events, 0.3 us)
Async XLA Ops:
  4.1 82.1 %copy-start = (s32[2048]{0:T(1024)S(1)}, s32[2048]{0:T(1024)}, u32[]{:S(2)}) copy-start(s32[2048]{0:T(1024)} %param.17) | copy-start | bytes 24580
  243.4 19.0 %copy-start.2 = (f32[8,768]{1,0:T(8,128)S(1)}, f32[8,768]{1,0:T(8,128)}, u32[]{:S(2)}) copy-start(f32[8,768]{1,0:T(8,128)} %get-tuple-element.72) | copy-start | bytes 73732
  243.4 20.1 %copy-start.1 = (f32[1,3072]{1,0:T(1,128)S(1)}, f32[1,3072]{1,0:T(1,128)}, u32[]{:S(2)}) copy-start(f32[1,3072]{1,0:T(1,128)} %get-tuple-element.73) | copy-start | bytes 36868

commit v7 on v6

--- a/solution.py
+++ b/solution.py
@@ -1033,18 +1033,17 @@
     loop(ends[3], task)
     upward(low)
     begin(last)
+    across(last)
     along(wide)
-    across(last)
     along(side)
     along(tiny)
     upward(wide)
+    along(last)
     upward(side)
     upward(tiny)
-    along(last)
-    for f in range(flows - 1):
+    upward(last)
+    for f in (low, wide, side, tiny, last):
         finish(f)
-    upward(last)
-    finish(last)
     for f in range(flows):
         _, in0, in1, in2, in3, total, theirs, _ = flow(f)
         if splits[f] is not None:

time: 377 us -> 378 us (level)
  no operation moved by 1% of the time
where the time goes in v7:
time: 378 us; the launch traced here: 371 us
  Pallas kernels  356 us (94%)
  local copies, waits for them, and re-layouts  9.56 us (3%)
    pallas_call x1, Pallas kernels, scatter_sums(): pl.pallas_call(functools.partial(scatter_kernel, depth, splits), in_specs...  101 us
    pallas_call x1, Pallas kernels, gather_shards(): pl.pallas_call(functools.partial(gather_kernel, blocks, depth, spots), in...  82.1 us
    pallas_call x1, Pallas kernels, middle_part(): pl.pallas_call(functools.partial(middle_kernel, spots), grid=(count // ro...  66.2 us
    pallas_call x1, Pallas kernels, attention_bwd(): pl.pallas_call(attn_bwd_kernel, grid_spec=pltpu.PrefetchScalarGridSpec(nu...  52.9 us
    pallas_call x1, Pallas kernels, attention_fwd(): pl.pallas_call(attn_fwd_kernel, grid_spec=pltpu.PrefetchScalarGridSpec(nu...  33 us
    pallas_call x1, Pallas kernels, first_norm_back(): pl.pallas_call(first_norm_kernel, grid=(count // TILE,), in_specs=[tile(c...  17 us

profile of v7, /device:TPU:0, one launch (start us, length us, event | category | flops | bytes accessed | tf_op | source)
XLA Modules:
  0.0 370.5 jit_solution(11912681785536927040)
XLA Ops:
  0.7 0.9 concatenate.27
  1.5 0.6 pad.8.refs_1_
  2.1 2.0 pack_shards.1
  4.1 82.1 %gather_and_qkv.1 = (bf16[2,16,160,384]{3,2,1,0:T(8,128)(2,1)}, bf16[2,16,240,384]{3,2,1,0:T(8,128)(2,1)}, bf16[2,16,192,384]{3,2,1,0:T(8,128)(2,1)}, bf16[2048,...) custom-call(bf16[80,384]{1,0:T(8,128)(2,1)} %get-tuple-element.52.re, ...), custom_call_target="tpu_custom_call" | custom-call | flops 7247757312 | bytes 30000000 | tf_op jit(solution)/shard_map/gather_and_qkv/pallas_call | solution.py:718
  86.2 0.1 slice.86
  86.3 0.1 slice.87
  86.4 0.2 convert_reduce_fusion
  86.7 0.6 and_select_fusion
  87.3 0.6 fusion.2.mr_ref
  87.9 1.2 fusion.1.oh_ref
  89.1 33.0 %attention_forward.1 = (bf16[2048,768]{1,0:T(8,128)(2,1)}, f32[2,768,1024]{2,1,0:T(8,128)}, f32[2,2,6,1024]{3,2,1,0:T(8,128)}) custom-call(s32[2,8]{1,0:T(2,128)} %get-tuple-element.104.lo, s32[2,8]{1,0:T(2,128)} %get-tuple-element.103.hi, bf16[2048,2304]{1,0:T(8,128)(2,1)} %get-tuple-element.58.q_ref.k_ref.v_ref, ...), custom_call_target="tpu_custom_call" | custom-call | flops 24000000000 | bytes 20000000 | tf_op jit(solution)/shard_map/attention_forward/pallas_call | solution.py:265
  122.1 66.2 %middle.1 = (bf16[2048,768]{1,0:T(8,128)(2,1)}, bf16[2048,768]{1,0:T(8,128)(2,1)}, bf16[2048,3072]{1,0:T(8,128)(2,1)}, bf16[2048,3072]{1,0:T(8,128)(2,1)}, f32[2...) custom-call(bf16[2048,768]{1,0:T(8,128)(2,1)} %get-tuple-element.59., ...), custom_call_target="tpu_custom_call" | custom-call | flops 43486543872 | bytes 60000000 | tf_op jit(solution)/shard_map/middle/pallas_call | solution.py:432
  188.4 52.9 %attention_backward.1.d_qkv.refs_8_ = bf16[2048,2304]{1,0:T(8,128)(2,1)} custom-call(s32[2,8]{1,0:T(2,128)} %get-tuple-element.104.lo, s32[2,8]{1,0:T(2,128)} %get-tuple-element.103.hi, bf16[2048,2304]{1,0:T(8,128)(2,1)} %get-tuple-element.58.q_ref.k_ref.v_ref, bf16[2048,2304]{1,0:T(8,128)(2,1)} %get-tuple-element.58.q_ref.k_ref.v_ref, ...), custom_call_target="tpu_custom_call" | custom-call | flops 44000002048 | bytes 40000000 | tf_op jit(solution)/shard_map/attention_backward/pallas_call | solution.py:303
  241.2 17.0 %first_norm_back.1 = (bf16[2048,768]{1,0:T(8,128)(2,1)}, f32[8,2304]{1,0:T(8,128)}) custom-call(bf16[2048,2304]{1,0:T(8,128)(2,1)} %attention_backward.1.d_qkv.refs_8_, bf16[768,2304]{1,0:T(8,128)(2,1)} %get-tuple-element.68.w, bf16[2048,768]{1,0:T(8,128)(2,1)} %tok.3, f32[2048,768]{1,0:T(8,128)} %get-tuple-element.69.d_mid, f32[8,768]{1,0:T(8,128)} %get-tuple-element.60.vec), custom_call_target="tpu_custom_call" | custom-call | flops 7247757312 | bytes 30000000 | tf_op jit(solution)/shard_map/first_norm_back/pallas_call | solution.py:470
  258.2 0.7 slice.88
  259.0 0.1 concatenate.28
  259.1 0.9 slice_reduce_fusion
  260.1 0.1 concatenate.29
  260.2 0.1 concatenate.30
  260.4 0.1 concatenate.32
  260.6 0.1 copy.34
  260.7 0.1 concatenate.35
  260.9 0.5 broadcast.64
  261.4 0.7 reduce.13
  262.1 0.1 concatenate.36
  262.2 0.1 maximum_bitcast_fusion
  262.3 0.8 pad.9.refs_0_
  263.1 101.1 %scatter_sums.1 = (f32[8,384]{1,0:T(8,128)}, f32[96,768]{1,0:T(8,128)}, f32[24,3072]{1,0:T(8,128)}, f32[24,768]{1,0:T(8,128)}, f32[24,2304]{1,0:T(8,128)}) custom-call(f32[2,16,8,384]{3,2,1,0:T(8,128)} %pad.9.refs_0_, bf16[2048,3072]{1,0:T(8,128)(2,1)} %get-tuple-element.74.refs_1_, bf16[2048,768]{1,0:T(8,128)(2,1)} %refs_2_.3, ...), custom_call_target="tpu_custom_call" | custom-call | bytes 30000000 | tf_op jit(solution)/shard_map/scatter_sums/pallas_call | solution.py:1082
  364.2 1.3 slice.95.refs_0_
  365.5 2.1 hand_over.1
  367.6 1.4 slice_bitcast_fusion
  369.0 1.3 slice_bitcast_fusion.1
  (24 shorter events, 0.3 us)
Async XLA Ops:
  4.1 82.1 %copy-start = (s32[2048]{0:T(1024)S(1)}, s32[2048]{0:T(1024)}, u32[]{:S(2)}) copy-start(s32[2048]{0:T(1024)} %param.17) | copy-start | bytes 24580
  241.2 19.0 %copy-start.2 = (f32[8,768]{1,0:T(8,128)S(1)}, f32[8,768]{1,0:T(8,128)}, u32[]{:S(2)}) copy-start(f32[8,768]{1,0:T(8,128)} %get-tuple-element.72) | copy-start | bytes 73732
  241.2 20.1 %copy-start.1 = (f32[1,3072]{1,0:T(1,128)S(1)}, f32[1,3072]{1,0:T(1,128)}, u32[]{:S(2)}) copy-start(f32[1,3072]{1,0:T(1,128)} %get-tuple-element.73) | copy-start | bytes 36868

commit v8 on v7

--- a/solution.py
+++ b/solution.py
@@ -369,7 +369,7 @@
 
 
 GAIN1, SHIFT1, BIAS_Q, BIAS_V, BIAS_OUT, GAIN2, SHIFT2, BIAS_DOWN = range(8)
-STRIP = 768
+STRIP = 256
 CURVE = 0.7978845608028654
 CUBIC = 0.044715
 
@@ -426,7 +426,7 @@
 def middle_part(attn, tokens, cotangent, vec, b1, gathered, spots):
     count, width = tokens.shape
     hidden = b1.shape[1]
-    rows = TILE // 2
+    rows = TILE
     tile = lambda w: pl.BlockSpec((rows, w), lambda i: (i, 0))
     row = lambda w, kind: jax.ShapeDtypeStruct((count, w), kind)
     return pl.pallas_call(

time: 378 us -> 374 us (0.989)
  no operation moved by 1% of the time
where the time goes in v8:
time: 374 us; the launch traced here: 369 us
  Pallas kernels  355 us (95%)
  local copies, waits for them, and re-layouts  9.56 us (3%)
    pallas_call x1, Pallas kernels, scatter_sums(): pl.pallas_call(functools.partial(scatter_kernel, depth, splits), in_specs...  99.6 us
    pallas_call x1, Pallas kernels, gather_shards(): pl.pallas_call(functools.partial(gather_kernel, blocks, depth, spots), in...  81.7 us
    pallas_call x1, Pallas kernels, middle_part(): pl.pallas_call(functools.partial(middle_kernel, spots), grid=(count // ro...  66.6 us
    pallas_call x1, Pallas kernels, attention_bwd(): pl.pallas_call(attn_bwd_kernel, grid_spec=pltpu.PrefetchScalarGridSpec(nu...  53.4 us
    pallas_call x1, Pallas kernels, attention_fwd(): pl.pallas_call(attn_fwd_kernel, grid_spec=pltpu.PrefetchScalarGridSpec(nu...  32.7 us
    pallas_call x1, Pallas kernels, first_norm_back(): pl.pallas_call(first_norm_kernel, grid=(count // TILE,), in_specs=[tile(c...  17 us

profile of v8, /device:TPU:0, one launch (start us, length us, event | category | flops | bytes accessed | tf_op | source)
XLA Modules:
  0.0 369.2 jit_solution(13355195762234126132)
XLA Ops:
  0.7 0.9 concatenate.27
  1.5 0.6 pad.8.refs_1_
  2.1 2.0 pack_shards.1
  4.1 81.7 %gather_and_qkv.1 = (bf16[2,16,160,384]{3,2,1,0:T(8,128)(2,1)}, bf16[2,16,240,384]{3,2,1,0:T(8,128)(2,1)}, bf16[2,16,192,384]{3,2,1,0:T(8,128)(2,1)}, bf16[2048,...) custom-call(bf16[80,384]{1,0:T(8,128)(2,1)} %get-tuple-element.52.re, ...), custom_call_target="tpu_custom_call" | custom-call | flops 7247757312 | bytes 30000000 | tf_op jit(solution)/shard_map/gather_and_qkv/pallas_call | solution.py:718
  85.9 0.1 slice.86
  86.0 0.1 slice.87
  86.1 0.2 convert_reduce_fusion
  86.4 0.6 and_select_fusion
  87.0 0.6 fusion.2.mr_ref
  87.6 1.2 fusion.1.oh_ref
  88.8 32.7 %attention_forward.1 = (bf16[2048,768]{1,0:T(8,128)(2,1)}, f32[2,768,1024]{2,1,0:T(8,128)}, f32[2,2,6,1024]{3,2,1,0:T(8,128)}) custom-call(s32[2,8]{1,0:T(2,128)} %get-tuple-element.104.lo, s32[2,8]{1,0:T(2,128)} %get-tuple-element.103.hi, bf16[2048,2304]{1,0:T(8,128)(2,1)} %get-tuple-element.58.q_ref.k_ref.v_ref, ...), custom_call_target="tpu_custom_call" | custom-call | flops 24000000000 | bytes 20000000 | tf_op jit(solution)/shard_map/attention_forward/pallas_call | solution.py:265
  121.5 66.6 %middle.1 = (bf16[2048,768]{1,0:T(8,128)(2,1)}, bf16[2048,768]{1,0:T(8,128)(2,1)}, bf16[2048,3072]{1,0:T(8,128)(2,1)}, bf16[2048,3072]{1,0:T(8,128)(2,1)}, f32[2...) custom-call(bf16[2048,768]{1,0:T(8,128)(2,1)} %get-tuple-element.59., ...), custom_call_target="tpu_custom_call" | custom-call | flops 43486543872 | bytes 60000000 | tf_op jit(solution)/shard_map/middle/pallas_call | solution.py:432
  188.1 53.4 %attention_backward.1.d_qkv.refs_8_ = bf16[2048,2304]{1,0:T(8,128)(2,1)} custom-call(s32[2,8]{1,0:T(2,128)} %get-tuple-element.104.lo, s32[2,8]{1,0:T(2,128)} %get-tuple-element.103.hi, bf16[2048,2304]{1,0:T(8,128)(2,1)} %get-tuple-element.58.q_ref.k_ref.v_ref, bf16[2048,2304]{1,0:T(8,128)(2,1)} %get-tuple-element.58.q_ref.k_ref.v_ref, ...), custom_call_target="tpu_custom_call" | custom-call | flops 44000002048 | bytes 40000000 | tf_op jit(solution)/shard_map/attention_backward/pallas_call | solution.py:303
  241.5 17.0 %first_norm_back.1 = (bf16[2048,768]{1,0:T(8,128)(2,1)}, f32[8,2304]{1,0:T(8,128)}) custom-call(bf16[2048,2304]{1,0:T(8,128)(2,1)} %attention_backward.1.d_qkv.refs_8_, bf16[768,2304]{1,0:T(8,128)(2,1)} %get-tuple-element.68.w, bf16[2048,768]{1,0:T(8,128)(2,1)} %tok.3, f32[2048,768]{1,0:T(8,128)} %get-tuple-element.69.d_mid, f32[8,768]{1,0:T(8,128)} %get-tuple-element.60.vec), custom_call_target="tpu_custom_call" | custom-call | flops 7247757312 | bytes 30000000 | tf_op jit(solution)/shard_map/first_norm_back/pallas_call | solution.py:470
  258.4 0.7 slice.88
  259.2 0.1 concatenate.28
  259.3 0.9 slice_reduce_fusion
  260.2 0.1 concatenate.29
  260.3 0.1 concatenate.30
  260.6 0.1 concatenate.32
  260.8 0.1 copy.34
  260.9 0.1 concatenate.35
  261.0 0.5 broadcast.64
  261.6 0.7 reduce.13
  262.2 0.1 concatenate.36
  262.4 0.1 maximum_bitcast_fusion
  262.5 0.8 pad.9.refs_0_
  263.3 99.6 %scatter_sums.1 = (f32[8,384]{1,0:T(8,128)}, f32[96,768]{1,0:T(8,128)}, f32[24,3072]{1,0:T(8,128)}, f32[24,768]{1,0:T(8,128)}, f32[24,2304]{1,0:T(8,128)}) custom-call(f32[2,16,8,384]{3,2,1,0:T(8,128)} %pad.9.refs_0_, bf16[2048,3072]{1,0:T(8,128)(2,1)} %get-tuple-element.74.refs_1_, bf16[2048,768]{1,0:T(8,128)(2,1)} %refs_2_.3, ...), custom_call_target="tpu_custom_call" | custom-call | bytes 30000000 | tf_op jit(solution)/shard_map/scatter_sums/pallas_call | solution.py:1082
  362.9 1.3 slice.95.refs_0_
  364.2 2.1 hand_over.1
  366.3 1.4 slice_bitcast_fusion
  367.7 1.3 slice_bitcast_fusion.1
  (24 shorter events, 0.3 us)
Async XLA Ops:
  4.1 81.8 %copy-start = (s32[2048]{0:T(1024)S(1)}, s32[2048]{0:T(1024)}, u32[]{:S(2)}) copy-start(s32[2048]{0:T(1024)} %param.17) | copy-start | bytes 24580
  241.4 19.0 %copy-start.2 = (f32[8,768]{1,0:T(8,128)S(1)}, f32[8,768]{1,0:T(8,128)}, u32[]{:S(2)}) copy-start(f32[8,768]{1,0:T(8,128)} %get-tuple-element.72) | copy-start | bytes 73732
  241.4 20.1 %copy-start.1 = (f32[1,3072]{1,0:T(1,128)S(1)}, f32[1,3072]{1,0:T(1,128)}, u32[]{:S(2)}) copy-start(f32[1,3072]{1,0:T(1,128)} %get-tuple-element.73) | copy-start | bytes 36868
